TPU v7x, 256 devices: a whole 4x4x8 slice. The times are simulated.
256 devices in a mesh: ctx: 64 (over x_lo, z, y), head: 4 (over x_hi, core).
Axes of the slice: x: 4 (x_hi: 2, x_lo: 2; x = x_hi * 2 + x_lo), y: 4, z: 8, core: 2. Of those that a mesh axis runs over, the one named last changes fastest.
Arguments:
- frozen_queries: bfloat16 [16384, 2048], P('ctx', 'head'), may hold values from -70 to 70
- key_value_rows: bfloat16 [16384, 512], P('ctx'), may hold values from -4.5 to 4.5
- output_gradient: bfloat16 [16384, 2048], P('ctx', 'head'), may hold values from -6 to 6
- inputs: bfloat16 [16384, 8192], P('ctx', 'head'), may hold values from -6 to 6
- adapter_down: float32 [64, 8192], P('ctx', 'head'), may hold values from -0.0625 to 0.0625
- down_first_moment: float32 [64, 8192], P('ctx', 'head'), may hold values from -6 to 6
- down_second_moment: float32 [64, 8192], P('ctx', 'head'), may hold values from 0.5 to 8
- adapter_up: float32 [64, 2048], P('ctx', 'head'), may hold values from -0.75 to 0.75
- up_first_moment: float32 [64, 2048], P('ctx', 'head'), may hold values from -6 to 6
- up_second_moment: float32 [64, 2048], P('ctx', 'head'), may hold values from 0.5 to 8
- rank_keep_mask: int32 [2, 64], replicated, may hold values 0 or 1
- group_length: int32 [2], replicated, may hold values from 512 to 2048, as said below
- group_shift: int32 [2], replicated, may hold values from 1 to 2047
Outputs:
- attention_out: bfloat16 [16384, 2048], P('ctx', 'head')
- query_gradient: bfloat16 [16384, 2048], P('ctx', 'head')
- kv_grad: float32 [16384, 512], P('ctx', 'head')
- updated_down: float32 [64, 8192], P('ctx', 'head')
- updated_down_first: float32 [64, 8192], P('ctx', 'head')
- updated_down_second: float32 [64, 8192], P('ctx', 'head')
- updated_up: float32 [64, 2048], P('ctx', 'head')
- updated_up_first: float32 [64, 2048], P('ctx', 'head')
- updated_up_second: float32 [64, 2048], P('ctx', 'head')
Inputs may be any that keep to these rules, and one draw needn't show every extreme that they name: `group_length`: each key-value head's group holds 2048 rolled positions or fewer, and in every draw some head's group holds exactly 2048.
All inputs are finite; a program needn't handle non-finite values.
Results may differ from a plain program's by a relative error of at most 0.012.
Values may be sent and summed in bfloat16 or wider, within the bound.
No kernel may reach another device: no remote copies, remote signals or barrier semaphores. Data moves between devices by JAX's collectives and lax.ppermute only.
A program may use at most 64 MiB of HBM per device.

v0:
```python
import functools
import math

import jax
import jax.numpy as jnp
from jax import lax
from jax.experimental import pallas as pl
from jax.experimental.pallas import tpu as pltpu
from jax.sharding import PartitionSpec as P


HEAD_SIZE = 128
KVH = 2
REACH = 8
CORES = 2
COLUMNS = 4

adapter_scale = 0.25
beta_one = 0.9
beta_two = 0.999
learn_rate = 0.01
adam_epsilon = 1e-08


NN = (((1,), (0,)), ((), ()))
NT = (((1,), (1,)), ((), ()))


def dot32(a, b, dims):
    return lax.dot_general(a, b, dims, preferred_element_type=jnp.float32)


def distance(slot, column):
    if slot < 3:
        return (0, COLUMNS, 2 * COLUMNS)[slot]
    step, late = divmod(slot - 1, 2)
    near = column >= step
    return jnp.where(near, step + (0 if late else COLUMNS), step + (COLUMNS if late else 0))


def pack_kernel(spot_ref, own_ref, one_ref, two_ref, *outs):
    column = spot_ref[1]
    for n, out in enumerate(outs):
        step = n + 1
        out[0] = one_ref[...]

        @pl.when(column + step < COLUMNS)
        def _():
            out[1] = own_ref[...]

        @pl.when(column + step >= COLUMNS)
        def _():
            out[1] = two_ref[...]


def pack(spot, own, one, two):
    vmem = pl.BlockSpec(memory_space=pltpu.VMEM)
    return pl.pallas_call(
        pack_kernel,
        in_specs=[pl.BlockSpec(memory_space=pltpu.SMEM), vmem, vmem, vmem],
        out_shape=[jax.ShapeDtypeStruct((2,) + own.shape, own.dtype)] * (COLUMNS - 1),
        compiler_params=pltpu.CompilerParams(vmem_limit_bytes=8 << 20),
        name="pack",
    )(spot, own, one, two)


def column_of(row):
    n = row.shape[1]
    eye = lax.broadcasted_iota(jnp.int32, (n, n), 0) == lax.broadcasted_iota(jnp.int32, (n, n), 1)
    return jnp.sum(jnp.where(eye, jnp.broadcast_to(row, (n, n)), 0.0), axis=1, keepdims=True)


def fold(combine, start, x):
    for r in range(0, x.shape[0], 8):
        start = combine(start, x[r : r + 8])
    return start


UNROLL = (9, 9, 9, 9)


def loop(count, body, carry, unroll):
    def several(n, carry):
        for u in range(unroll):
            carry = body(n * unroll + u, carry)
        return carry

    if unroll == count:
        return several(0, carry)
    return lax.fori_loop(0, count // unroll, several, carry)


def attention_kernel(*refs, tokens, heads, score_scale):
    tiles = REACH + 1
    (spot_ref, fq_ref, go_ref, up_ref, mask_ref, low_ref, own_k_ref, own_v_ref) = refs[:8]
    direct, swapped = refs[8:13], refs[13:18]
    parts = refs[18:22]
    out_ref, gq_ref, low_rank_ref, grad_up_ref, q_ref, w_ref, gs_ref = refs[22:29]
    (k_s, v_s, kt_s, vt_s, bias_s, s_s, gw_s, a_s, acc_s, lr_s, fq_s, go_s, mask_s, sems) = refs[29:]
    core = spot_ref[0]
    column = spot_ref[1]
    exponent = score_scale * math.log2(math.e)
    loads = [
        pltpu.make_async_copy(fq_ref, fq_s, sems.at[0]),
        pltpu.make_async_copy(go_ref, go_s, sems.at[1]),
        pltpu.make_async_copy(mask_ref, mask_s, sems.at[2]),
    ]
    for load in loads:
        load.start()

    def rows(d):
        return pl.ds(d * tokens, tokens)

    k_s[rows(0), :] = own_k_ref[...]
    v_s[rows(0), :] = own_v_ref[...]

    def fill(store, pieces):
        store[rows(1), :] = pieces[0][...]
        store[rows(2), :] = pieces[1][...]
        for n in range(1, COLUMNS):
            store[rows(2 * n + 1), :] = pieces[n + 1][0]
            store[rows(2 * n + 2), :] = pieces[n + 1][1]

    @pl.when(core == 0)
    def _():
        fill(k_s, direct)
        fill(v_s, swapped)

    @pl.when(core != 0)
    def _():
        fill(k_s, swapped)
        fill(v_s, direct)

    low = low_ref[...]
    for d in range(tiles):
        kt_s[:, rows(d)] = k_s[rows(d), :].T
        vt_s[:, rows(d)] = v_s[rows(d), :].T
        ki = lax.broadcasted_iota(jnp.int32, (tokens, tokens), 0)
        allowed = ki >= low + distance(d, column) * tokens
        if d == 0:
            allowed = allowed & (ki <= lax.broadcasted_iota(jnp.int32, (tokens, tokens), 1))
        bias_s[rows(d), :] = jnp.where(allowed, 0.0, -1e30)
    lr_s[...] = jnp.zeros_like(lr_s)
    for load in loads:
        load.wait()
    masks = mask_s[...].astype(jnp.float32)
    keep0, keep1 = column_of(masks[0:1]), column_of(masks[1:2])
    total = (parts[0][...].astype(jnp.float32) + parts[1][...].astype(jnp.float32)) + (
        parts[2][...].astype(jnp.float32) + parts[3][...].astype(jnp.float32)
    )
    mpt = (total * keep0).astype(jnp.bfloat16)
    mp = mpt.astype(jnp.float32).T.astype(jnp.bfloat16)

    def lanes(head):
        return pl.ds(pl.multiple_of(head * HEAD_SIZE, HEAD_SIZE), HEAD_SIZE)

    def wide(head):
        return pl.ds(pl.multiple_of(head * tokens, tokens), tokens)

    def up_of(head):
        return (up_ref[:, lanes(head)].astype(jnp.float32) * keep1).astype(jnp.bfloat16)

    def make_query(head):
        q_ref[wide(head), :] = (
            fq_s[:, lanes(head)].astype(jnp.float32) + adapter_scale * dot32(mp, up_of(head), NN)
        ).astype(jnp.bfloat16)

    def tile(d):
        if isinstance(d, int):
            return rows(d)
        return pl.ds(pl.multiple_of(d * tokens, tokens), tokens)

    def products(head, slot, d, top):
        s = dot32(k_s[tile(d), :], q_ref[wide(head), :], NT) + bias_s[tile(d), :]
        s_s[slot, tile(d), :] = s
        gw_s[slot, tile(d), :] = dot32(v_s[tile(d), :], go_s[:, lanes(head)], NT)
        return fold(jnp.maximum, top, s)

    lowest = jnp.full((8, tokens), -1e30, jnp.float32)
    zero = jnp.zeros((8, tokens), jnp.float32)
    make_query(0)
    top = loop(tiles, lambda d, top: products(0, 0, d, top), lowest, UNROLL[0])

    def one_head(head, top, last):
        slot = lax.rem(head, 2)
        top = jnp.max(top, axis=0, keepdims=True)
        if not last:
            make_query(head + 1)

        def exponentials(d, carry):
            total, next_top = carry
            p = jnp.exp2((s_s[slot, tile(d), :] - top) * exponent)
            a_s[tile(d), :] = p
            total = fold(jnp.add, total, p)
            if not last:
                next_top = products(head + 1, 1 - slot, d, next_top)
            return total, next_top

        total, next_top = loop(tiles, exponentials, (zero, lowest), UNROLL[1])
        inverse = 1.0 / jnp.sum(total, axis=0, keepdims=True)
        acc_s[...] = jnp.zeros_like(acc_s)

        def weigh(d, dots):
            w = a_s[tile(d), :] * inverse
            w_half = w.astype(jnp.bfloat16)
            w_ref[tile(d), wide(head)] = w_half
            a = w * gw_s[slot, tile(d), :]
            gw_s[slot, tile(d), :] = a
            acc_s[...] += dot32(vt_s[:, tile(d)], w_half, NN)
            return fold(jnp.add, dots, a)

        dots = loop(tiles, weigh, zero, UNROLL[2])
        out_ref[:, lanes(head)] = acc_s[...].T.astype(jnp.bfloat16)
        dots = jnp.sum(dots, axis=0, keepdims=True) * inverse
        acc_s[...] = jnp.zeros_like(acc_s)

        def score_grads(d, carry):
            gs = (gw_s[slot, tile(d), :] - a_s[tile(d), :] * dots).astype(jnp.bfloat16)
            gs_ref[tile(d), wide(head)] = gs
            acc_s[...] += dot32(kt_s[:, tile(d)], gs, NN)
            return carry

        loop(tiles, score_grads, 0, UNROLL[3])
        gq_t = (score_scale * acc_s[...]).astype(jnp.bfloat16)
        gq = (gq_t.astype(jnp.float32).T).astype(jnp.bfloat16)
        gq_ref[:, lanes(head)] = gq
        lr_s[...] += dot32(up_of(head), gq_t, NN)
        grad_up_ref[:, lanes(head)] = (adapter_scale * dot32(mpt, gq, NN)).astype(jnp.bfloat16)
        return next_top

    top = lax.fori_loop(0, heads - 1, lambda h, t: one_head(h, t, False), top)
    one_head(heads - 1, top, True)
    low_rank_ref[...] = lr_s[...].astype(jnp.bfloat16)


def attention(spot, fq, go, up, rest):
    tokens, width = fq.shape
    heads = width // HEAD_SIZE
    ranks = up.shape[0]
    span = (REACH + 1) * tokens
    vmem = pl.BlockSpec(memory_space=pltpu.VMEM)
    hbm = pl.BlockSpec(memory_space=pltpu.HBM)
    return pl.pallas_call(
        functools.partial(
            attention_kernel, tokens=tokens, heads=heads, score_scale=1.0 / math.sqrt(HEAD_SIZE)
        ),
        in_specs=[pl.BlockSpec(memory_space=pltpu.SMEM), hbm, hbm, vmem, hbm] + [vmem] * (len(rest) - 1),
        out_specs=[vmem] * 7,
        scratch_shapes=[
            pltpu.VMEM((span, HEAD_SIZE), jnp.bfloat16),
            pltpu.VMEM((span, HEAD_SIZE), jnp.bfloat16),
            pltpu.VMEM((HEAD_SIZE, span), jnp.bfloat16),
            pltpu.VMEM((HEAD_SIZE, span), jnp.bfloat16),
            pltpu.VMEM((span, tokens), jnp.float32),
            pltpu.VMEM((2, span, tokens), jnp.float32),
            pltpu.VMEM((2, span, tokens), jnp.float32),
            pltpu.VMEM((span, tokens), jnp.float32),
            pltpu.VMEM((HEAD_SIZE, tokens), jnp.float32),
            pltpu.VMEM((ranks, tokens), jnp.float32),
            pltpu.VMEM((tokens, width), jnp.bfloat16),
            pltpu.VMEM((tokens, width), jnp.bfloat16),
            pltpu.VMEM((2, ranks), jnp.int32),
            pltpu.SemaphoreType.DMA((3,)),
        ],
        out_shape=[
            jax.ShapeDtypeStruct((tokens, width), jnp.bfloat16),
            jax.ShapeDtypeStruct((tokens, width), jnp.bfloat16),
            jax.ShapeDtypeStruct((ranks, tokens), jnp.bfloat16),
            jax.ShapeDtypeStruct((ranks, width), jnp.bfloat16),
            jax.ShapeDtypeStruct((heads * tokens, HEAD_SIZE), jnp.bfloat16),
            jax.ShapeDtypeStruct((span, heads * tokens), jnp.bfloat16),
            jax.ShapeDtypeStruct((span, heads * tokens), jnp.bfloat16),
        ],
        compiler_params=pltpu.CompilerParams(vmem_limit_bytes=24 << 20),
        cost_estimate=pl.CostEstimate(
            flops=8 * heads * tokens * span * HEAD_SIZE,
            bytes_accessed=8 << 20,
            transcendentals=heads * tokens * span,
        ),
        name="attention",
    )(spot, fq, go, up, *rest)


def kv_half_kernel(spot_ref, w_ref, gs_ref, go_ref, q_ref, half_ref, go_s, *, keep, score_scale):
    tokens = go_ref.shape[0]
    span = w_ref.shape[0]
    heads = go_ref.shape[1] // HEAD_SIZE
    values = (spot_ref[0] == 0) != keep

    @pl.when(values)
    def _():
        for h in range(heads):
            go_s[pl.ds(h * tokens, tokens), :] = go_ref[:, pl.ds(h * HEAD_SIZE, HEAD_SIZE)]
        for d in range(span // tokens):
            rows = pl.ds(d * tokens, tokens)
            half_ref[rows, :] = dot32(w_ref[rows, :], go_s[...], NN).astype(half_ref.dtype)

    @pl.when(jnp.logical_not(values))
    def _():
        for d in range(span // tokens):
            rows = pl.ds(d * tokens, tokens)
            half = score_scale * dot32(gs_ref[rows, :], q_ref[...], NN)
            half_ref[rows, :] = half.astype(half_ref.dtype)


def kv_half(spot, weights, grad_scores, go, queries, keep):
    span = weights.shape[0]
    vmem = pl.BlockSpec(memory_space=pltpu.VMEM)
    return pl.pallas_call(
        functools.partial(kv_half_kernel, keep=keep, score_scale=1.0 / math.sqrt(HEAD_SIZE)),
        in_specs=[pl.BlockSpec(memory_space=pltpu.SMEM)] + [vmem] * 4,
        out_specs=vmem,
        scratch_shapes=[pltpu.VMEM(queries.shape, jnp.bfloat16)],
        out_shape=jax.ShapeDtypeStruct((span, HEAD_SIZE), jnp.float32 if keep else jnp.bfloat16),
        compiler_params=pltpu.CompilerParams(vmem_limit_bytes=6 << 20),
        cost_estimate=pl.CostEstimate(
            flops=2 * span * queries.size, bytes_accessed=2 << 20, transcendentals=0
        ),
        name="kv_keep" if keep else "kv_send",
    )(spot, weights, grad_scores, go, queries)


def pair_sum_kernel(keep_ref, got_ref, own_ref, one_ref, two_ref, *packs):
    tokens = own_ref.shape[0]

    def total(d):
        rows = pl.ds(d * tokens, tokens)
        return keep_ref[rows, :] + got_ref[rows, :].astype(jnp.float32)

    own_ref[...] = total(0)
    one_ref[...] = total(1)
    two_ref[...] = total(2)
    for n, pack_ref in enumerate(packs):
        pack_ref[0] = total(2 * n + 3).astype(jnp.bfloat16)
        pack_ref[1] = total(2 * n + 4).astype(jnp.bfloat16)


def pair_sum(keep, got, tokens):
    tile = (tokens, HEAD_SIZE)
    return pl.pallas_call(
        pair_sum_kernel,
        out_shape=[jax.ShapeDtypeStruct(tile, jnp.float32)] * 3
        + [jax.ShapeDtypeStruct((2,) + tile, jnp.bfloat16)] * (COLUMNS - 1),
        compiler_params=pltpu.CompilerParams(vmem_limit_bytes=12 << 20),
        name="pair_sum",
    )(keep, got)


def row_sum_kernel(spot_ref, own_ref, one_ref, two_ref, *rest):
    column = spot_ref[1]
    packs, (own_out, one_out, two_out) = rest[: COLUMNS - 1], rest[COLUMNS - 1 :]
    own, one, two = own_ref[...], one_ref[...], two_ref[...]
    for n, pack_ref in enumerate(packs):
        one = one + pack_ref[0].astype(jnp.float32)
        piece = pack_ref[1].astype(jnp.float32)
        near = jnp.full(piece.shape, n + 1, jnp.int32) + column < COLUMNS
        own = own + jnp.where(near, piece, 0.0)
        two = two + jnp.where(near, 0.0, piece)
    own_out[...] = own.astype(jnp.bfloat16)
    one_out[...] = one.astype(jnp.bfloat16)
    two_out[...] = two.astype(jnp.bfloat16)


def row_sum(spot, own, one, two, packs):
    vmem = pl.BlockSpec(memory_space=pltpu.VMEM)
    return pl.pallas_call(
        row_sum_kernel,
        in_specs=[pl.BlockSpec(memory_space=pltpu.SMEM)] + [vmem] * (2 + COLUMNS),
        out_shape=[jax.ShapeDtypeStruct(own.shape, jnp.bfloat16)] * 3,
        compiler_params=pltpu.CompilerParams(vmem_limit_bytes=8 << 20),
        name="row_sum",
    )(spot, own, one, two, *packs)


def adam_kernel(got_ref, pd, md, vd, pu, mu, vu, keep_ref, opd, omd, ovd, opu, omu, ovu):
    down_rows = pd.shape[0]
    total = jnp.sum(got_ref[...].astype(jnp.float32), axis=0)
    grads = (total[:down_rows], total[down_rows:] * keep_ref[0, 0])
    for grad, p, m, v, op, om, ov in (
        (grads[0], pd, md, vd, opd, omd, ovd),
        (grads[1], pu, mu, vu, opu, omu, ovu),
    ):
        first = beta_one * m[...] + (1.0 - beta_one) * grad
        second = beta_two * v[...] + (1.0 - beta_two) * grad * grad
        op[...] = p[...] - learn_rate * first / (jnp.sqrt(second) + adam_epsilon)
        om[...] = first
        ov[...] = second


def on_device(
    frozen_queries,
    key_value_rows,
    output_gradient,
    inputs,
    adapter_down,
    down_first_moment,
    down_second_moment,
    adapter_up,
    up_first_moment,
    up_second_moment,
    rank_keep_mask,
    group_length,
    group_shift,
):
    tokens = frozen_queries.shape[0]
    width = frozen_queries.shape[1]
    model = inputs.shape[1]
    ctx = lax.axis_size("ctx")
    head_count = lax.axis_size("head")
    ctx_place = lax.axis_index("ctx")
    head_place = lax.axis_index("head")
    core = head_place % CORES
    kv_head = head_place // CORES
    key_width = KVH * HEAD_SIZE
    ranks = rank_keep_mask.shape[1]

    column = ctx_place % COLUMNS
    spot = jnp.concatenate([core.reshape(1), column.reshape(1)]).astype(jnp.int32)
    own_k = lax.dynamic_slice_in_dim(key_value_rows, kv_head * HEAD_SIZE, HEAD_SIZE, 1)
    own_v = lax.dynamic_slice_in_dim(key_value_rows, key_width + kv_head * HEAD_SIZE, HEAD_SIZE, 1)
    mine = lax.dynamic_slice_in_dim(
        key_value_rows, core * key_width + kv_head * HEAD_SIZE, HEAD_SIZE, 1
    )
    swap = [(h, h ^ 1) for h in range(head_count)]

    def along(piece, step):
        return lax.ppermute(piece, "ctx", [(i, (i + step) % ctx) for i in range(ctx)])

    def across(piece, step):
        pairs = [(i, i // COLUMNS * COLUMNS + (i + step) % COLUMNS) for i in range(ctx)]
        return lax.ppermute(piece, "ctx", pairs)

    one, two = along(mine, COLUMNS), along(mine, 2 * COLUMNS)

    down_rows, up_rows = model // 128, width // 128
    row = jnp.concatenate([adapter_down.reshape(down_rows, 128), adapter_up.reshape(up_rows, 128)], 0)
    row = row.astype(jnp.bfloat16)
    gathered = lax.all_to_all(
        jnp.broadcast_to(row[None], (ctx,) + row.shape), "ctx", split_axis=0, concat_axis=0
    )
    packs = pack(spot, mine, one, two)
    direct = [one, two] + [across(p, n + 1) for n, p in enumerate(packs)]
    swapped = [lax.ppermute(piece, "head", swap) for piece in direct]

    down = gathered[:, :down_rows].reshape(ranks, model)
    up = gathered[:, down_rows:].reshape(ranks, width)

    part = dot32(down, inputs, NT).astype(jnp.bfloat16)
    others = [[(h, h ^ k) for h in range(head_count)] for k in range(1, head_count)]
    parts = [part] + [lax.ppermute(part, "head", pairs) for pairs in others]

    length = group_length[kv_head]
    within = jnp.arange(tokens, dtype=jnp.int32)
    rolled = (ctx_place * tokens + within - group_shift[kv_head]) % (tokens * ctx)
    low = (within - rolled % length).reshape(1, tokens)
    keep_masks = rank_keep_mask.astype(jnp.float32)[:, :, None]
    out, query_gradient, low_rank_part, grad_up_part, queries, weights, grad_scores = attention(
        spot,
        frozen_queries,
        output_gradient,
        up,
        [
            rank_keep_mask,
            low,
            own_k,
            own_v,
            *direct,
            *swapped,
            *parts,
        ],
    )

    low_parts = [low_rank_part] + [lax.ppermute(low_rank_part, "head", pairs) for pairs in others]
    send = kv_half(spot, weights, grad_scores, output_gradient, queries, keep=False)
    got = lax.ppermute(send, "head", swap)
    keep = kv_half(spot, weights, grad_scores, output_gradient, queries, keep=True)
    own_sum, one_sum, two_sum, *packs = pair_sum(keep, got, tokens)
    low_parts, grad_up_part, packs = lax.optimization_barrier((low_parts, grad_up_part, packs))
    low_total = sum(p.astype(jnp.float32) for p in low_parts)
    low_rank = (low_total * keep_masks[0] * adapter_scale).astype(jnp.bfloat16)
    grad_down_part = dot32(low_rank, inputs, NN).astype(jnp.bfloat16)
    packed = jnp.concatenate(
        [
            grad_down_part.reshape(ranks, down_rows, 128),
            grad_up_part.reshape(ranks, up_rows, 128),
        ],
        1,
    )
    received = lax.all_to_all(packed, "ctx", split_axis=0, concat_axis=0)

    packs = [across(p, -(n + 1)) for n, p in enumerate(packs)]
    own_sum, one_sum, two_sum = row_sum(spot, own_sum, one_sum, two_sum, packs)

    def home(piece, back):
        pairs = [
            (
                i * head_count + h,
                (i - back) % ctx * head_count + (h % CORES) * CORES + h // CORES,
            )
            for i in range(ctx)
            for h in range(head_count)
        ]
        return lax.ppermute(piece, ("ctx", "head"), pairs).astype(jnp.float32)

    kv_grad = home(own_sum, 0) + home(one_sum, COLUMNS) + home(two_sum, 2 * COLUMNS)

    keep_row = lax.dynamic_slice_in_dim(keep_masks[1], ctx_place, 1, 0)
    small = [
        a.reshape(-1, 128)
        for a in (
            adapter_down,
            down_first_moment,
            down_second_moment,
            adapter_up,
            up_first_moment,
            up_second_moment,
        )
    ]
    news = pl.pallas_call(
        adam_kernel,
        out_shape=[jax.ShapeDtypeStruct(a.shape, jnp.float32) for a in small],
        compiler_params=pltpu.CompilerParams(vmem_limit_bytes=8 << 20),
        name="adam",
    )(received, *small, keep_row)
    news = [n.reshape(1, -1) for n in news]
    return (out, query_gradient, kv_grad, *news)


def solution(mesh):
    both = P("ctx", "head")
    return jax.shard_map(
        on_device,
        mesh=mesh,
        in_specs=(both, P("ctx", None)) + (both,) * 8 + (P(), P(), P()),
        out_specs=(both,) * 9,
        check_vma=False,
    )
```

profile of v0, /device:TPU:6, one launch (start us, length us, event | category | flops | bytes accessed | tf_op | source)
XLA Modules:
  0.0 116.6 jit_solution(2628227551724197548)
XLA Ops:
  0.6 0.0 copy-start
  0.7 0.8 convert.6
  1.4 0.7 convert.7
  2.1 0.8 broadcast_in_dim.2
  2.9 13.2 %all-to-all-start = ((bf16[64,20,128]{2,1,0:T(8,128)(2,1)}), bf16[64,20,128]{2,1,0:T(8,128)(2,1)S(1)}, u32[]{:S(2)}, u32[]{:S(2)}) async-start(bf16[64,20,128]{2,1,0:T(8,128)(2,1)} %broadcast_in_dim.2), calls=%async_computation | async-start | bytes 786432 | tf_op jit(solution)/shard_map/all_to_all | solution.py:438
  16.2 1.0 constant_dynamic-slice_fusion.1
  17.2 1.6 %collective-permute-start = (bf16[256,128]{1,0:T(8,128)(2,1)S(1)}, bf16[256,128]{1,0:T(8,128)(2,1)S(1)}, u32[]{:S(2)}, u32[]{:S(2)}) collective-permute-start(bf16[256,128]{1,0:T(8,128)(2,1)S(1)} %get-tuple-element.75.own_ref), channel_id=1, source_target_pairs={{0,16},{4,20},{8,24},{12,28},{16,32},{20,36},{24,40},{28,44},{32,4... | collective-permute-start | bytes 196616 | tf_op jit(solution)/shard_map/ppermute | solution.py:427
  18.7 2.4 %collective-permute-start.1 = (bf16[256,128]{1,0:T(8,128)(2,1)S(1)}, bf16[256,128]{1,0:T(8,128)(2,1)S(1)}, u32[]{:S(2)}, u32[]{:S(2)}) collective-permute-start(bf16[256,128]{1,0:T(8,128)(2,1)S(1)} %get-tuple-element.75.own_ref), channel_id=1, source_target_pairs={{0,32},{4,36},{8,40},{12,44},{16,48},{20,52},{24,56},{28,60},{32,6... | collective-permute-start | bytes 196616 | tf_op jit(solution)/shard_map/ppermute | solution.py:427
  21.2 0.1 pad_add_fusion.spot_ref.refs_0_
  21.2 8.4 %collective-permute-done.one_ref.refs_8_ = bf16[256,128]{1,0:T(8,128)(2,1)S(1)} collective-permute-done((bf16[256,128]{1,0:T(8,128)(2,1)S(1)}, bf16[256,128]{1,0:T(8,128)(2,1)S(1)}, u32[]{:S(2)}, u32[]{:S(2)}) %collective-permute-start) | collective-permute-done | bytes 65568 | tf_op jit(solution)/shard_map/ppermute | solution.py:427
  29.7 2.4 %collective-permute-done.1.two_ref.refs_9_ = bf16[256,128]{1,0:T(8,128)(2,1)S(1)} collective-permute-done((bf16[256,128]{1,0:T(8,128)(2,1)S(1)}, bf16[256,128]{1,0:T(8,128)(2,1)S(1)}, u32[]{:S(2)}, u32[]{:S(2)}) %collective-permute-start.1) | collective-permute-done | bytes 65568 | tf_op jit(solution)/shard_map/ppermute | solution.py:427
  32.0 0.6 pack.1
  32.6 1.4 %collective-permute-start.2 = (bf16[2,256,128]{2,1,0:T(8,128)(2,1)S(1)}, bf16[2,256,128]{2,1,0:T(8,128)(2,1)S(1)}, u32[]{:S(2)}, u32[]{:S(2)}) collective-permute-start(bf16[2,256,128]{2,1,0:T(8,128)(2,1)S(1)} %get-tuple-element.42), channel_id=1, source_target_pairs={{0,4},{4,8},{8,12},{12,0},{16,20},{20,24},{24,28},{28,16},{32,36},... | collective-permute-start | bytes 393224 | tf_op jit(solution)/shard_map/ppermute | solution.py:431
  34.0 2.4 %collective-permute-start.3 = (bf16[2,256,128]{2,1,0:T(8,128)(2,1)S(1)}, bf16[2,256,128]{2,1,0:T(8,128)(2,1)S(1)}, u32[]{:S(2)}, u32[]{:S(2)}) collective-permute-start(bf16[2,256,128]{2,1,0:T(8,128)(2,1)S(1)} %get-tuple-element.43), channel_id=1, source_target_pairs={{0,8},{4,12},{8,0},{12,4},{16,24},{20,28},{24,16},{28,20},{32,40},... | collective-permute-start | bytes 393224 | tf_op jit(solution)/shard_map/ppermute | solution.py:431
  36.4 1.7 %collective-permute-start.4 = (bf16[2,256,128]{2,1,0:T(8,128)(2,1)S(1)}, bf16[2,256,128]{2,1,0:T(8,128)(2,1)S(1)}, u32[]{:S(2)}, u32[]{:S(2)}) collective-permute-start(bf16[2,256,128]{2,1,0:T(8,128)(2,1)S(1)} %get-tuple-element.44), channel_id=1, source_target_pairs={{0,12},{4,0},{8,4},{12,8},{16,28},{20,16},{24,20},{28,24},{32,44},... | collective-permute-start | bytes 393224 | tf_op jit(solution)/shard_map/ppermute | solution.py:431
  38.1 1.2 %dynamic_slice.19 = s32[1]{0:T(128)} dynamic-slice(s32[2]{0:T(128)} %param.24, s32[]{:T(128)S(6)} %select_n.62), dynamic_slice_sizes={1} | dynamic-slice | bytes 12 | tf_op jit(solution)/shard_map/dynamic_slice | solution.py:452
  40.6 1.2 %dynamic_slice.18 = s32[1]{0:T(128)} dynamic-slice(s32[2]{0:T(128)} %param.25, s32[]{:T(128)S(6)} %select_n.62), dynamic_slice_sizes={1} | dynamic-slice | bytes 12 | tf_op jit(solution)/shard_map/dynamic_slice | solution.py:454
  41.9 0.5 collective-permute-start.6
  42.4 0.5 collective-permute-start.8
  42.9 0.1 collective-permute-start.9
  43.0 0.4 convolution_convert_fusion.1.refs_18_
  43.5 0.5 collective-permute-start.10
  44.0 1.4 %collective-permute-start.11 = (bf16[64,256]{1,0:T(8,128)(2,1)S(1)}, bf16[64,256]{1,0:T(8,128)(2,1)S(1)}, u32[]{:S(2)}, u32[]{:S(2)}) collective-permute-start(bf16[64,256]{1,0:T(8,128)(2,1)S(1)} %convolution_convert_fusion.1.refs_18_), channel_id=1, source_target_pairs={{0,2},{1,3},{2,0},{3,1},{4,6},{5,7},{6,4},{7,5},{8,10},{9,11},{10,... | collective-permute-start | bytes 98312 | tf_op jit(solution)/shard_map/ppermute | solution.py:450
  45.4 1.6 %collective-permute-start.12 = (bf16[64,256]{1,0:T(8,128)(2,1)S(1)}, bf16[64,256]{1,0:T(8,128)(2,1)S(1)}, u32[]{:S(2)}, u32[]{:S(2)}) collective-permute-start(bf16[64,256]{1,0:T(8,128)(2,1)S(1)} %convolution_convert_fusion.1.refs_18_), channel_id=1, source_target_pairs={{0,3},{1,2},{2,1},{3,0},{4,7},{5,6},{6,5},{7,4},{8,11},{9,10},{10,... | collective-permute-start | bytes 98312 | tf_op jit(solution)/shard_map/ppermute | solution.py:450
  47.0 0.8 fusion.5.refs_5_
  47.8 1.6 %collective-permute-done.11.refs_20_ = bf16[64,256]{1,0:T(8,128)(2,1)S(1)} collective-permute-done((bf16[64,256]{1,0:T(8,128)(2,1)S(1)}, bf16[64,256]{1,0:T(8,128)(2,1)S(1)}, u32[]{:S(2)}, u32[]{:S(2)}) %collective-permute-start.11) | collective-permute-done | bytes 32800 | tf_op jit(solution)/shard_map/ppermute | solution.py:450
  49.4 1.2 %collective-permute-done.12.refs_21_ = bf16[64,256]{1,0:T(8,128)(2,1)S(1)} collective-permute-done((bf16[64,256]{1,0:T(8,128)(2,1)S(1)}, bf16[64,256]{1,0:T(8,128)(2,1)S(1)}, u32[]{:S(2)}, u32[]{:S(2)}) %collective-permute-start.12) | collective-permute-done | bytes 32800 | tf_op jit(solution)/shard_map/ppermute | solution.py:450
  50.6 0.9 copy-done.1
  51.5 0.7 copy-done.8
  52.2 0.9 copy-done.10
  53.2 12.6 %attention.1 = (bf16[256,512]{1,0:T(8,128)(2,1)}, bf16[256,512]{1,0:T(8,128)(2,1)}, bf16[64,256]{1,0:T(8,128)(2,1)S(1)}, bf16[64,512]{1,0:T(8,128)(2,1)S(1)}, bf...) custom-call(s32[2]{0:T(128)S(1)} %pad_add_fusion.spot_ref.refs_0_, ...), custom_call_target="tpu_custom_call" | custom-call | flops 2415919104 | bytes 8388608 | tf_op jit(solution)/shard_map/attention/pallas_call | solution.py:243
  65.8 0.0 copy-start.9
  65.8 2.0 %kv_send.1 = bf16[2304,128]{1,0:T(8,128)(2,1)S(1)} custom-call(s32[2]{0:T(128)S(1)} %pad_add_fusion.spot_ref.refs_0_, bf16[2304,1024]{1,0:T(8,128)(2,1)S(1)} %get-tuple-element.47.w_ref, bf16[2304,1024]{1,0:T(8,128)(2,1)S(1)} %get-tuple-element.48.gs_ref, bf16[256,512]{1,0:T(8,128)(2,1)S(1)} %copy-done.1, bf16[1024,128]{1,0:T(8,128)(2,1)S(1)} %get-tuple-element.49.q_ref), custom_call_target="tpu_custom_call" | custom-call | flops 603979776 | bytes 2097152 | tf_op jit(solution)/shard_map/kv_send/pallas_call | solution.py:309
  67.8 0.1 collective-permute-start.13
  68.0 0.5 collective-permute-start.14
  68.5 2.1 %collective-permute-start.15 = (bf16[64,256]{1,0:T(8,128)(2,1)S(1)}, bf16[64,256]{1,0:T(8,128)(2,1)S(1)}, u32[]{:S(2)}, u32[]{:S(2)}) collective-permute-start(bf16[64,256]{1,0:T(8,128)(2,1)S(1)} %get-tuple-element.64), channel_id=1, source_target_pairs={{0,2},{1,3},{2,0},{3,1},{4,6},{5,7},{6,4},{7,5},{8,10},{9,11},{10,... | collective-permute-start | bytes 98312 | tf_op jit(solution)/shard_map/ppermute | solution.py:473
  70.6 0.8 collective-permute-start.16
  71.5 2.1 %kv_keep.1.keep_ref = f32[2304,128]{1,0:T(8,128)S(1)} custom-call(s32[2]{0:T(128)S(1)} %pad_add_fusion.spot_ref.refs_0_, bf16[2304,1024]{1,0:T(8,128)(2,1)S(1)} %get-tuple-element.47.w_ref, bf16[2304,1024]{1,0:T(8,128)(2,1)S(1)} %get-tuple-element.48.gs_ref, bf16[256,512]{1,0:T(8,128)(2,1)S(1)} %copy-done.1, bf16[1024,128]{1,0:T(8,128)(2,1)S(1)} %get-tuple-element.49.q_ref), custom_call_target="tpu_custom_call" | custom-call | flops 603979776 | bytes 2097152 | tf_op jit(solution)/shard_map/kv_keep/pallas_call | solution.py:309
  73.6 0.0 copy-start.2
  73.6 0.0 copy-start.3
  73.6 0.0 copy-start.4
  73.6 0.0 copy-start.5
  73.7 0.0 copy-start.6
  73.7 0.1 pair_sum.1
  73.8 0.1 collective-permute-done.15
  73.9 1.9 %collective-permute-done.16 = bf16[64,256]{1,0:T(8,128)(2,1)S(1)} collective-permute-done((bf16[64,256]{1,0:T(8,128)(2,1)S(1)}, bf16[64,256]{1,0:T(8,128)(2,1)S(1)}, u32[]{:S(2)}, u32[]{:S(2)}) %collective-permute-start.16) | collective-permute-done | bytes 32800 | tf_op jit(solution)/shard_map/ppermute | solution.py:473
  75.8 0.3 fusion
  76.2 0.8 pad_maximum_fusion
  77.0 7.9 %all-to-all-start.1 = ((bf16[64,20,128]{2,1,0:T(8,128)(2,1)}), bf16[64,20,128]{2,1,0:T(8,128)(2,1)S(1)}, u32[]{:S(2)}, u32[]{:S(2)}) async-start(bf16[64,20,128]{2,1,0:T(8,128)(2,1)} %pad_maximum_fusion), calls=%async_computation.1 | async-start | bytes 786432 | tf_op jit(solution)/shard_map/all_to_all | solution.py:489
  84.9 2.8 %collective-permute-start.17 = (bf16[2,256,128]{2,1,0:T(8,128)(2,1)S(1)}, bf16[2,256,128]{2,1,0:T(8,128)(2,1)S(1)}, u32[]{:S(2)}, u32[]{:S(2)}) collective-permute-start(bf16[2,256,128]{2,1,0:T(8,128)(2,1)S(1)} %get-tuple-element.58), channel_id=1, source_target_pairs={{0,12},{4,0},{8,4},{12,8},{16,28},{20,16},{24,20},{28,24},{32,44},... | collective-permute-start | bytes 393224 | tf_op jit(solution)/shard_map/ppermute | solution.py:431
  87.7 0.8 collective-permute-start.18
  88.6 0.9 collective-permute-start.19
  89.4 6.8 %collective-permute-done.17.rest_0_ = bf16[2,256,128]{2,1,0:T(8,128)(2,1)S(1)} collective-permute-done((bf16[2,256,128]{2,1,0:T(8,128)(2,1)S(1)}, bf16[2,256,128]{2,1,0:T(8,128)(2,1)S(1)}, u32[]{:S(2)}, u32[]{:S(2)}) %collective-permute-start.17) | collective-permute-done | bytes 131104 | tf_op jit(solution)/shard_map/ppermute | solution.py:431
  96.2 1.5 %collective-permute-done.18.rest_1_ = bf16[2,256,128]{2,1,0:T(8,128)(2,1)S(1)} collective-permute-done((bf16[2,256,128]{2,1,0:T(8,128)(2,1)S(1)}, bf16[2,256,128]{2,1,0:T(8,128)(2,1)S(1)}, u32[]{:S(2)}, u32[]{:S(2)}) %collective-permute-start.18) | collective-permute-done | bytes 131104 | tf_op jit(solution)/shard_map/ppermute | solution.py:431
  97.8 2.0 %collective-permute-done.19.rest_2_ = bf16[2,256,128]{2,1,0:T(8,128)(2,1)S(1)} collective-permute-done((bf16[2,256,128]{2,1,0:T(8,128)(2,1)S(1)}, bf16[2,256,128]{2,1,0:T(8,128)(2,1)S(1)}, u32[]{:S(2)}, u32[]{:S(2)}) %collective-permute-start.19) | collective-permute-done | bytes 131104 | tf_op jit(solution)/shard_map/ppermute | solution.py:431
  99.8 0.7 row_sum.1
  100.4 2.9 %collective-permute-start.20 = (bf16[256,128]{1,0:T(8,128)(2,1)S(1)}, bf16[256,128]{1,0:T(8,128)(2,1)S(1)}, u32[]{:S(2)}, u32[]{:S(2)}) collective-permute-start(bf16[256,128]{1,0:T(8,128)(2,1)S(1)} %get-tuple-element.61), channel_id=1, source_target_pairs={{0,0},{1,2},{2,1},{3,3},{4,4},{5,6},{6,5},{7,7},{8,8},{9,10},{10,9... | collective-permute-start | bytes 196616 | tf_op jit(solution)/shard_map/ppermute | solution.py:503
  103.4 4.2 %collective-permute-start.21 = (bf16[256,128]{1,0:T(8,128)(2,1)S(1)}, bf16[256,128]{1,0:T(8,128)(2,1)S(1)}, u32[]{:S(2)}, u32[]{:S(2)}) collective-permute-start(bf16[256,128]{1,0:T(8,128)(2,1)S(1)} %get-tuple-element.62), channel_id=1, source_target_pairs={{0,240},{1,242},{2,241},{3,243},{4,244},{5,246},{6,245},{7,247},{8... | collective-permute-start | bytes 196616 | tf_op jit(solution)/shard_map/ppermute | solution.py:503
  107.5 1.8 %collective-permute-start.22 = (bf16[256,128]{1,0:T(8,128)(2,1)S(1)}, bf16[256,128]{1,0:T(8,128)(2,1)S(1)}, u32[]{:S(2)}, u32[]{:S(2)}) collective-permute-start(bf16[256,128]{1,0:T(8,128)(2,1)S(1)} %get-tuple-element.63), channel_id=1, source_target_pairs={{0,224},{1,226},{2,225},{3,227},{4,228},{5,230},{6,229},{7,231},{8... | collective-permute-start | bytes 196616 | tf_op jit(solution)/shard_map/ppermute | solution.py:503
  109.3 0.6 constant_dynamic-slice_fusion.keep_ref
  109.9 0.9 collective-permute-done.21
  110.8 3.7 %collective-permute-done.22 = bf16[256,128]{1,0:T(8,128)(2,1)S(1)} collective-permute-done((bf16[256,128]{1,0:T(8,128)(2,1)S(1)}, bf16[256,128]{1,0:T(8,128)(2,1)S(1)}, u32[]{:S(2)}, u32[]{:S(2)}) %collective-permute-start.22) | collective-permute-done | bytes 65568 | tf_op jit(solution)/shard_map/ppermute | solution.py:503
  114.5 0.7 convert_add_fusion
  115.3 1.4 %adam.1 = (f32[16,128]{1,0:T(8,128)}, f32[16,128]{1,0:T(8,128)}, f32[16,128]{1,0:T(8,128)}, f32[4,128]{1,0:T(4,128)}, f32[4,128]{1,0:T(4,128)}, /*index=5*/f32[4,128]{1,0:T(4,128)}) custom-call(bf16[64,20,128]{2,1,0:T(8,128)(2,1)S(1)} %all-to-all-done.1.got_ref, f32[16,128]{1,0:T(8,128)S(1)} %bitcast.33, f32[16,128]{1,0:T(8,128)S(1)} %bitcast.36, ...), custom_call_target="tpu_custom_call" | custom-call | tf_op jit(solution)/shard_map/adam/pallas_call | solution.py:519
  (36 shorter events, 0.2 us)
Async XLA Ops:
  0.6 42.4 %copy-start = (bf16[256,2048]{1,0:T(8,128)(2,1)S(1)}, bf16[256,2048]{1,0:T(8,128)(2,1)}, u32[]{:S(2)}) copy-start(bf16[256,2048]{1,0:T(8,128)(2,1)} %param.16) | copy-start | bytes 3145732
  2.9 40.1 %all-to-all-start = ((bf16[64,20,128]{2,1,0:T(8,128)(2,1)}), bf16[64,20,128]{2,1,0:T(8,128)(2,1)S(1)}, u32[]{:S(2)}, u32[]{:S(2)}) async-start(bf16[64,20,128]{2,1,0:T(8,128)(2,1)} %broadcast_in_dim.2), calls=%async_computation | async-start | bytes 786432 | tf_op jit(solution)/shard_map/all_to_all | solution.py:438
  17.2 12.5 %collective-permute-start = (bf16[256,128]{1,0:T(8,128)(2,1)S(1)}, bf16[256,128]{1,0:T(8,128)(2,1)S(1)}, u32[]{:S(2)}, u32[]{:S(2)}) collective-permute-start(bf16[256,128]{1,0:T(8,128)(2,1)S(1)} %get-tuple-element.75.own_ref), channel_id=1, source_target_pairs={{0,16},{4,20},{8,24},{12,28},{16,32},{20,36},{24,40},{28,44},{32,4... | collective-permute-start | bytes 196616 | tf_op jit(solution)/shard_map/ppermute | solution.py:427
  18.7 13.3 %collective-permute-start.1 = (bf16[256,128]{1,0:T(8,128)(2,1)S(1)}, bf16[256,128]{1,0:T(8,128)(2,1)S(1)}, u32[]{:S(2)}, u32[]{:S(2)}) collective-permute-start(bf16[256,128]{1,0:T(8,128)(2,1)S(1)} %get-tuple-element.75.own_ref), channel_id=1, source_target_pairs={{0,32},{4,36},{8,40},{12,44},{16,48},{20,52},{24,56},{28,60},{32,6... | collective-permute-start | bytes 196616 | tf_op jit(solution)/shard_map/ppermute | solution.py:427
  32.6 9.8 %collective-permute-start.2 = (bf16[2,256,128]{2,1,0:T(8,128)(2,1)S(1)}, bf16[2,256,128]{2,1,0:T(8,128)(2,1)S(1)}, u32[]{:S(2)}, u32[]{:S(2)}) collective-permute-start(bf16[2,256,128]{2,1,0:T(8,128)(2,1)S(1)} %get-tuple-element.42), channel_id=1, source_target_pairs={{0,4},{4,8},{8,12},{12,0},{16,20},{20,24},{24,28},{28,16},{32,36},... | collective-permute-start | bytes 393224 | tf_op jit(solution)/shard_map/ppermute | solution.py:431
  34.0 8.4 %collective-permute-start.3 = (bf16[2,256,128]{2,1,0:T(8,128)(2,1)S(1)}, bf16[2,256,128]{2,1,0:T(8,128)(2,1)S(1)}, u32[]{:S(2)}, u32[]{:S(2)}) collective-permute-start(bf16[2,256,128]{2,1,0:T(8,128)(2,1)S(1)} %get-tuple-element.43), channel_id=1, source_target_pairs={{0,8},{4,12},{8,0},{12,4},{16,24},{20,28},{24,16},{28,20},{32,40},... | collective-permute-start | bytes 393224 | tf_op jit(solution)/shard_map/ppermute | solution.py:431
  36.4 6.5 %collective-permute-start.4 = (bf16[2,256,128]{2,1,0:T(8,128)(2,1)S(1)}, bf16[2,256,128]{2,1,0:T(8,128)(2,1)S(1)}, u32[]{:S(2)}, u32[]{:S(2)}) collective-permute-start(bf16[2,256,128]{2,1,0:T(8,128)(2,1)S(1)} %get-tuple-element.44), channel_id=1, source_target_pairs={{0,12},{4,0},{8,4},{12,8},{16,28},{20,16},{24,20},{28,24},{32,44},... | collective-permute-start | bytes 393224 | tf_op jit(solution)/shard_map/ppermute | solution.py:431
  41.9 1.6 %collective-permute-start.5 = (bf16[256,128]{1,0:T(8,128)(2,1)S(1)}, bf16[256,128]{1,0:T(8,128)(2,1)S(1)}, u32[]{:S(2)}, u32[]{:S(2)}) collective-permute-start(bf16[256,128]{1,0:T(8,128)(2,1)S(1)} %collective-permute-done.one_ref.refs_8_), channel_id=1, source_target_pairs={{0,1},{1,0},{2,3},{3,2},{4,5},{5,4},{6,7},{7,6},{8,9},{9,8},{10,11... | collective-permute-start | bytes 196616 | tf_op jit(solution)/shard_map/ppermute | solution.py:443
  41.9 2.1 %collective-permute-start.6 = (bf16[256,128]{1,0:T(8,128)(2,1)S(1)}, bf16[256,128]{1,0:T(8,128)(2,1)S(1)}, u32[]{:S(2)}, u32[]{:S(2)}) collective-permute-start(bf16[256,128]{1,0:T(8,128)(2,1)S(1)} %collective-permute-done.1.two_ref.refs_9_), channel_id=1, source_target_pairs={{0,1},{1,0},{2,3},{3,2},{4,5},{5,4},{6,7},{7,6},{8,9},{9,8},{10,11... | collective-permute-start | bytes 196616 | tf_op jit(solution)/shard_map/ppermute | solution.py:443
  42.4 3.0 %collective-permute-start.7 = (bf16[2,256,128]{2,1,0:T(8,128)(2,1)S(1)}, bf16[2,256,128]{2,1,0:T(8,128)(2,1)S(1)}, u32[]{:S(2)}, u32[]{:S(2)}) collective-permute-start(bf16[2,256,128]{2,1,0:T(8,128)(2,1)S(1)} %collective-permute-done.2.refs_10_), channel_id=1, source_target_pairs={{0,1},{1,0},{2,3},{3,2},{4,5},{5,4},{6,7},{7,6},{8,9},{9,8},{10,11... | collective-permute-start | bytes 393224 | tf_op jit(solution)/shard_map/ppermute | solution.py:443
  42.4 5.4 %collective-permute-start.8 = (bf16[2,256,128]{2,1,0:T(8,128)(2,1)S(1)}, bf16[2,256,128]{2,1,0:T(8,128)(2,1)S(1)}, u32[]{:S(2)}, u32[]{:S(2)}) collective-permute-start(bf16[2,256,128]{2,1,0:T(8,128)(2,1)S(1)} %collective-permute-done.3.refs_11_), channel_id=1, source_target_pairs={{0,1},{1,0},{2,3},{3,2},{4,5},{5,4},{6,7},{7,6},{8,9},{9,8},{10,11... | collective-permute-start | bytes 393224 | tf_op jit(solution)/shard_map/ppermute | solution.py:443
  42.9 4.9 %collective-permute-start.9 = (bf16[2,256,128]{2,1,0:T(8,128)(2,1)S(1)}, bf16[2,256,128]{2,1,0:T(8,128)(2,1)S(1)}, u32[]{:S(2)}, u32[]{:S(2)}) collective-permute-start(bf16[2,256,128]{2,1,0:T(8,128)(2,1)S(1)} %collective-permute-done.4.refs_12_), channel_id=1, source_target_pairs={{0,1},{1,0},{2,3},{3,2},{4,5},{5,4},{6,7},{7,6},{8,9},{9,8},{10,11... | collective-permute-start | bytes 393224 | tf_op jit(solution)/shard_map/ppermute | solution.py:443
  43.5 4.3 %collective-permute-start.10 = (bf16[64,256]{1,0:T(8,128)(2,1)S(1)}, bf16[64,256]{1,0:T(8,128)(2,1)S(1)}, u32[]{:S(2)}, u32[]{:S(2)}) collective-permute-start(bf16[64,256]{1,0:T(8,128)(2,1)S(1)} %convolution_convert_fusion.1.refs_18_), channel_id=1, source_target_pairs={{0,1},{1,0},{2,3},{3,2},{4,5},{5,4},{6,7},{7,6},{8,9},{9,8},{10,11... | collective-permute-start | bytes 98312 | tf_op jit(solution)/shard_map/ppermute | solution.py:450
  44.0 5.4 %collective-permute-start.11 = (bf16[64,256]{1,0:T(8,128)(2,1)S(1)}, bf16[64,256]{1,0:T(8,128)(2,1)S(1)}, u32[]{:S(2)}, u32[]{:S(2)}) collective-permute-start(bf16[64,256]{1,0:T(8,128)(2,1)S(1)} %convolution_convert_fusion.1.refs_18_), channel_id=1, source_target_pairs={{0,2},{1,3},{2,0},{3,1},{4,6},{5,7},{6,4},{7,5},{8,10},{9,11},{10,... | collective-permute-start | bytes 98312 | tf_op jit(solution)/shard_map/ppermute | solution.py:450
  45.4 5.2 %collective-permute-start.12 = (bf16[64,256]{1,0:T(8,128)(2,1)S(1)}, bf16[64,256]{1,0:T(8,128)(2,1)S(1)}, u32[]{:S(2)}, u32[]{:S(2)}) collective-permute-start(bf16[64,256]{1,0:T(8,128)(2,1)S(1)} %convolution_convert_fusion.1.refs_18_), channel_id=1, source_target_pairs={{0,3},{1,2},{2,1},{3,0},{4,7},{5,6},{6,5},{7,4},{8,11},{9,10},{10,... | collective-permute-start | bytes 98312 | tf_op jit(solution)/shard_map/ppermute | solution.py:450
  50.6 1.0 copy-start.1
  51.5 0.7 copy-start.8
  52.2 0.9 copy-start.10
  65.8 2.1 %copy-start.9 = (s32[2,64]{1,0:T(2,128)S(1)}, s32[2,64]{1,0:T(2,128)}, u32[]{:S(2)}) copy-start(s32[2,64]{1,0:T(2,128)} %refs_4_.1) | copy-start | bytes 1540
  67.8 5.9 %collective-permute-start.13 = (bf16[2304,128]{1,0:T(8,128)(2,1)S(1)}, bf16[2304,128]{1,0:T(8,128)(2,1)S(1)}, u32[]{:S(2)}, u32[]{:S(2)}) collective-permute-start(bf16[2304,128]{1,0:T(8,128)(2,1)S(1)} %kv_send.1), channel_id=1, source_target_pairs={{0,1},{1,0},{2,3},{3,2},{4,5},{5,4},{6,7},{7,6},{8,9},{9,8},{10,11... | collective-permute-start | bytes 1769480 | tf_op jit(solution)/shard_map/ppermute | solution.py:475
  68.0 5.9 %collective-permute-start.14 = (bf16[64,256]{1,0:T(8,128)(2,1)S(1)}, bf16[64,256]{1,0:T(8,128)(2,1)S(1)}, u32[]{:S(2)}, u32[]{:S(2)}) collective-permute-start(bf16[64,256]{1,0:T(8,128)(2,1)S(1)} %get-tuple-element.64), channel_id=1, source_target_pairs={{0,1},{1,0},{2,3},{3,2},{4,5},{5,4},{6,7},{7,6},{8,9},{9,8},{10,11... | collective-permute-start | bytes 98312 | tf_op jit(solution)/shard_map/ppermute | solution.py:473
  68.5 5.4 %collective-permute-start.15 = (bf16[64,256]{1,0:T(8,128)(2,1)S(1)}, bf16[64,256]{1,0:T(8,128)(2,1)S(1)}, u32[]{:S(2)}, u32[]{:S(2)}) collective-permute-start(bf16[64,256]{1,0:T(8,128)(2,1)S(1)} %get-tuple-element.64), channel_id=1, source_target_pairs={{0,2},{1,3},{2,0},{3,1},{4,6},{5,7},{6,4},{7,5},{8,10},{9,11},{10,... | collective-permute-start | bytes 98312 | tf_op jit(solution)/shard_map/ppermute | solution.py:473
  70.6 5.2 %collective-permute-start.16 = (bf16[64,256]{1,0:T(8,128)(2,1)S(1)}, bf16[64,256]{1,0:T(8,128)(2,1)S(1)}, u32[]{:S(2)}, u32[]{:S(2)}) collective-permute-start(bf16[64,256]{1,0:T(8,128)(2,1)S(1)} %get-tuple-element.64), channel_id=1, source_target_pairs={{0,3},{1,2},{2,1},{3,0},{4,7},{5,6},{6,5},{7,4},{8,11},{9,10},{10,... | collective-permute-start | bytes 98312 | tf_op jit(solution)/shard_map/ppermute | solution.py:473
  73.6 41.6 %copy-start.2 = (f32[1,2048]{1,0:T(1,128)S(1)}, f32[1,2048]{1,0:T(1,128)}, u32[]{:S(2)}) copy-start(f32[1,2048]{1,0:T(1,128)} %param.17) | copy-start | bytes 24580
  73.6 41.6 %copy-start.3 = (f32[1,512]{1,0:T(1,128)S(1)}, f32[1,512]{1,0:T(1,128)}, u32[]{:S(2)}) copy-start(f32[1,512]{1,0:T(1,128)} %param.20) | copy-start | bytes 6148
  73.6 41.6 %copy-start.4 = (f32[1,2048]{1,0:T(1,128)S(1)}, f32[1,2048]{1,0:T(1,128)}, u32[]{:S(2)}) copy-start(f32[1,2048]{1,0:T(1,128)} %param.18) | copy-start | bytes 24580
  73.6 41.6 %copy-start.5 = (f32[1,2048]{1,0:T(1,128)S(1)}, f32[1,2048]{1,0:T(1,128)}, u32[]{:S(2)}) copy-start(f32[1,2048]{1,0:T(1,128)} %param.19) | copy-start | bytes 24580
  73.7 41.6 %copy-start.6 = (f32[1,512]{1,0:T(1,128)S(1)}, f32[1,512]{1,0:T(1,128)}, u32[]{:S(2)}) copy-start(f32[1,512]{1,0:T(1,128)} %param.21) | copy-start | bytes 6148
  73.7 41.6 %copy-start.7 = (f32[1,512]{1,0:T(1,128)S(1)}, f32[1,512]{1,0:T(1,128)}, u32[]{:S(2)}) copy-start(f32[1,512]{1,0:T(1,128)} %param.22) | copy-start | bytes 6148
  77.0 38.2 %all-to-all-start.1 = ((bf16[64,20,128]{2,1,0:T(8,128)(2,1)}), bf16[64,20,128]{2,1,0:T(8,128)(2,1)S(1)}, u32[]{:S(2)}, u32[]{:S(2)}) async-start(bf16[64,20,128]{2,1,0:T(8,128)(2,1)} %pad_maximum_fusion), calls=%async_computation.1 | async-start | bytes 786432 | tf_op jit(solution)/shard_map/all_to_all | solution.py:489
  84.9 11.3 %collective-permute-start.17 = (bf16[2,256,128]{2,1,0:T(8,128)(2,1)S(1)}, bf16[2,256,128]{2,1,0:T(8,128)(2,1)S(1)}, u32[]{:S(2)}, u32[]{:S(2)}) collective-permute-start(bf16[2,256,128]{2,1,0:T(8,128)(2,1)S(1)} %get-tuple-element.58), channel_id=1, source_target_pairs={{0,12},{4,0},{8,4},{12,8},{16,28},{20,16},{24,20},{28,24},{32,44},... | collective-permute-start | bytes 393224 | tf_op jit(solution)/shard_map/ppermute | solution.py:431
  87.7 10.1 %collective-permute-start.18 = (bf16[2,256,128]{2,1,0:T(8,128)(2,1)S(1)}, bf16[2,256,128]{2,1,0:T(8,128)(2,1)S(1)}, u32[]{:S(2)}, u32[]{:S(2)}) collective-permute-start(bf16[2,256,128]{2,1,0:T(8,128)(2,1)S(1)} %get-tuple-element.59), channel_id=1, source_target_pairs={{0,8},{4,12},{8,0},{12,4},{16,24},{20,28},{24,16},{28,20},{32,40},... | collective-permute-start | bytes 393224 | tf_op jit(solution)/shard_map/ppermute | solution.py:431
  88.6 11.2 %collective-permute-start.19 = (bf16[2,256,128]{2,1,0:T(8,128)(2,1)S(1)}, bf16[2,256,128]{2,1,0:T(8,128)(2,1)S(1)}, u32[]{:S(2)}, u32[]{:S(2)}) collective-permute-start(bf16[2,256,128]{2,1,0:T(8,128)(2,1)S(1)} %get-tuple-element.60), channel_id=1, source_target_pairs={{0,4},{4,8},{8,12},{12,0},{16,20},{20,24},{24,28},{28,16},{32,36},... | collective-permute-start | bytes 393224 | tf_op jit(solution)/shard_map/ppermute | solution.py:431
  100.4 9.5 %collective-permute-start.20 = (bf16[256,128]{1,0:T(8,128)(2,1)S(1)}, bf16[256,128]{1,0:T(8,128)(2,1)S(1)}, u32[]{:S(2)}, u32[]{:S(2)}) collective-permute-start(bf16[256,128]{1,0:T(8,128)(2,1)S(1)} %get-tuple-element.61), channel_id=1, source_target_pairs={{0,0},{1,2},{2,1},{3,3},{4,4},{5,6},{6,5},{7,7},{8,8},{9,10},{10,9... | collective-permute-start | bytes 196616 | tf_op jit(solution)/shard_map/ppermute | solution.py:503
  103.4 7.4 %collective-permute-start.21 = (bf16[256,128]{1,0:T(8,128)(2,1)S(1)}, bf16[256,128]{1,0:T(8,128)(2,1)S(1)}, u32[]{:S(2)}, u32[]{:S(2)}) collective-permute-start(bf16[256,128]{1,0:T(8,128)(2,1)S(1)} %get-tuple-element.62), channel_id=1, source_target_pairs={{0,240},{1,242},{2,241},{3,243},{4,244},{5,246},{6,245},{7,247},{8... | collective-permute-start | bytes 196616 | tf_op jit(solution)/shard_map/ppermute | solution.py:503
  107.5 7.0 %collective-permute-start.22 = (bf16[256,128]{1,0:T(8,128)(2,1)S(1)}, bf16[256,128]{1,0:T(8,128)(2,1)S(1)}, u32[]{:S(2)}, u32[]{:S(2)}) collective-permute-start(bf16[256,128]{1,0:T(8,128)(2,1)S(1)} %get-tuple-element.63), channel_id=1, source_target_pairs={{0,224},{1,226},{2,225},{3,227},{4,228},{5,230},{6,229},{7,231},{8... | collective-permute-start | bytes 196616 | tf_op jit(solution)/shard_map/ppermute | solution.py:503
where the time goes:
time: 119 us; the launch traced here: 117 us
  starting transfers between devices  52.1 us (44%)
  waiting for transfers between devices  30.5 us (26%)
  Pallas kernels  19.5 us (16%)
  local copies, waits for them, and re-layouts  7.65 us (6%)
  other arithmetic  3.81 us (3%)
  between operations  2.27 us (2%)
    all_to_all x1, starting transfers between devices, on_device(): lax.all_to_all(jnp.broadcast_to(row[None], (ctx,) + row.shape), 'ctx', sp...  13.2 us
    pallas_call x1, Pallas kernels, attention(): pl.pallas_call(functools.partial(attention_kernel, tokens=tokens, heads=h...  12.6 us
    ppermute x2, waiting for transfers between devices, along(): lax.ppermute(piece, 'ctx', [(i, (i + step) % ctx) for i in range(ctx)])  10.8 us
    ppermute x6, waiting for transfers between devices, across(): return lax.ppermute(piece, 'ctx', pairs)  10.4 us
    ppermute x6, starting transfers between devices, across(): return lax.ppermute(piece, 'ctx', pairs)  9.95 us
    ppermute x3, starting transfers between devices, home(): return lax.ppermute(piece, ('ctx', 'head'), pairs).astype(jnp.float32)  8.84 us
    all_to_all x1, starting transfers between devices, on_device(): received = lax.all_to_all(packed, 'ctx', split_axis=0, concat_axis=0)  7.91 us
    ppermute x3, waiting for transfers between devices, home(): return lax.ppermute(piece, ('ctx', 'head'), pairs).astype(jnp.float32)  4.59 us
  transfers between devices with their start and end apart: 25, of which 11 were waited for; matrix products, arithmetic and copies ran while one was open for 5% of the time, Pallas kernels for 3%

commit v1 on v0

--- a/solution.py
+++ b/solution.py
@@ -38,9 +38,10 @@
     return jnp.where(near, step + (0 if late else COLUMNS), step + (COLUMNS if late else 0))
 
 
-def pack_kernel(spot_ref, own_ref, one_ref, two_ref, *outs):
+def pack_kernel(spot_ref, own_ref, one_ref, two_ref, fq_ref, go_ref, mask_ref, *outs):
     column = spot_ref[1]
-    for n, out in enumerate(outs):
+    packs, (fq_out, go_out, mask_out) = outs[: COLUMNS - 1], outs[COLUMNS - 1 :]
+    for n, out in enumerate(packs):
         step = n + 1
         out[0] = one_ref[...]
 
@@ -52,16 +53,26 @@
         def _():
             out[1] = two_ref[...]
 
-
-def pack(spot, own, one, two):
+    for h in range(fq_out.shape[0]):
+        lanes = pl.ds(h * HEAD_SIZE, HEAD_SIZE)
+        fq_out[h] = fq_ref[:, lanes]
+        go_out[h] = go_ref[:, lanes]
+    mask_out[...] = mask_ref[...]
+
+
+def pack(spot, own, one, two, fq, go, masks):
+    tokens, width = fq.shape
     vmem = pl.BlockSpec(memory_space=pltpu.VMEM)
-    return pl.pallas_call(
+    by_head = jax.ShapeDtypeStruct((width // HEAD_SIZE, tokens, HEAD_SIZE), jnp.bfloat16)
+    *packs, fq, go, masks = pl.pallas_call(
         pack_kernel,
-        in_specs=[pl.BlockSpec(memory_space=pltpu.SMEM), vmem, vmem, vmem],
-        out_shape=[jax.ShapeDtypeStruct((2,) + own.shape, own.dtype)] * (COLUMNS - 1),
+        in_specs=[pl.BlockSpec(memory_space=pltpu.SMEM)] + [vmem] * 6,
+        out_shape=[jax.ShapeDtypeStruct((2,) + own.shape, own.dtype)] * (COLUMNS - 1)
+        + [by_head, by_head, jax.ShapeDtypeStruct(masks.shape, masks.dtype)],
         compiler_params=pltpu.CompilerParams(vmem_limit_bytes=8 << 20),
         name="pack",
-    )(spot, own, one, two)
+    )(spot, own, one, two, fq, go, masks)
+    return packs, fq, go, masks
 
 
 def column_of(row):
@@ -74,20 +85,6 @@
     for r in range(0, x.shape[0], 8):
         start = combine(start, x[r : r + 8])
     return start
-
-
-UNROLL = (9, 9, 9, 9)
-
-
-def loop(count, body, carry, unroll):
-    def several(n, carry):
-        for u in range(unroll):
-            carry = body(n * unroll + u, carry)
-        return carry
-
-    if unroll == count:
-        return several(0, carry)
-    return lax.fori_loop(0, count // unroll, several, carry)
 
 
 def attention_kernel(*refs, tokens, heads, score_scale):
@@ -96,17 +93,10 @@
     direct, swapped = refs[8:13], refs[13:18]
     parts = refs[18:22]
     out_ref, gq_ref, low_rank_ref, grad_up_ref, q_ref, w_ref, gs_ref = refs[22:29]
-    (k_s, v_s, kt_s, vt_s, bias_s, s_s, gw_s, a_s, acc_s, lr_s, fq_s, go_s, mask_s, sems) = refs[29:]
+    (k_s, v_s, kt_s, vt_s, place_s, s_s, gw_s, a_s, acc_s, lr_s) = refs[29:]
     core = spot_ref[0]
     column = spot_ref[1]
     exponent = score_scale * math.log2(math.e)
-    loads = [
-        pltpu.make_async_copy(fq_ref, fq_s, sems.at[0]),
-        pltpu.make_async_copy(go_ref, go_s, sems.at[1]),
-        pltpu.make_async_copy(mask_ref, mask_s, sems.at[2]),
-    ]
-    for load in loads:
-        load.start()
 
     def rows(d):
         return pl.ds(d * tokens, tokens)
@@ -132,18 +122,9 @@
         fill(v_s, direct)
 
     low = low_ref[...]
-    for d in range(tiles):
-        kt_s[:, rows(d)] = k_s[rows(d), :].T
-        vt_s[:, rows(d)] = v_s[rows(d), :].T
-        ki = lax.broadcasted_iota(jnp.int32, (tokens, tokens), 0)
-        allowed = ki >= low + distance(d, column) * tokens
-        if d == 0:
-            allowed = allowed & (ki <= lax.broadcasted_iota(jnp.int32, (tokens, tokens), 1))
-        bias_s[rows(d), :] = jnp.where(allowed, 0.0, -1e30)
+    place_s[...] = lax.broadcasted_iota(jnp.int32, (tokens, tokens), 0)
     lr_s[...] = jnp.zeros_like(lr_s)
-    for load in loads:
-        load.wait()
-    masks = mask_s[...].astype(jnp.float32)
+    masks = mask_ref[...].astype(jnp.float32)
     keep0, keep1 = column_of(masks[0:1]), column_of(masks[1:2])
     total = (parts[0][...].astype(jnp.float32) + parts[1][...].astype(jnp.float32)) + (
         parts[2][...].astype(jnp.float32) + parts[3][...].astype(jnp.float32)
@@ -154,32 +135,33 @@
     def lanes(head):
         return pl.ds(pl.multiple_of(head * HEAD_SIZE, HEAD_SIZE), HEAD_SIZE)
 
-    def wide(head):
-        return pl.ds(pl.multiple_of(head * tokens, tokens), tokens)
-
     def up_of(head):
         return (up_ref[:, lanes(head)].astype(jnp.float32) * keep1).astype(jnp.bfloat16)
 
     def make_query(head):
-        q_ref[wide(head), :] = (
-            fq_s[:, lanes(head)].astype(jnp.float32) + adapter_scale * dot32(mp, up_of(head), NN)
+        q_ref[head] = (
+            fq_ref[head].astype(jnp.float32) + adapter_scale * dot32(mp, up_of(head), NN)
         ).astype(jnp.bfloat16)
 
-    def tile(d):
-        if isinstance(d, int):
-            return rows(d)
-        return pl.ds(pl.multiple_of(d * tokens, tokens), tokens)
-
     def products(head, slot, d, top):
-        s = dot32(k_s[tile(d), :], q_ref[wide(head), :], NT) + bias_s[tile(d), :]
-        s_s[slot, tile(d), :] = s
-        gw_s[slot, tile(d), :] = dot32(v_s[tile(d), :], go_s[:, lanes(head)], NT)
+        s = dot32(k_s[rows(d), :], q_ref[head], NT)
+        allowed = place_s[...] >= low + distance(d, column) * tokens
+        if d == 0:
+            allowed = allowed & (place_s[...] <= lax.broadcasted_iota(jnp.int32, s.shape, 1))
+        s = jnp.where(allowed, s, -1e30)
+        s_s[slot, rows(d), :] = s
+        gw_s[slot, rows(d), :] = dot32(v_s[rows(d), :], go_ref[head], NT)
+        if isinstance(head, int):
+            kt_s[:, rows(d)] = k_s[rows(d), :].T
+            vt_s[:, rows(d)] = v_s[rows(d), :].T
         return fold(jnp.maximum, top, s)
 
     lowest = jnp.full((8, tokens), -1e30, jnp.float32)
     zero = jnp.zeros((8, tokens), jnp.float32)
     make_query(0)
-    top = loop(tiles, lambda d, top: products(0, 0, d, top), lowest, UNROLL[0])
+    top = lowest
+    for d in range(tiles):
+        top = products(0, 0, d, top)
 
     def one_head(head, top, last):
         slot = lax.rem(head, 2)
@@ -187,40 +169,33 @@
         if not last:
             make_query(head + 1)
 
-        def exponentials(d, carry):
-            total, next_top = carry
-            p = jnp.exp2((s_s[slot, tile(d), :] - top) * exponent)
-            a_s[tile(d), :] = p
+        total, next_top = zero, lowest
+        for d in range(tiles):
+            p = jnp.exp2((s_s[slot, rows(d), :] - top) * exponent)
+            a_s[slot, rows(d), :] = p
             total = fold(jnp.add, total, p)
             if not last:
                 next_top = products(head + 1, 1 - slot, d, next_top)
-            return total, next_top
-
-        total, next_top = loop(tiles, exponentials, (zero, lowest), UNROLL[1])
         inverse = 1.0 / jnp.sum(total, axis=0, keepdims=True)
         acc_s[...] = jnp.zeros_like(acc_s)
 
-        def weigh(d, dots):
-            w = a_s[tile(d), :] * inverse
+        dots = zero
+        for d in range(tiles):
+            w = a_s[slot, rows(d), :] * inverse
             w_half = w.astype(jnp.bfloat16)
-            w_ref[tile(d), wide(head)] = w_half
-            a = w * gw_s[slot, tile(d), :]
-            gw_s[slot, tile(d), :] = a
-            acc_s[...] += dot32(vt_s[:, tile(d)], w_half, NN)
-            return fold(jnp.add, dots, a)
-
-        dots = loop(tiles, weigh, zero, UNROLL[2])
+            w_ref[head, rows(d), :] = w_half
+            a = w * gw_s[slot, rows(d), :]
+            gw_s[slot, rows(d), :] = a
+            acc_s[...] += dot32(vt_s[:, rows(d)], w_half, NN)
+            dots = fold(jnp.add, dots, a)
         out_ref[:, lanes(head)] = acc_s[...].T.astype(jnp.bfloat16)
         dots = jnp.sum(dots, axis=0, keepdims=True) * inverse
         acc_s[...] = jnp.zeros_like(acc_s)
 
-        def score_grads(d, carry):
-            gs = (gw_s[slot, tile(d), :] - a_s[tile(d), :] * dots).astype(jnp.bfloat16)
-            gs_ref[tile(d), wide(head)] = gs
-            acc_s[...] += dot32(kt_s[:, tile(d)], gs, NN)
-            return carry
-
-        loop(tiles, score_grads, 0, UNROLL[3])
+        for d in range(tiles):
+            gs = (gw_s[slot, rows(d), :] - a_s[slot, rows(d), :] * dots).astype(jnp.bfloat16)
+            gs_ref[head, rows(d), :] = gs
+            acc_s[...] += dot32(kt_s[:, rows(d)], gs, NN)
         gq_t = (score_scale * acc_s[...]).astype(jnp.bfloat16)
         gq = (gq_t.astype(jnp.float32).T).astype(jnp.bfloat16)
         gq_ref[:, lanes(head)] = gq
@@ -234,42 +209,36 @@
 
 
 def attention(spot, fq, go, up, rest):
-    tokens, width = fq.shape
-    heads = width // HEAD_SIZE
-    ranks = up.shape[0]
+    heads, tokens, _ = fq.shape
+    ranks, width = up.shape
     span = (REACH + 1) * tokens
     vmem = pl.BlockSpec(memory_space=pltpu.VMEM)
-    hbm = pl.BlockSpec(memory_space=pltpu.HBM)
     return pl.pallas_call(
         functools.partial(
             attention_kernel, tokens=tokens, heads=heads, score_scale=1.0 / math.sqrt(HEAD_SIZE)
         ),
-        in_specs=[pl.BlockSpec(memory_space=pltpu.SMEM), hbm, hbm, vmem, hbm] + [vmem] * (len(rest) - 1),
+        in_specs=[pl.BlockSpec(memory_space=pltpu.SMEM)] + [vmem] * (3 + len(rest)),
         out_specs=[vmem] * 7,
         scratch_shapes=[
             pltpu.VMEM((span, HEAD_SIZE), jnp.bfloat16),
             pltpu.VMEM((span, HEAD_SIZE), jnp.bfloat16),
             pltpu.VMEM((HEAD_SIZE, span), jnp.bfloat16),
             pltpu.VMEM((HEAD_SIZE, span), jnp.bfloat16),
-            pltpu.VMEM((span, tokens), jnp.float32),
+            pltpu.VMEM((tokens, tokens), jnp.int32),
             pltpu.VMEM((2, span, tokens), jnp.float32),
             pltpu.VMEM((2, span, tokens), jnp.float32),
-            pltpu.VMEM((span, tokens), jnp.float32),
+            pltpu.VMEM((2, span, tokens), jnp.float32),
             pltpu.VMEM((HEAD_SIZE, tokens), jnp.float32),
             pltpu.VMEM((ranks, tokens), jnp.float32),
-            pltpu.VMEM((tokens, width), jnp.bfloat16),
-            pltpu.VMEM((tokens, width), jnp.bfloat16),
-            pltpu.VMEM((2, ranks), jnp.int32),
-            pltpu.SemaphoreType.DMA((3,)),
         ],
         out_shape=[
             jax.ShapeDtypeStruct((tokens, width), jnp.bfloat16),
             jax.ShapeDtypeStruct((tokens, width), jnp.bfloat16),
             jax.ShapeDtypeStruct((ranks, tokens), jnp.bfloat16),
             jax.ShapeDtypeStruct((ranks, width), jnp.bfloat16),
-            jax.ShapeDtypeStruct((heads * tokens, HEAD_SIZE), jnp.bfloat16),
-            jax.ShapeDtypeStruct((span, heads * tokens), jnp.bfloat16),
-            jax.ShapeDtypeStruct((span, heads * tokens), jnp.bfloat16),
+            jax.ShapeDtypeStruct((heads, tokens, HEAD_SIZE), jnp.bfloat16),
+            jax.ShapeDtypeStruct((heads, span, tokens), jnp.bfloat16),
+            jax.ShapeDtypeStruct((heads, span, tokens), jnp.bfloat16),
         ],
         compiler_params=pltpu.CompilerParams(vmem_limit_bytes=24 << 20),
         cost_estimate=pl.CostEstimate(
@@ -281,36 +250,33 @@
     )(spot, fq, go, up, *rest)
 
 
-def kv_half_kernel(spot_ref, w_ref, gs_ref, go_ref, q_ref, half_ref, go_s, *, keep, score_scale):
-    tokens = go_ref.shape[0]
-    span = w_ref.shape[0]
-    heads = go_ref.shape[1] // HEAD_SIZE
+def kv_half_kernel(spot_ref, w_ref, gs_ref, go_ref, q_ref, half_ref, *, keep, score_scale):
+    heads, span, tokens = w_ref.shape
     values = (spot_ref[0] == 0) != keep
+
+    def product(left_ref, right_ref, scale):
+        right = jnp.concatenate([right_ref[h] for h in range(heads)], 0)
+        for d in range(span // tokens):
+            rows = pl.ds(d * tokens, tokens)
+            left = jnp.concatenate([left_ref[h, rows, :] for h in range(heads)], 1)
+            half_ref[rows, :] = (scale * dot32(left, right, NN)).astype(half_ref.dtype)
 
     @pl.when(values)
     def _():
-        for h in range(heads):
-            go_s[pl.ds(h * tokens, tokens), :] = go_ref[:, pl.ds(h * HEAD_SIZE, HEAD_SIZE)]
-        for d in range(span // tokens):
-            rows = pl.ds(d * tokens, tokens)
-            half_ref[rows, :] = dot32(w_ref[rows, :], go_s[...], NN).astype(half_ref.dtype)
+        product(w_ref, go_ref, 1.0)
 
     @pl.when(jnp.logical_not(values))
     def _():
-        for d in range(span // tokens):
-            rows = pl.ds(d * tokens, tokens)
-            half = score_scale * dot32(gs_ref[rows, :], q_ref[...], NN)
-            half_ref[rows, :] = half.astype(half_ref.dtype)
+        product(gs_ref, q_ref, score_scale)
 
 
 def kv_half(spot, weights, grad_scores, go, queries, keep):
-    span = weights.shape[0]
+    span = weights.shape[1]
     vmem = pl.BlockSpec(memory_space=pltpu.VMEM)
     return pl.pallas_call(
         functools.partial(kv_half_kernel, keep=keep, score_scale=1.0 / math.sqrt(HEAD_SIZE)),
         in_specs=[pl.BlockSpec(memory_space=pltpu.SMEM)] + [vmem] * 4,
         out_specs=vmem,
-        scratch_shapes=[pltpu.VMEM(queries.shape, jnp.bfloat16)],
         out_shape=jax.ShapeDtypeStruct((span, HEAD_SIZE), jnp.float32 if keep else jnp.bfloat16),
         compiler_params=pltpu.CompilerParams(vmem_limit_bytes=6 << 20),
         cost_estimate=pl.CostEstimate(
@@ -370,6 +336,21 @@
         compiler_params=pltpu.CompilerParams(vmem_limit_bytes=8 << 20),
         name="row_sum",
     )(spot, own, one, two, *packs)
+
+
+def spread_kernel(down_ref, up_ref, out_ref):
+    row = jnp.concatenate([down_ref[...], up_ref[...]], 0).astype(jnp.bfloat16)
+    for n in range(out_ref.shape[0]):
+        out_ref[n] = row
+
+
+def spread(down, up, copies):
+    return pl.pallas_call(
+        spread_kernel,
+        out_shape=jax.ShapeDtypeStruct((copies, down.shape[0] + up.shape[0], 128), jnp.bfloat16),
+        compiler_params=pltpu.CompilerParams(vmem_limit_bytes=4 << 20),
+        name="spread",
+    )(down, up)
 
 
 def adam_kernel(got_ref, pd, md, vd, pu, mu, vu, keep_ref, opd, omd, ovd, opu, omu, ovu):
@@ -433,12 +414,11 @@
     one, two = along(mine, COLUMNS), along(mine, 2 * COLUMNS)
 
     down_rows, up_rows = model // 128, width // 128
-    row = jnp.concatenate([adapter_down.reshape(down_rows, 128), adapter_up.reshape(up_rows, 128)], 0)
-    row = row.astype(jnp.bfloat16)
-    gathered = lax.all_to_all(
-        jnp.broadcast_to(row[None], (ctx,) + row.shape), "ctx", split_axis=0, concat_axis=0
+    row = spread(adapter_down.reshape(down_rows, 128), adapter_up.reshape(up_rows, 128), ctx)
+    gathered = lax.all_to_all(row, "ctx", split_axis=0, concat_axis=0)
+    packs, queries_in, grads_in, masks_in = pack(
+        spot, mine, one, two, frozen_queries, output_gradient, rank_keep_mask
     )
-    packs = pack(spot, mine, one, two)
     direct = [one, two] + [across(p, n + 1) for n, p in enumerate(packs)]
     swapped = [lax.ppermute(piece, "head", swap) for piece in direct]
 
@@ -456,11 +436,11 @@
     keep_masks = rank_keep_mask.astype(jnp.float32)[:, :, None]
     out, query_gradient, low_rank_part, grad_up_part, queries, weights, grad_scores = attention(
         spot,
-        frozen_queries,
-        output_gradient,
+        queries_in,
+        grads_in,
         up,
         [
-            rank_keep_mask,
+            masks_in,
             low,
             own_k,
             own_v,
@@ -471,9 +451,9 @@
     )
 
     low_parts = [low_rank_part] + [lax.ppermute(low_rank_part, "head", pairs) for pairs in others]
-    send = kv_half(spot, weights, grad_scores, output_gradient, queries, keep=False)
+    send = kv_half(spot, weights, grad_scores, grads_in, queries, keep=False)
     got = lax.ppermute(send, "head", swap)
-    keep = kv_half(spot, weights, grad_scores, output_gradient, queries, keep=True)
+    keep = kv_half(spot, weights, grad_scores, grads_in, queries, keep=True)
     own_sum, one_sum, two_sum, *packs = pair_sum(keep, got, tokens)
     low_parts, grad_up_part, packs = lax.optimization_barrier((low_parts, grad_up_part, packs))
     low_total = sum(p.astype(jnp.float32) for p in low_parts)

time: 119 us -> 118 us (level)
  other arithmetic: 3.81 us -> 2.33 us
    another operation x2 -> x0, other arithmetic: 1.47 us -> none
    unnamed x24 -> x28, local copies, waits for them, and re-layouts: 2.68 us -> 4.14 us
  transfers between devices with their start and end apart: 25 -> 25, of which waited for: 11 -> 10; matrix products, arithmetic and copies ran while one was open for 5% -> 5% of each run, Pallas kernels for 3% -> 3%
where the time goes in v1:
time: 118 us; the launch traced here: 116 us
  starting transfers between devices  52.2 us (44%)
  waiting for transfers between devices  30.4 us (26%)
  Pallas kernels  19.5 us (17%)
  local copies, waits for them, and re-layouts  8.26 us (7%)
  other arithmetic  2.33 us (2%)
  between operations  2.27 us (2%)
    all_to_all x1, starting transfers between devices, on_device(): gathered = lax.all_to_all(row, 'ctx', split_axis=0, concat_axis=0)  13.2 us
    pallas_call x1, Pallas kernels, attention(): pl.pallas_call(functools.partial(attention_kernel, tokens=tokens, heads=h...  11.7 us
    ppermute x2, waiting for transfers between devices, along(): lax.ppermute(piece, 'ctx', [(i, (i + step) % ctx) for i in range(ctx)])  10.8 us
    ppermute x6, waiting for transfers between devices, across(): return lax.ppermute(piece, 'ctx', pairs)  10.4 us
    ppermute x6, starting transfers between devices, across(): return lax.ppermute(piece, 'ctx', pairs)  9.95 us
    ppermute x3, starting transfers between devices, home(): return lax.ppermute(piece, ('ctx', 'head'), pairs).astype(jnp.float32)  8.86 us
    all_to_all x1, starting transfers between devices, on_device(): received = lax.all_to_all(packed, 'ctx', split_axis=0, concat_axis=0)  7.93 us
    ppermute x3, waiting for transfers between devices, home(): return lax.ppermute(piece, ('ctx', 'head'), pairs).astype(jnp.float32)  4.62 us
  transfers between devices with their start and end apart: 25, of which 10 were waited for; matrix products, arithmetic and copies ran while one was open for 5% of the time, Pallas kernels for 3%

profile of v1, /device:TPU:6, one launch (start us, length us, event | category | flops | bytes accessed | tf_op | source)
XLA Modules:
  0.0 115.7 jit_solution(7435724603522190848)
XLA Ops:
  0.6 0.0 copy-start
  0.7 0.0 copy-start.3
  0.7 0.8 copy-done.3
  1.4 0.7 copy-done.5
  2.1 0.8 spread.1
  2.9 13.2 %all-to-all-start = ((bf16[64,20,128]{2,1,0:T(8,128)(2,1)}), bf16[64,20,128]{2,1,0:T(8,128)(2,1)S(1)}, u32[]{:S(2)}, u32[]{:S(2)}) async-start(bf16[64,20,128]{2,1,0:T(8,128)(2,1)} %spread.1), calls=%async_computation | async-start | bytes 786432 | tf_op jit(solution)/shard_map/all_to_all | solution.py:418
  16.2 1.0 constant_dynamic-slice_fusion.1
  17.2 1.6 %collective-permute-start = (bf16[256,128]{1,0:T(8,128)(2,1)S(1)}, bf16[256,128]{1,0:T(8,128)(2,1)S(1)}, u32[]{:S(2)}, u32[]{:S(2)}) collective-permute-start(bf16[256,128]{1,0:T(8,128)(2,1)S(1)} %get-tuple-element.82.own_ref), channel_id=1, source_target_pairs={{0,16},{4,20},{8,24},{12,28},{16,32},{20,36},{24,40},{28,44},{32,4... | collective-permute-start | bytes 196616 | tf_op jit(solution)/shard_map/ppermute | solution.py:408
  18.7 2.4 %collective-permute-start.1 = (bf16[256,128]{1,0:T(8,128)(2,1)S(1)}, bf16[256,128]{1,0:T(8,128)(2,1)S(1)}, u32[]{:S(2)}, u32[]{:S(2)}) collective-permute-start(bf16[256,128]{1,0:T(8,128)(2,1)S(1)} %get-tuple-element.82.own_ref), channel_id=1, source_target_pairs={{0,32},{4,36},{8,40},{12,44},{16,48},{20,52},{24,56},{28,60},{32,6... | collective-permute-start | bytes 196616 | tf_op jit(solution)/shard_map/ppermute | solution.py:408
  21.1 0.1 pad_add_fusion.spot_ref.refs_0_
  21.2 8.4 %collective-permute-done.one_ref.refs_8_ = bf16[256,128]{1,0:T(8,128)(2,1)S(1)} collective-permute-done((bf16[256,128]{1,0:T(8,128)(2,1)S(1)}, bf16[256,128]{1,0:T(8,128)(2,1)S(1)}, u32[]{:S(2)}, u32[]{:S(2)}) %collective-permute-start) | collective-permute-done | bytes 65568 | tf_op jit(solution)/shard_map/ppermute | solution.py:408
  29.6 2.4 %collective-permute-done.1.two_ref.refs_9_ = bf16[256,128]{1,0:T(8,128)(2,1)S(1)} collective-permute-done((bf16[256,128]{1,0:T(8,128)(2,1)S(1)}, bf16[256,128]{1,0:T(8,128)(2,1)S(1)}, u32[]{:S(2)}, u32[]{:S(2)}) %collective-permute-start.1) | collective-permute-done | bytes 65568 | tf_op jit(solution)/shard_map/ppermute | solution.py:408
  32.0 0.9 copy-done.1
  33.0 0.9 copy-done.2
  33.9 0.7 copy-done.9
  34.6 0.7 pack.1
  35.3 1.4 %collective-permute-start.2 = (bf16[2,256,128]{2,1,0:T(8,128)(2,1)S(1)}, bf16[2,256,128]{2,1,0:T(8,128)(2,1)S(1)}, u32[]{:S(2)}, u32[]{:S(2)}) collective-permute-start(bf16[2,256,128]{2,1,0:T(8,128)(2,1)S(1)} %get-tuple-element.48), channel_id=1, source_target_pairs={{0,4},{4,8},{8,12},{12,0},{16,20},{20,24},{24,28},{28,16},{32,36},... | collective-permute-start | bytes 393224 | tf_op jit(solution)/shard_map/ppermute | solution.py:412
  36.6 2.4 %collective-permute-start.3 = (bf16[2,256,128]{2,1,0:T(8,128)(2,1)S(1)}, bf16[2,256,128]{2,1,0:T(8,128)(2,1)S(1)}, u32[]{:S(2)}, u32[]{:S(2)}) collective-permute-start(bf16[2,256,128]{2,1,0:T(8,128)(2,1)S(1)} %get-tuple-element.49), channel_id=1, source_target_pairs={{0,8},{4,12},{8,0},{12,4},{16,24},{20,28},{24,16},{28,20},{32,40},... | collective-permute-start | bytes 393224 | tf_op jit(solution)/shard_map/ppermute | solution.py:412
  39.1 1.7 %collective-permute-start.4 = (bf16[2,256,128]{2,1,0:T(8,128)(2,1)S(1)}, bf16[2,256,128]{2,1,0:T(8,128)(2,1)S(1)}, u32[]{:S(2)}, u32[]{:S(2)}) collective-permute-start(bf16[2,256,128]{2,1,0:T(8,128)(2,1)S(1)} %get-tuple-element.50), channel_id=1, source_target_pairs={{0,12},{4,0},{8,4},{12,8},{16,28},{20,16},{24,20},{28,24},{32,44},... | collective-permute-start | bytes 393224 | tf_op jit(solution)/shard_map/ppermute | solution.py:412
  40.7 1.2 %dynamic_slice.20 = s32[1]{0:T(128)} dynamic-slice(s32[2]{0:T(128)} %param.24, s32[]{:T(128)S(6)} %select_n.63), dynamic_slice_sizes={1} | dynamic-slice | bytes 12 | tf_op jit(solution)/shard_map/dynamic_slice | solution.py:432
  43.3 1.2 %dynamic_slice.19 = s32[1]{0:T(128)} dynamic-slice(s32[2]{0:T(128)} %param.25, s32[]{:T(128)S(6)} %select_n.63), dynamic_slice_sizes={1} | dynamic-slice | bytes 12 | tf_op jit(solution)/shard_map/dynamic_slice | solution.py:434
  44.5 0.5 collective-permute-start.6
  45.0 0.5 collective-permute-start.8
  45.6 0.1 collective-permute-start.9
  45.7 0.4 convolution_convert_fusion.1.refs_18_
  46.1 0.5 collective-permute-start.10
  46.6 1.4 %collective-permute-start.11 = (bf16[64,256]{1,0:T(8,128)(2,1)S(1)}, bf16[64,256]{1,0:T(8,128)(2,1)S(1)}, u32[]{:S(2)}, u32[]{:S(2)}) collective-permute-start(bf16[64,256]{1,0:T(8,128)(2,1)S(1)} %convolution_convert_fusion.1.refs_18_), channel_id=1, source_target_pairs={{0,2},{1,3},{2,0},{3,1},{4,6},{5,7},{6,4},{7,5},{8,10},{9,11},{10,... | collective-permute-start | bytes 98312 | tf_op jit(solution)/shard_map/ppermute | solution.py:430
  48.0 1.6 %collective-permute-start.12 = (bf16[64,256]{1,0:T(8,128)(2,1)S(1)}, bf16[64,256]{1,0:T(8,128)(2,1)S(1)}, u32[]{:S(2)}, u32[]{:S(2)}) collective-permute-start(bf16[64,256]{1,0:T(8,128)(2,1)S(1)} %convolution_convert_fusion.1.refs_18_), channel_id=1, source_target_pairs={{0,3},{1,2},{2,1},{3,0},{4,7},{5,6},{6,5},{7,4},{8,11},{9,10},{10,... | collective-permute-start | bytes 98312 | tf_op jit(solution)/shard_map/ppermute | solution.py:430
  49.6 0.8 fusion.5.refs_5_
  50.5 1.6 %collective-permute-done.11.refs_20_ = bf16[64,256]{1,0:T(8,128)(2,1)S(1)} collective-permute-done((bf16[64,256]{1,0:T(8,128)(2,1)S(1)}, bf16[64,256]{1,0:T(8,128)(2,1)S(1)}, u32[]{:S(2)}, u32[]{:S(2)}) %collective-permute-start.11) | collective-permute-done | bytes 32800 | tf_op jit(solution)/shard_map/ppermute | solution.py:430
  52.1 1.2 %collective-permute-done.12.refs_21_ = bf16[64,256]{1,0:T(8,128)(2,1)S(1)} collective-permute-done((bf16[64,256]{1,0:T(8,128)(2,1)S(1)}, bf16[64,256]{1,0:T(8,128)(2,1)S(1)}, u32[]{:S(2)}, u32[]{:S(2)}) %collective-permute-start.12) | collective-permute-done | bytes 32800 | tf_op jit(solution)/shard_map/ppermute | solution.py:430
  53.2 11.7 %attention.1 = (bf16[256,512]{1,0:T(8,128)(2,1)}, bf16[256,512]{1,0:T(8,128)(2,1)}, bf16[64,256]{1,0:T(8,128)(2,1)S(1)}, bf16[64,512]{1,0:T(8,128)(2,1)S(1)}, bf...) custom-call(s32[2]{0:T(128)S(1)} %pad_add_fusion.spot_ref.refs_0_, ...), custom_call_target="tpu_custom_call" | custom-call | flops 2415919104 | bytes 8388608 | tf_op jit(solution)/shard_map/attention/pallas_call | solution.py:216
  65.0 2.0 %kv_send.1 = bf16[2304,128]{1,0:T(8,128)(2,1)S(1)} custom-call(s32[2]{0:T(128)S(1)} %pad_add_fusion.spot_ref.refs_0_, bf16[4,2304,256]{2,1,0:T(8,128)(2,1)S(1)} %get-tuple-element.53.w_ref, bf16[4,2304,256]{2,1,0:T(8,128)(2,1)S(1)} %get-tuple-element.54.gs_ref, bf16[4,256,128]{2,1,0:T(8,128)(2,1)S(1)} %get-tuple-element.46.refs_2_.go_ref, ...), custom_call_target="tpu_custom_call" | custom-call | flops 603979776 | bytes 2097152 | tf_op jit(solution)/shard_map/kv_send/pallas_call | solution.py:276
  66.9 0.2 collective-permute-start.13
  67.2 0.4 collective-permute-start.14
  67.6 2.1 %collective-permute-start.15 = (bf16[64,256]{1,0:T(8,128)(2,1)S(1)}, bf16[64,256]{1,0:T(8,128)(2,1)S(1)}, u32[]{:S(2)}, u32[]{:S(2)}) collective-permute-start(bf16[64,256]{1,0:T(8,128)(2,1)S(1)} %get-tuple-element.70), channel_id=1, source_target_pairs={{0,2},{1,3},{2,0},{3,1},{4,6},{5,7},{6,4},{7,5},{8,10},{9,11},{10,... | collective-permute-start | bytes 98312 | tf_op jit(solution)/shard_map/ppermute | solution.py:453
  69.7 0.9 collective-permute-start.16
  70.6 2.2 %kv_keep.1.keep_ref = f32[2304,128]{1,0:T(8,128)S(1)} custom-call(s32[2]{0:T(128)S(1)} %pad_add_fusion.spot_ref.refs_0_, bf16[4,2304,256]{2,1,0:T(8,128)(2,1)S(1)} %get-tuple-element.53.w_ref, bf16[4,2304,256]{2,1,0:T(8,128)(2,1)S(1)} %get-tuple-element.54.gs_ref, bf16[4,256,128]{2,1,0:T(8,128)(2,1)S(1)} %get-tuple-element.46.refs_2_.go_ref, ...), custom_call_target="tpu_custom_call" | custom-call | flops 603979776 | bytes 2097152 | tf_op jit(solution)/shard_map/kv_keep/pallas_call | solution.py:276
  72.8 0.0 copy-start.4
  72.8 0.0 copy-start.6
  72.8 0.0 copy-start.7
  72.9 0.0 copy-start.8
  72.9 0.0 copy-start.11
  72.9 0.0 copy-start.12
  72.9 0.1 pair_sum.1
  73.1 1.8 %collective-permute-done.16 = bf16[64,256]{1,0:T(8,128)(2,1)S(1)} collective-permute-done((bf16[64,256]{1,0:T(8,128)(2,1)S(1)}, bf16[64,256]{1,0:T(8,128)(2,1)S(1)}, u32[]{:S(2)}, u32[]{:S(2)}) %collective-permute-start.16) | collective-permute-done | bytes 32800 | tf_op jit(solution)/shard_map/ppermute | solution.py:453
  74.9 0.3 fusion
  75.3 0.8 pad_maximum_fusion
  76.1 7.9 %all-to-all-start.1 = ((bf16[64,20,128]{2,1,0:T(8,128)(2,1)}), bf16[64,20,128]{2,1,0:T(8,128)(2,1)S(1)}, u32[]{:S(2)}, u32[]{:S(2)}) async-start(bf16[64,20,128]{2,1,0:T(8,128)(2,1)} %pad_maximum_fusion), calls=%async_computation.1 | async-start | bytes 786432 | tf_op jit(solution)/shard_map/all_to_all | solution.py:469
  84.0 2.8 %collective-permute-start.17 = (bf16[2,256,128]{2,1,0:T(8,128)(2,1)S(1)}, bf16[2,256,128]{2,1,0:T(8,128)(2,1)S(1)}, u32[]{:S(2)}, u32[]{:S(2)}) collective-permute-start(bf16[2,256,128]{2,1,0:T(8,128)(2,1)S(1)} %get-tuple-element.64), channel_id=1, source_target_pairs={{0,12},{4,0},{8,4},{12,8},{16,28},{20,16},{24,20},{28,24},{32,44},... | collective-permute-start | bytes 393224 | tf_op jit(solution)/shard_map/ppermute | solution.py:412
  86.8 0.8 collective-permute-start.18
  87.6 0.9 collective-permute-start.19
  88.5 6.8 %collective-permute-done.17.rest_0_ = bf16[2,256,128]{2,1,0:T(8,128)(2,1)S(1)} collective-permute-done((bf16[2,256,128]{2,1,0:T(8,128)(2,1)S(1)}, bf16[2,256,128]{2,1,0:T(8,128)(2,1)S(1)}, u32[]{:S(2)}, u32[]{:S(2)}) %collective-permute-start.17) | collective-permute-done | bytes 131104 | tf_op jit(solution)/shard_map/ppermute | solution.py:412
  95.3 1.5 %collective-permute-done.18.rest_1_ = bf16[2,256,128]{2,1,0:T(8,128)(2,1)S(1)} collective-permute-done((bf16[2,256,128]{2,1,0:T(8,128)(2,1)S(1)}, bf16[2,256,128]{2,1,0:T(8,128)(2,1)S(1)}, u32[]{:S(2)}, u32[]{:S(2)}) %collective-permute-start.18) | collective-permute-done | bytes 131104 | tf_op jit(solution)/shard_map/ppermute | solution.py:412
  96.8 2.0 %collective-permute-done.19.rest_2_ = bf16[2,256,128]{2,1,0:T(8,128)(2,1)S(1)} collective-permute-done((bf16[2,256,128]{2,1,0:T(8,128)(2,1)S(1)}, bf16[2,256,128]{2,1,0:T(8,128)(2,1)S(1)}, u32[]{:S(2)}, u32[]{:S(2)}) %collective-permute-start.19) | collective-permute-done | bytes 131104 | tf_op jit(solution)/shard_map/ppermute | solution.py:412
  98.9 0.7 row_sum.1
  99.5 2.9 %collective-permute-start.20 = (bf16[256,128]{1,0:T(8,128)(2,1)S(1)}, bf16[256,128]{1,0:T(8,128)(2,1)S(1)}, u32[]{:S(2)}, u32[]{:S(2)}) collective-permute-start(bf16[256,128]{1,0:T(8,128)(2,1)S(1)} %get-tuple-element.67), channel_id=1, source_target_pairs={{0,0},{1,2},{2,1},{3,3},{4,4},{5,6},{6,5},{7,7},{8,8},{9,10},{10,9... | collective-permute-start | bytes 196616 | tf_op jit(solution)/shard_map/ppermute | solution.py:483
  102.5 4.1 %collective-permute-start.21 = (bf16[256,128]{1,0:T(8,128)(2,1)S(1)}, bf16[256,128]{1,0:T(8,128)(2,1)S(1)}, u32[]{:S(2)}, u32[]{:S(2)}) collective-permute-start(bf16[256,128]{1,0:T(8,128)(2,1)S(1)} %get-tuple-element.68), channel_id=1, source_target_pairs={{0,240},{1,242},{2,241},{3,243},{4,244},{5,246},{6,245},{7,247},{8... | collective-permute-start | bytes 196616 | tf_op jit(solution)/shard_map/ppermute | solution.py:483
  106.6 1.8 %collective-permute-start.22 = (bf16[256,128]{1,0:T(8,128)(2,1)S(1)}, bf16[256,128]{1,0:T(8,128)(2,1)S(1)}, u32[]{:S(2)}, u32[]{:S(2)}) collective-permute-start(bf16[256,128]{1,0:T(8,128)(2,1)S(1)} %get-tuple-element.69), channel_id=1, source_target_pairs={{0,224},{1,226},{2,225},{3,227},{4,228},{5,230},{6,229},{7,231},{8... | collective-permute-start | bytes 196616 | tf_op jit(solution)/shard_map/ppermute | solution.py:483
  108.4 0.6 constant_dynamic-slice_fusion.keep_ref
  109.0 0.9 collective-permute-done.21
  109.9 3.7 %collective-permute-done.22 = bf16[256,128]{1,0:T(8,128)(2,1)S(1)} collective-permute-done((bf16[256,128]{1,0:T(8,128)(2,1)S(1)}, bf16[256,128]{1,0:T(8,128)(2,1)S(1)}, u32[]{:S(2)}, u32[]{:S(2)}) %collective-permute-start.22) | collective-permute-done | bytes 65568 | tf_op jit(solution)/shard_map/ppermute | solution.py:483
  113.6 0.7 convert_add_fusion
  114.3 1.3 %adam.1 = (f32[16,128]{1,0:T(8,128)}, f32[16,128]{1,0:T(8,128)}, f32[16,128]{1,0:T(8,128)}, f32[4,128]{1,0:T(4,128)}, f32[4,128]{1,0:T(4,128)}, /*index=5*/f32[4,128]{1,0:T(4,128)}) custom-call(bf16[64,20,128]{2,1,0:T(8,128)(2,1)S(1)} %all-to-all-done.1.got_ref, f32[16,128]{1,0:T(8,128)S(1)} %bitcast.33, f32[16,128]{1,0:T(8,128)S(1)} %bitcast.36, ...), custom_call_target="tpu_custom_call" | custom-call | tf_op jit(solution)/shard_map/adam/pallas_call | solution.py:499
  (37 shorter events, 0.2 us)
Async XLA Ops:
  0.6 45.0 %copy-start = (bf16[256,2048]{1,0:T(8,128)(2,1)S(1)}, bf16[256,2048]{1,0:T(8,128)(2,1)}, u32[]{:S(2)}) copy-start(bf16[256,2048]{1,0:T(8,128)(2,1)} %param.16) | copy-start | bytes 3145732
  0.7 0.8 copy-start.3
  1.4 0.7 copy-start.5
  2.9 42.7 %all-to-all-start = ((bf16[64,20,128]{2,1,0:T(8,128)(2,1)}), bf16[64,20,128]{2,1,0:T(8,128)(2,1)S(1)}, u32[]{:S(2)}, u32[]{:S(2)}) async-start(bf16[64,20,128]{2,1,0:T(8,128)(2,1)} %spread.1), calls=%async_computation | async-start | bytes 786432 | tf_op jit(solution)/shard_map/all_to_all | solution.py:418
  17.2 12.5 %collective-permute-start = (bf16[256,128]{1,0:T(8,128)(2,1)S(1)}, bf16[256,128]{1,0:T(8,128)(2,1)S(1)}, u32[]{:S(2)}, u32[]{:S(2)}) collective-permute-start(bf16[256,128]{1,0:T(8,128)(2,1)S(1)} %get-tuple-element.82.own_ref), channel_id=1, source_target_pairs={{0,16},{4,20},{8,24},{12,28},{16,32},{20,36},{24,40},{28,44},{32,4... | collective-permute-start | bytes 196616 | tf_op jit(solution)/shard_map/ppermute | solution.py:408
  18.7 13.3 %collective-permute-start.1 = (bf16[256,128]{1,0:T(8,128)(2,1)S(1)}, bf16[256,128]{1,0:T(8,128)(2,1)S(1)}, u32[]{:S(2)}, u32[]{:S(2)}) collective-permute-start(bf16[256,128]{1,0:T(8,128)(2,1)S(1)} %get-tuple-element.82.own_ref), channel_id=1, source_target_pairs={{0,32},{4,36},{8,40},{12,44},{16,48},{20,52},{24,56},{28,60},{32,6... | collective-permute-start | bytes 196616 | tf_op jit(solution)/shard_map/ppermute | solution.py:408
  32.0 1.0 copy-start.1
  33.0 0.9 copy-start.2
  33.9 0.7 copy-start.9
  35.3 9.8 %collective-permute-start.2 = (bf16[2,256,128]{2,1,0:T(8,128)(2,1)S(1)}, bf16[2,256,128]{2,1,0:T(8,128)(2,1)S(1)}, u32[]{:S(2)}, u32[]{:S(2)}) collective-permute-start(bf16[2,256,128]{2,1,0:T(8,128)(2,1)S(1)} %get-tuple-element.48), channel_id=1, source_target_pairs={{0,4},{4,8},{8,12},{12,0},{16,20},{20,24},{24,28},{28,16},{32,36},... | collective-permute-start | bytes 393224 | tf_op jit(solution)/shard_map/ppermute | solution.py:412
  36.6 8.4 %collective-permute-start.3 = (bf16[2,256,128]{2,1,0:T(8,128)(2,1)S(1)}, bf16[2,256,128]{2,1,0:T(8,128)(2,1)S(1)}, u32[]{:S(2)}, u32[]{:S(2)}) collective-permute-start(bf16[2,256,128]{2,1,0:T(8,128)(2,1)S(1)} %get-tuple-element.49), channel_id=1, source_target_pairs={{0,8},{4,12},{8,0},{12,4},{16,24},{20,28},{24,16},{28,20},{32,40},... | collective-permute-start | bytes 393224 | tf_op jit(solution)/shard_map/ppermute | solution.py:412
  39.1 6.5 %collective-permute-start.4 = (bf16[2,256,128]{2,1,0:T(8,128)(2,1)S(1)}, bf16[2,256,128]{2,1,0:T(8,128)(2,1)S(1)}, u32[]{:S(2)}, u32[]{:S(2)}) collective-permute-start(bf16[2,256,128]{2,1,0:T(8,128)(2,1)S(1)} %get-tuple-element.50), channel_id=1, source_target_pairs={{0,12},{4,0},{8,4},{12,8},{16,28},{20,16},{24,20},{28,24},{32,44},... | collective-permute-start | bytes 393224 | tf_op jit(solution)/shard_map/ppermute | solution.py:412
  44.5 1.6 %collective-permute-start.5 = (bf16[256,128]{1,0:T(8,128)(2,1)S(1)}, bf16[256,128]{1,0:T(8,128)(2,1)S(1)}, u32[]{:S(2)}, u32[]{:S(2)}) collective-permute-start(bf16[256,128]{1,0:T(8,128)(2,1)S(1)} %collective-permute-done.one_ref.refs_8_), channel_id=1, source_target_pairs={{0,1},{1,0},{2,3},{3,2},{4,5},{5,4},{6,7},{7,6},{8,9},{9,8},{10,11... | collective-permute-start | bytes 196616 | tf_op jit(solution)/shard_map/ppermute | solution.py:423
  44.5 2.1 %collective-permute-start.6 = (bf16[256,128]{1,0:T(8,128)(2,1)S(1)}, bf16[256,128]{1,0:T(8,128)(2,1)S(1)}, u32[]{:S(2)}, u32[]{:S(2)}) collective-permute-start(bf16[256,128]{1,0:T(8,128)(2,1)S(1)} %collective-permute-done.1.two_ref.refs_9_), channel_id=1, source_target_pairs={{0,1},{1,0},{2,3},{3,2},{4,5},{5,4},{6,7},{7,6},{8,9},{9,8},{10,11... | collective-permute-start | bytes 196616 | tf_op jit(solution)/shard_map/ppermute | solution.py:423
  45.0 3.0 %collective-permute-start.7 = (bf16[2,256,128]{2,1,0:T(8,128)(2,1)S(1)}, bf16[2,256,128]{2,1,0:T(8,128)(2,1)S(1)}, u32[]{:S(2)}, u32[]{:S(2)}) collective-permute-start(bf16[2,256,128]{2,1,0:T(8,128)(2,1)S(1)} %collective-permute-done.2.refs_10_), channel_id=1, source_target_pairs={{0,1},{1,0},{2,3},{3,2},{4,5},{5,4},{6,7},{7,6},{8,9},{9,8},{10,11... | collective-permute-start | bytes 393224 | tf_op jit(solution)/shard_map/ppermute | solution.py:423
  45.0 5.4 %collective-permute-start.8 = (bf16[2,256,128]{2,1,0:T(8,128)(2,1)S(1)}, bf16[2,256,128]{2,1,0:T(8,128)(2,1)S(1)}, u32[]{:S(2)}, u32[]{:S(2)}) collective-permute-start(bf16[2,256,128]{2,1,0:T(8,128)(2,1)S(1)} %collective-permute-done.3.refs_11_), channel_id=1, source_target_pairs={{0,1},{1,0},{2,3},{3,2},{4,5},{5,4},{6,7},{7,6},{8,9},{9,8},{10,11... | collective-permute-start | bytes 393224 | tf_op jit(solution)/shard_map/ppermute | solution.py:423
  45.6 4.9 %collective-permute-start.9 = (bf16[2,256,128]{2,1,0:T(8,128)(2,1)S(1)}, bf16[2,256,128]{2,1,0:T(8,128)(2,1)S(1)}, u32[]{:S(2)}, u32[]{:S(2)}) collective-permute-start(bf16[2,256,128]{2,1,0:T(8,128)(2,1)S(1)} %collective-permute-done.4.refs_12_), channel_id=1, source_target_pairs={{0,1},{1,0},{2,3},{3,2},{4,5},{5,4},{6,7},{7,6},{8,9},{9,8},{10,11... | collective-permute-start | bytes 393224 | tf_op jit(solution)/shard_map/ppermute | solution.py:423
  46.1 4.3 %collective-permute-start.10 = (bf16[64,256]{1,0:T(8,128)(2,1)S(1)}, bf16[64,256]{1,0:T(8,128)(2,1)S(1)}, u32[]{:S(2)}, u32[]{:S(2)}) collective-permute-start(bf16[64,256]{1,0:T(8,128)(2,1)S(1)} %convolution_convert_fusion.1.refs_18_), channel_id=1, source_target_pairs={{0,1},{1,0},{2,3},{3,2},{4,5},{5,4},{6,7},{7,6},{8,9},{9,8},{10,11... | collective-permute-start | bytes 98312 | tf_op jit(solution)/shard_map/ppermute | solution.py:430
  46.6 5.4 %collective-permute-start.11 = (bf16[64,256]{1,0:T(8,128)(2,1)S(1)}, bf16[64,256]{1,0:T(8,128)(2,1)S(1)}, u32[]{:S(2)}, u32[]{:S(2)}) collective-permute-start(bf16[64,256]{1,0:T(8,128)(2,1)S(1)} %convolution_convert_fusion.1.refs_18_), channel_id=1, source_target_pairs={{0,2},{1,3},{2,0},{3,1},{4,6},{5,7},{6,4},{7,5},{8,10},{9,11},{10,... | collective-permute-start | bytes 98312 | tf_op jit(solution)/shard_map/ppermute | solution.py:430
  48.0 5.2 %collective-permute-start.12 = (bf16[64,256]{1,0:T(8,128)(2,1)S(1)}, bf16[64,256]{1,0:T(8,128)(2,1)S(1)}, u32[]{:S(2)}, u32[]{:S(2)}) collective-permute-start(bf16[64,256]{1,0:T(8,128)(2,1)S(1)} %convolution_convert_fusion.1.refs_18_), channel_id=1, source_target_pairs={{0,3},{1,2},{2,1},{3,0},{4,7},{5,6},{6,5},{7,4},{8,11},{9,10},{10,... | collective-permute-start | bytes 98312 | tf_op jit(solution)/shard_map/ppermute | solution.py:430
  64.9 2.2 %copy-start.10 = (s32[2,64]{1,0:T(2,128)S(1)}, s32[2,64]{1,0:T(2,128)}, u32[]{:S(2)}) copy-start(s32[2,64]{1,0:T(2,128)} %mask_ref.1) | copy-start | bytes 1540
  66.9 6.0 %collective-permute-start.13 = (bf16[2304,128]{1,0:T(8,128)(2,1)S(1)}, bf16[2304,128]{1,0:T(8,128)(2,1)S(1)}, u32[]{:S(2)}, u32[]{:S(2)}) collective-permute-start(bf16[2304,128]{1,0:T(8,128)(2,1)S(1)} %kv_send.1), channel_id=1, source_target_pairs={{0,1},{1,0},{2,3},{3,2},{4,5},{5,4},{6,7},{7,6},{8,9},{9,8},{10,11... | collective-permute-start | bytes 1769480 | tf_op jit(solution)/shard_map/ppermute | solution.py:455
  67.2 5.9 %collective-permute-start.14 = (bf16[64,256]{1,0:T(8,128)(2,1)S(1)}, bf16[64,256]{1,0:T(8,128)(2,1)S(1)}, u32[]{:S(2)}, u32[]{:S(2)}) collective-permute-start(bf16[64,256]{1,0:T(8,128)(2,1)S(1)} %get-tuple-element.70), channel_id=1, source_target_pairs={{0,1},{1,0},{2,3},{3,2},{4,5},{5,4},{6,7},{7,6},{8,9},{9,8},{10,11... | collective-permute-start | bytes 98312 | tf_op jit(solution)/shard_map/ppermute | solution.py:453
  67.6 5.5 %collective-permute-start.15 = (bf16[64,256]{1,0:T(8,128)(2,1)S(1)}, bf16[64,256]{1,0:T(8,128)(2,1)S(1)}, u32[]{:S(2)}, u32[]{:S(2)}) collective-permute-start(bf16[64,256]{1,0:T(8,128)(2,1)S(1)} %get-tuple-element.70), channel_id=1, source_target_pairs={{0,2},{1,3},{2,0},{3,1},{4,6},{5,7},{6,4},{7,5},{8,10},{9,11},{10,... | collective-permute-start | bytes 98312 | tf_op jit(solution)/shard_map/ppermute | solution.py:453
  69.7 5.1 %collective-permute-start.16 = (bf16[64,256]{1,0:T(8,128)(2,1)S(1)}, bf16[64,256]{1,0:T(8,128)(2,1)S(1)}, u32[]{:S(2)}, u32[]{:S(2)}) collective-permute-start(bf16[64,256]{1,0:T(8,128)(2,1)S(1)} %get-tuple-element.70), channel_id=1, source_target_pairs={{0,3},{1,2},{2,1},{3,0},{4,7},{5,6},{6,5},{7,4},{8,11},{9,10},{10,... | collective-permute-start | bytes 98312 | tf_op jit(solution)/shard_map/ppermute | solution.py:453
  72.8 41.5 %copy-start.4 = (f32[1,2048]{1,0:T(1,128)S(1)}, f32[1,2048]{1,0:T(1,128)}, u32[]{:S(2)}) copy-start(f32[1,2048]{1,0:T(1,128)} %param.17) | copy-start | bytes 24580
  72.8 41.5 %copy-start.6 = (f32[1,512]{1,0:T(1,128)S(1)}, f32[1,512]{1,0:T(1,128)}, u32[]{:S(2)}) copy-start(f32[1,512]{1,0:T(1,128)} %param.20) | copy-start | bytes 6148
  72.8 41.5 %copy-start.7 = (f32[1,2048]{1,0:T(1,128)S(1)}, f32[1,2048]{1,0:T(1,128)}, u32[]{:S(2)}) copy-start(f32[1,2048]{1,0:T(1,128)} %param.18) | copy-start | bytes 24580
  72.9 41.5 %copy-start.8 = (f32[1,2048]{1,0:T(1,128)S(1)}, f32[1,2048]{1,0:T(1,128)}, u32[]{:S(2)}) copy-start(f32[1,2048]{1,0:T(1,128)} %param.19) | copy-start | bytes 24580
  72.9 41.5 %copy-start.11 = (f32[1,512]{1,0:T(1,128)S(1)}, f32[1,512]{1,0:T(1,128)}, u32[]{:S(2)}) copy-start(f32[1,512]{1,0:T(1,128)} %param.21) | copy-start | bytes 6148
  72.9 41.5 %copy-start.12 = (f32[1,512]{1,0:T(1,128)S(1)}, f32[1,512]{1,0:T(1,128)}, u32[]{:S(2)}) copy-start(f32[1,512]{1,0:T(1,128)} %param.22) | copy-start | bytes 6148
  76.1 38.2 %all-to-all-start.1 = ((bf16[64,20,128]{2,1,0:T(8,128)(2,1)}), bf16[64,20,128]{2,1,0:T(8,128)(2,1)S(1)}, u32[]{:S(2)}, u32[]{:S(2)}) async-start(bf16[64,20,128]{2,1,0:T(8,128)(2,1)} %pad_maximum_fusion), calls=%async_computation.1 | async-start | bytes 786432 | tf_op jit(solution)/shard_map/all_to_all | solution.py:469
  84.0 11.3 %collective-permute-start.17 = (bf16[2,256,128]{2,1,0:T(8,128)(2,1)S(1)}, bf16[2,256,128]{2,1,0:T(8,128)(2,1)S(1)}, u32[]{:S(2)}, u32[]{:S(2)}) collective-permute-start(bf16[2,256,128]{2,1,0:T(8,128)(2,1)S(1)} %get-tuple-element.64), channel_id=1, source_target_pairs={{0,12},{4,0},{8,4},{12,8},{16,28},{20,16},{24,20},{28,24},{32,44},... | collective-permute-start | bytes 393224 | tf_op jit(solution)/shard_map/ppermute | solution.py:412
  86.8 10.1 %collective-permute-start.18 = (bf16[2,256,128]{2,1,0:T(8,128)(2,1)S(1)}, bf16[2,256,128]{2,1,0:T(8,128)(2,1)S(1)}, u32[]{:S(2)}, u32[]{:S(2)}) collective-permute-start(bf16[2,256,128]{2,1,0:T(8,128)(2,1)S(1)} %get-tuple-element.65), channel_id=1, source_target_pairs={{0,8},{4,12},{8,0},{12,4},{16,24},{20,28},{24,16},{28,20},{32,40},... | collective-permute-start | bytes 393224 | tf_op jit(solution)/shard_map/ppermute | solution.py:412
  87.6 11.2 %collective-permute-start.19 = (bf16[2,256,128]{2,1,0:T(8,128)(2,1)S(1)}, bf16[2,256,128]{2,1,0:T(8,128)(2,1)S(1)}, u32[]{:S(2)}, u32[]{:S(2)}) collective-permute-start(bf16[2,256,128]{2,1,0:T(8,128)(2,1)S(1)} %get-tuple-element.66), channel_id=1, source_target_pairs={{0,4},{4,8},{8,12},{12,0},{16,20},{20,24},{24,28},{28,16},{32,36},... | collective-permute-start | bytes 393224 | tf_op jit(solution)/shard_map/ppermute | solution.py:412
  99.5 9.5 %collective-permute-start.20 = (bf16[256,128]{1,0:T(8,128)(2,1)S(1)}, bf16[256,128]{1,0:T(8,128)(2,1)S(1)}, u32[]{:S(2)}, u32[]{:S(2)}) collective-permute-start(bf16[256,128]{1,0:T(8,128)(2,1)S(1)} %get-tuple-element.67), channel_id=1, source_target_pairs={{0,0},{1,2},{2,1},{3,3},{4,4},{5,6},{6,5},{7,7},{8,8},{9,10},{10,9... | collective-permute-start | bytes 196616 | tf_op jit(solution)/shard_map/ppermute | solution.py:483
  102.5 7.5 %collective-permute-start.21 = (bf16[256,128]{1,0:T(8,128)(2,1)S(1)}, bf16[256,128]{1,0:T(8,128)(2,1)S(1)}, u32[]{:S(2)}, u32[]{:S(2)}) collective-permute-start(bf16[256,128]{1,0:T(8,128)(2,1)S(1)} %get-tuple-element.68), channel_id=1, source_target_pairs={{0,240},{1,242},{2,241},{3,243},{4,244},{5,246},{6,245},{7,247},{8... | collective-permute-start | bytes 196616 | tf_op jit(solution)/shard_map/ppermute | solution.py:483
  106.6 7.0 %collective-permute-start.22 = (bf16[256,128]{1,0:T(8,128)(2,1)S(1)}, bf16[256,128]{1,0:T(8,128)(2,1)S(1)}, u32[]{:S(2)}, u32[]{:S(2)}) collective-permute-start(bf16[256,128]{1,0:T(8,128)(2,1)S(1)} %get-tuple-element.69), channel_id=1, source_target_pairs={{0,224},{1,226},{2,225},{3,227},{4,228},{5,230},{6,229},{7,231},{8... | collective-permute-start | bytes 196616 | tf_op jit(solution)/shard_map/ppermute | solution.py:483

commit v2 on v1

--- a/solution.py
+++ b/solution.py
@@ -38,10 +38,9 @@
     return jnp.where(near, step + (0 if late else COLUMNS), step + (COLUMNS if late else 0))
 
 
-def pack_kernel(spot_ref, own_ref, one_ref, two_ref, fq_ref, go_ref, mask_ref, *outs):
+def pack_kernel(spot_ref, own_ref, one_ref, two_ref, *outs):
     column = spot_ref[1]
-    packs, (fq_out, go_out, mask_out) = outs[: COLUMNS - 1], outs[COLUMNS - 1 :]
-    for n, out in enumerate(packs):
+    for n, out in enumerate(outs):
         step = n + 1
         out[0] = one_ref[...]
 
@@ -53,6 +52,19 @@
         def _():
             out[1] = two_ref[...]
 
+
+def pack(spot, own, one, two):
+    vmem = pl.BlockSpec(memory_space=pltpu.VMEM)
+    return pl.pallas_call(
+        pack_kernel,
+        in_specs=[pl.BlockSpec(memory_space=pltpu.SMEM)] + [vmem] * 3,
+        out_shape=[jax.ShapeDtypeStruct((2,) + own.shape, own.dtype)] * (COLUMNS - 1),
+        compiler_params=pltpu.CompilerParams(vmem_limit_bytes=8 << 20),
+        name="pack",
+    )(spot, own, one, two)
+
+
+def stage_kernel(fq_ref, go_ref, mask_ref, fq_out, go_out, mask_out):
     for h in range(fq_out.shape[0]):
         lanes = pl.ds(h * HEAD_SIZE, HEAD_SIZE)
         fq_out[h] = fq_ref[:, lanes]
@@ -60,19 +72,15 @@
     mask_out[...] = mask_ref[...]
 
 
-def pack(spot, own, one, two, fq, go, masks):
+def stage(fq, go, masks):
     tokens, width = fq.shape
-    vmem = pl.BlockSpec(memory_space=pltpu.VMEM)
     by_head = jax.ShapeDtypeStruct((width // HEAD_SIZE, tokens, HEAD_SIZE), jnp.bfloat16)
-    *packs, fq, go, masks = pl.pallas_call(
-        pack_kernel,
-        in_specs=[pl.BlockSpec(memory_space=pltpu.SMEM)] + [vmem] * 6,
-        out_shape=[jax.ShapeDtypeStruct((2,) + own.shape, own.dtype)] * (COLUMNS - 1)
-        + [by_head, by_head, jax.ShapeDtypeStruct(masks.shape, masks.dtype)],
+    return pl.pallas_call(
+        stage_kernel,
+        out_shape=[by_head, by_head, jax.ShapeDtypeStruct(masks.shape, masks.dtype)],
         compiler_params=pltpu.CompilerParams(vmem_limit_bytes=8 << 20),
-        name="pack",
-    )(spot, own, one, two, fq, go, masks)
-    return packs, fq, go, masks
+        name="stage",
+    )(fq, go, masks)
 
 
 def column_of(row):
@@ -143,17 +151,13 @@
             fq_ref[head].astype(jnp.float32) + adapter_scale * dot32(mp, up_of(head), NN)
         ).astype(jnp.bfloat16)
 
-    def products(head, slot, d, top):
+    def scores(head, slot, d, top):
         s = dot32(k_s[rows(d), :], q_ref[head], NT)
         allowed = place_s[...] >= low + distance(d, column) * tokens
         if d == 0:
             allowed = allowed & (place_s[...] <= lax.broadcasted_iota(jnp.int32, s.shape, 1))
         s = jnp.where(allowed, s, -1e30)
         s_s[slot, rows(d), :] = s
-        gw_s[slot, rows(d), :] = dot32(v_s[rows(d), :], go_ref[head], NT)
-        if isinstance(head, int):
-            kt_s[:, rows(d)] = k_s[rows(d), :].T
-            vt_s[:, rows(d)] = v_s[rows(d), :].T
         return fold(jnp.maximum, top, s)
 
     lowest = jnp.full((8, tokens), -1e30, jnp.float32)
@@ -161,7 +165,9 @@
     make_query(0)
     top = lowest
     for d in range(tiles):
-        top = products(0, 0, d, top)
+        top = scores(0, 0, d, top)
+        kt_s[:, rows(d)] = k_s[rows(d), :].T
+        vt_s[:, rows(d)] = v_s[rows(d), :].T
 
     def one_head(head, top, last):
         slot = lax.rem(head, 2)
@@ -174,8 +180,7 @@
             p = jnp.exp2((s_s[slot, rows(d), :] - top) * exponent)
             a_s[slot, rows(d), :] = p
             total = fold(jnp.add, total, p)
-            if not last:
-                next_top = products(head + 1, 1 - slot, d, next_top)
+            gw_s[slot, rows(d), :] = dot32(v_s[rows(d), :], go_ref[head], NT)
         inverse = 1.0 / jnp.sum(total, axis=0, keepdims=True)
         acc_s[...] = jnp.zeros_like(acc_s)
 
@@ -188,6 +193,8 @@
             gw_s[slot, rows(d), :] = a
             acc_s[...] += dot32(vt_s[:, rows(d)], w_half, NN)
             dots = fold(jnp.add, dots, a)
+            if not last:
+                next_top = scores(head + 1, 1 - slot, d, next_top)
         out_ref[:, lanes(head)] = acc_s[...].T.astype(jnp.bfloat16)
         dots = jnp.sum(dots, axis=0, keepdims=True) * inverse
         acc_s[...] = jnp.zeros_like(acc_s)
@@ -338,8 +345,16 @@
     )(spot, own, one, two, *packs)
 
 
-def spread_kernel(down_ref, up_ref, out_ref):
-    row = jnp.concatenate([down_ref[...], up_ref[...]], 0).astype(jnp.bfloat16)
+def spread_kernel(down_ref, up_ref, out_ref, down_s, up_s, sems):
+    loads = [
+        pltpu.make_async_copy(down_ref, down_s, sems.at[0]),
+        pltpu.make_async_copy(up_ref, up_s, sems.at[1]),
+    ]
+    for load in loads:
+        load.start()
+    for load in loads:
+        load.wait()
+    row = jnp.concatenate([down_s[...], up_s[...]], 0).astype(jnp.bfloat16)
     for n in range(out_ref.shape[0]):
         out_ref[n] = row
 
@@ -347,8 +362,14 @@
 def spread(down, up, copies):
     return pl.pallas_call(
         spread_kernel,
+        in_specs=[pl.BlockSpec(memory_space=pl.ANY)] * 2,
+        scratch_shapes=[
+            pltpu.VMEM(down.shape, down.dtype),
+            pltpu.VMEM(up.shape, up.dtype),
+            pltpu.SemaphoreType.DMA((2,)),
+        ],
         out_shape=jax.ShapeDtypeStruct((copies, down.shape[0] + up.shape[0], 128), jnp.bfloat16),
-        compiler_params=pltpu.CompilerParams(vmem_limit_bytes=4 << 20),
+        compiler_params=pltpu.CompilerParams(vmem_limit_bytes=63 << 20),
         name="spread",
     )(down, up)
 
@@ -416,10 +437,9 @@
     down_rows, up_rows = model // 128, width // 128
     row = spread(adapter_down.reshape(down_rows, 128), adapter_up.reshape(up_rows, 128), ctx)
     gathered = lax.all_to_all(row, "ctx", split_axis=0, concat_axis=0)
-    packs, queries_in, grads_in, masks_in = pack(
-        spot, mine, one, two, frozen_queries, output_gradient, rank_keep_mask
-    )
+    packs = pack(spot, mine, one, two)
     direct = [one, two] + [across(p, n + 1) for n, p in enumerate(packs)]
+    queries_in, grads_in, masks_in = stage(frozen_queries, output_gradient, rank_keep_mask)
     swapped = [lax.ppermute(piece, "head", swap) for piece in direct]
 
     down = gathered[:, :down_rows].reshape(ranks, model)
@@ -429,9 +449,10 @@
     others = [[(h, h ^ k) for h in range(head_count)] for k in range(1, head_count)]
     parts = [part] + [lax.ppermute(part, "head", pairs) for pairs in others]
 
-    length = group_length[kv_head]
+    length = jnp.where(kv_head == 0, group_length[0:1], group_length[1:2])
+    shift = jnp.where(kv_head == 0, group_shift[0:1], group_shift[1:2])
     within = jnp.arange(tokens, dtype=jnp.int32)
-    rolled = (ctx_place * tokens + within - group_shift[kv_head]) % (tokens * ctx)
+    rolled = (ctx_place * tokens + within - shift) % (tokens * ctx)
     low = (within - rolled % length).reshape(1, tokens)
     keep_masks = rank_keep_mask.astype(jnp.float32)[:, :, None]
     out, query_gradient, low_rank_part, grad_up_part, queries, weights, grad_scores = attention(

time: 118 us -> 114 us (0.966)
  waiting for transfers between devices: 30.4 us -> 28.5 us
  starting transfers between devices: 52.2 us -> 50.7 us
  between operations: 2.27 us -> 3.59 us
  local copies, waits for them, and re-layouts: 8.26 us -> 6.98 us
  matrix products: 0.78 us -> 2 us
    slice x0 -> x2, local copies, waits for them, and re-layouts: none -> 2.63 us  [the longest x1 1.31 us: on_device(): shift = jnp.where(kv_head == 0, group_shift[0:1], group_shift[1:2])]
    dynamic_slice x3 -> x1, local copies, waits for them, and re-layouts: 3.45 us -> 0.97 us  [on_device(): lax.dynamic_slice_in_dim(key_value_rows, core * key_width + kv_head * HEA...]
    ppermute x3, waiting for transfers between devices: 2.77 us -> 0.72 us  [on_device(): parts = [part] + [lax.ppermute(part, 'head', pairs) for pairs in others]]
    all_to_all x1, starting transfers between devices: 7.93 us -> 6.4 us  [on_device(): received = lax.all_to_all(packed, 'ctx', split_axis=0, concat_axis=0)]
    unnamed x28 -> x24, local copies, waits for them, and re-layouts: 4.14 us -> 2.67 us
    pallas_call x1, Pallas kernels: 11.7 us -> 10.3 us  [attention(): pl.pallas_call(functools.partial(attention_kernel, tokens=tokens, heads=h...]
    dot_general x2, matrix products: 0.78 us -> 2 us  [dot32(): return lax.dot_general(a, b, dims, preferred_element_type=jnp.float32)]
  transfers between devices with their start and end apart: 25 -> 25, of which waited for: 10 -> 10; matrix products, arithmetic and copies ran while one was open for 5% -> 6% of each run, Pallas kernels for 3% -> 3%
where the time goes in v2:
time: 114 us; the launch traced here: 112 us
  starting transfers between devices  50.7 us (44%)
  waiting for transfers between devices  28.5 us (25%)
  Pallas kernels  18.7 us (16%)
  local copies, waits for them, and re-layouts  6.98 us (6%)
  between operations  3.59 us (3%)
  matrix products  2 us (2%)
  other arithmetic  1.69 us (1%)
    all_to_all x1, starting transfers between devices, on_device(): gathered = lax.all_to_all(row, 'ctx', split_axis=0, concat_axis=0)  13.2 us
    ppermute x2, waiting for transfers between devices, along(): lax.ppermute(piece, 'ctx', [(i, (i + step) % ctx) for i in range(ctx)])  10.8 us
    ppermute x6, waiting for transfers between devices, across(): return lax.ppermute(piece, 'ctx', pairs)  10.4 us
    pallas_call x1, Pallas kernels, attention(): pl.pallas_call(functools.partial(attention_kernel, tokens=tokens, heads=h...  10.3 us
    ppermute x6, starting transfers between devices, across(): return lax.ppermute(piece, 'ctx', pairs)  9.95 us
    ppermute x3, starting transfers between devices, home(): return lax.ppermute(piece, ('ctx', 'head'), pairs).astype(jnp.float32)  8.84 us
    all_to_all x1, starting transfers between devices, on_device(): received = lax.all_to_all(packed, 'ctx', split_axis=0, concat_axis=0)  6.4 us
    ppermute x3, waiting for transfers between devices, home(): return lax.ppermute(piece, ('ctx', 'head'), pairs).astype(jnp.float32)  4.59 us
  transfers between devices with their start and end apart: 25, of which 10 were waited for; matrix products, arithmetic and copies ran while one was open for 6% of the time, Pallas kernels for 3%

profile of v2, /device:TPU:6, one launch (start us, length us, event | category | flops | bytes accessed | tf_op | source)
XLA Modules:
  0.0 112.2 jit_solution(8647413358815959262)
XLA Ops:
  0.6 1.5 %spread.1 = bf16[64,20,128]{2,1,0:T(8,128)(2,1)} custom-call(f32[16,128]{1,0:T(8,128)} %bitcast.34, f32[4,128]{1,0:T(4,128)} %bitcast.36), custom_call_target="tpu_custom_call" | custom-call | tf_op jit(solution)/shard_map/spread/pallas_call | solution.py:363
  2.2 13.2 %all-to-all-start = ((bf16[64,20,128]{2,1,0:T(8,128)(2,1)}), bf16[64,20,128]{2,1,0:T(8,128)(2,1)S(1)}, u32[]{:S(2)}, u32[]{:S(2)}) async-start(bf16[64,20,128]{2,1,0:T(8,128)(2,1)} %spread.1), calls=%async_computation | async-start | bytes 786432 | tf_op jit(solution)/shard_map/all_to_all | solution.py:439
  15.4 1.0 constant_dynamic-slice_fusion.1
  16.4 1.6 %collective-permute-start = (bf16[256,128]{1,0:T(8,128)(2,1)S(1)}, bf16[256,128]{1,0:T(8,128)(2,1)S(1)}, u32[]{:S(2)}, u32[]{:S(2)}) collective-permute-start(bf16[256,128]{1,0:T(8,128)(2,1)S(1)} %get-tuple-element.81.own_ref), channel_id=1, source_target_pairs={{0,16},{4,20},{8,24},{12,28},{16,32},{20,36},{24,40},{28,44},{32,4... | collective-permute-start | bytes 196616 | tf_op jit(solution)/shard_map/ppermute | solution.py:429
  18.0 2.4 %collective-permute-start.1 = (bf16[256,128]{1,0:T(8,128)(2,1)S(1)}, bf16[256,128]{1,0:T(8,128)(2,1)S(1)}, u32[]{:S(2)}, u32[]{:S(2)}) collective-permute-start(bf16[256,128]{1,0:T(8,128)(2,1)S(1)} %get-tuple-element.81.own_ref), channel_id=1, source_target_pairs={{0,32},{4,36},{8,40},{12,44},{16,48},{20,52},{24,56},{28,60},{32,6... | collective-permute-start | bytes 196616 | tf_op jit(solution)/shard_map/ppermute | solution.py:429
  20.4 0.1 pad_add_fusion.spot_ref.refs_0_
  20.5 8.4 %collective-permute-done.one_ref.refs_8_ = bf16[256,128]{1,0:T(8,128)(2,1)S(1)} collective-permute-done((bf16[256,128]{1,0:T(8,128)(2,1)S(1)}, bf16[256,128]{1,0:T(8,128)(2,1)S(1)}, u32[]{:S(2)}, u32[]{:S(2)}) %collective-permute-start) | collective-permute-done | bytes 65568 | tf_op jit(solution)/shard_map/ppermute | solution.py:429
  28.9 2.4 %collective-permute-done.1.two_ref.refs_9_ = bf16[256,128]{1,0:T(8,128)(2,1)S(1)} collective-permute-done((bf16[256,128]{1,0:T(8,128)(2,1)S(1)}, bf16[256,128]{1,0:T(8,128)(2,1)S(1)}, u32[]{:S(2)}, u32[]{:S(2)}) %collective-permute-start.1) | collective-permute-done | bytes 65568 | tf_op jit(solution)/shard_map/ppermute | solution.py:429
  31.2 0.6 pack.1
  31.8 1.4 %collective-permute-start.2 = (bf16[2,256,128]{2,1,0:T(8,128)(2,1)S(1)}, bf16[2,256,128]{2,1,0:T(8,128)(2,1)S(1)}, u32[]{:S(2)}, u32[]{:S(2)}) collective-permute-start(bf16[2,256,128]{2,1,0:T(8,128)(2,1)S(1)} %get-tuple-element.48), channel_id=1, source_target_pairs={{0,4},{4,8},{8,12},{12,0},{16,20},{20,24},{24,28},{28,16},{32,36},... | collective-permute-start | bytes 393224 | tf_op jit(solution)/shard_map/ppermute | solution.py:433
  33.2 2.4 %collective-permute-start.3 = (bf16[2,256,128]{2,1,0:T(8,128)(2,1)S(1)}, bf16[2,256,128]{2,1,0:T(8,128)(2,1)S(1)}, u32[]{:S(2)}, u32[]{:S(2)}) collective-permute-start(bf16[2,256,128]{2,1,0:T(8,128)(2,1)S(1)} %get-tuple-element.49), channel_id=1, source_target_pairs={{0,8},{4,12},{8,0},{12,4},{16,24},{20,28},{24,16},{28,20},{32,40},... | collective-permute-start | bytes 393224 | tf_op jit(solution)/shard_map/ppermute | solution.py:433
  35.6 1.7 %collective-permute-start.4 = (bf16[2,256,128]{2,1,0:T(8,128)(2,1)S(1)}, bf16[2,256,128]{2,1,0:T(8,128)(2,1)S(1)}, u32[]{:S(2)}, u32[]{:S(2)}) collective-permute-start(bf16[2,256,128]{2,1,0:T(8,128)(2,1)S(1)} %get-tuple-element.50), channel_id=1, source_target_pairs={{0,12},{4,0},{8,4},{12,8},{16,28},{20,16},{24,20},{28,24},{32,44},... | collective-permute-start | bytes 393224 | tf_op jit(solution)/shard_map/ppermute | solution.py:433
  37.3 1.3 %fusion.11 = (s32[1]{0:T(128)}, s32[1]{0:T(128)}) fusion(s32[2]{0:T(128)} %param.24), kind=kLoop, calls=%fused_computation.27 | loop fusion | bytes 16 | tf_op jit(solution)/shard_map/slice | solution.py:452
  39.9 1.3 %fusion.10 = (s32[1]{0:T(128)}, s32[1]{0:T(128)}) fusion(s32[2]{0:T(128)} %param.25), kind=kLoop, calls=%fused_computation.26 | loop fusion | bytes 16 | tf_op jit(solution)/shard_map/slice | solution.py:453
  42.5 0.1 collective-permute-start.5
  42.6 0.5 collective-permute-start.6
  43.1 0.1 collective-permute-start.7
  43.2 0.4 collective-permute-start.8
  43.7 0.1 collective-permute-start.9
  43.8 1.7 %convolution_convert_fusion.1.refs_18_ = bf16[64,256]{1,0:T(8,128)(2,1)S(1)} fusion(bf16[256,2048]{1,0:T(8,128)(2,1)} %param.16, bf16[8,8,16,128]{3,2,1,0:T(8,128)(2,1)S(1)} %bitcast.43), kind=kOutput, calls=%fused_computation.2 | convolution fusion | flops 67125248 | bytes 1343488 | tf_op jit(solution)/shard_map/dot_general | solution.py:30
  45.5 0.5 collective-permute-start.10
  46.0 1.4 %collective-permute-start.11 = (bf16[64,256]{1,0:T(8,128)(2,1)S(1)}, bf16[64,256]{1,0:T(8,128)(2,1)S(1)}, u32[]{:S(2)}, u32[]{:S(2)}) collective-permute-start(bf16[64,256]{1,0:T(8,128)(2,1)S(1)} %convolution_convert_fusion.1.refs_18_), channel_id=1, source_target_pairs={{0,2},{1,3},{2,0},{3,1},{4,6},{5,7},{6,4},{7,5},{8,10},{9,11},{10,... | collective-permute-start | bytes 98312 | tf_op jit(solution)/shard_map/ppermute | solution.py:450
  47.4 1.6 %collective-permute-start.12 = (bf16[64,256]{1,0:T(8,128)(2,1)S(1)}, bf16[64,256]{1,0:T(8,128)(2,1)S(1)}, u32[]{:S(2)}, u32[]{:S(2)}) collective-permute-start(bf16[64,256]{1,0:T(8,128)(2,1)S(1)} %convolution_convert_fusion.1.refs_18_), channel_id=1, source_target_pairs={{0,3},{1,2},{2,1},{3,0},{4,7},{5,6},{6,5},{7,4},{8,11},{9,10},{10,... | collective-permute-start | bytes 98312 | tf_op jit(solution)/shard_map/ppermute | solution.py:450
  48.9 0.1 fusion.5.refs_5_
  49.1 0.0 copy-start
  49.1 0.9 copy-done
  50.0 0.9 copy-done.1
  51.0 0.7 copy-done.6
  51.7 0.1 stage.1
  51.8 0.7 collective-permute-done.12.refs_21_
  52.6 10.3 %attention.1 = (bf16[256,512]{1,0:T(8,128)(2,1)}, bf16[256,512]{1,0:T(8,128)(2,1)}, bf16[64,256]{1,0:T(8,128)(2,1)S(1)}, bf16[64,512]{1,0:T(8,128)(2,1)S(1)}, bf...) custom-call(s32[2]{0:T(128)S(1)} %pad_add_fusion.spot_ref.refs_0_, ...), custom_call_target="tpu_custom_call" | custom-call | flops 2415919104 | bytes 8388608 | tf_op jit(solution)/shard_map/attention/pallas_call | solution.py:223
  62.9 2.0 %kv_send.1 = bf16[2304,128]{1,0:T(8,128)(2,1)S(1)} custom-call(s32[2]{0:T(128)S(1)} %pad_add_fusion.spot_ref.refs_0_, bf16[4,2304,256]{2,1,0:T(8,128)(2,1)S(1)} %get-tuple-element.53.w_ref, bf16[4,2304,256]{2,1,0:T(8,128)(2,1)S(1)} %get-tuple-element.54.gs_ref, bf16[4,256,128]{2,1,0:T(8,128)(2,1)S(1)} %get-tuple-element.46.refs_2_.go_ref, ...), custom_call_target="tpu_custom_call" | custom-call | flops 603979776 | bytes 2097152 | tf_op jit(solution)/shard_map/kv_send/pallas_call | solution.py:283
  64.9 0.1 collective-permute-start.13
  65.1 0.6 collective-permute-start.14
  65.6 2.1 %collective-permute-start.15 = (bf16[64,256]{1,0:T(8,128)(2,1)S(1)}, bf16[64,256]{1,0:T(8,128)(2,1)S(1)}, u32[]{:S(2)}, u32[]{:S(2)}) collective-permute-start(bf16[64,256]{1,0:T(8,128)(2,1)S(1)} %get-tuple-element.70), channel_id=1, source_target_pairs={{0,2},{1,3},{2,0},{3,1},{4,6},{5,7},{6,4},{7,5},{8,10},{9,11},{10,... | collective-permute-start | bytes 98312 | tf_op jit(solution)/shard_map/ppermute | solution.py:474
  67.7 0.8 collective-permute-start.16
  68.6 2.1 %kv_keep.1.keep_ref = f32[2304,128]{1,0:T(8,128)S(1)} custom-call(s32[2]{0:T(128)S(1)} %pad_add_fusion.spot_ref.refs_0_, bf16[4,2304,256]{2,1,0:T(8,128)(2,1)S(1)} %get-tuple-element.53.w_ref, bf16[4,2304,256]{2,1,0:T(8,128)(2,1)S(1)} %get-tuple-element.54.gs_ref, bf16[4,256,128]{2,1,0:T(8,128)(2,1)S(1)} %get-tuple-element.46.refs_2_.go_ref, ...), custom_call_target="tpu_custom_call" | custom-call | flops 603979776 | bytes 2097152 | tf_op jit(solution)/shard_map/kv_keep/pallas_call | solution.py:283
  70.7 0.0 copy-start.2
  70.7 0.0 copy-start.3
  70.7 0.0 copy-start.4
  70.8 0.0 copy-start.5
  70.8 0.0 copy-start.8
  70.8 0.0 copy-start.9
  70.8 0.1 pair_sum.1
  70.9 0.1 collective-permute-done.15
  71.0 1.9 %collective-permute-done.16 = bf16[64,256]{1,0:T(8,128)(2,1)S(1)} collective-permute-done((bf16[64,256]{1,0:T(8,128)(2,1)S(1)}, bf16[64,256]{1,0:T(8,128)(2,1)S(1)}, u32[]{:S(2)}, u32[]{:S(2)}) %collective-permute-start.16) | collective-permute-done | bytes 32800 | tf_op jit(solution)/shard_map/ppermute | solution.py:474
  72.9 0.3 fusion
  73.4 0.8 pad_maximum_fusion
  74.1 6.4 %all-to-all-start.1 = ((bf16[64,20,128]{2,1,0:T(8,128)(2,1)}), bf16[64,20,128]{2,1,0:T(8,128)(2,1)S(1)}, u32[]{:S(2)}, u32[]{:S(2)}) async-start(bf16[64,20,128]{2,1,0:T(8,128)(2,1)} %pad_maximum_fusion), calls=%async_computation.1 | async-start | bytes 786432 | tf_op jit(solution)/shard_map/all_to_all | solution.py:490
  80.5 2.8 %collective-permute-start.17 = (bf16[2,256,128]{2,1,0:T(8,128)(2,1)S(1)}, bf16[2,256,128]{2,1,0:T(8,128)(2,1)S(1)}, u32[]{:S(2)}, u32[]{:S(2)}) collective-permute-start(bf16[2,256,128]{2,1,0:T(8,128)(2,1)S(1)} %get-tuple-element.64), channel_id=1, source_target_pairs={{0,12},{4,0},{8,4},{12,8},{16,28},{20,16},{24,20},{28,24},{32,44},... | collective-permute-start | bytes 393224 | tf_op jit(solution)/shard_map/ppermute | solution.py:433
  83.3 0.8 collective-permute-start.18
  84.2 0.9 collective-permute-start.19
  85.0 6.8 %collective-permute-done.17.rest_0_ = bf16[2,256,128]{2,1,0:T(8,128)(2,1)S(1)} collective-permute-done((bf16[2,256,128]{2,1,0:T(8,128)(2,1)S(1)}, bf16[2,256,128]{2,1,0:T(8,128)(2,1)S(1)}, u32[]{:S(2)}, u32[]{:S(2)}) %collective-permute-start.17) | collective-permute-done | bytes 131104 | tf_op jit(solution)/shard_map/ppermute | solution.py:433
  91.8 1.5 %collective-permute-done.18.rest_1_ = bf16[2,256,128]{2,1,0:T(8,128)(2,1)S(1)} collective-permute-done((bf16[2,256,128]{2,1,0:T(8,128)(2,1)S(1)}, bf16[2,256,128]{2,1,0:T(8,128)(2,1)S(1)}, u32[]{:S(2)}, u32[]{:S(2)}) %collective-permute-start.18) | collective-permute-done | bytes 131104 | tf_op jit(solution)/shard_map/ppermute | solution.py:433
  93.4 2.0 %collective-permute-done.19.rest_2_ = bf16[2,256,128]{2,1,0:T(8,128)(2,1)S(1)} collective-permute-done((bf16[2,256,128]{2,1,0:T(8,128)(2,1)S(1)}, bf16[2,256,128]{2,1,0:T(8,128)(2,1)S(1)}, u32[]{:S(2)}, u32[]{:S(2)}) %collective-permute-start.19) | collective-permute-done | bytes 131104 | tf_op jit(solution)/shard_map/ppermute | solution.py:433
  95.4 0.7 row_sum.1
  96.0 2.9 %collective-permute-start.20 = (bf16[256,128]{1,0:T(8,128)(2,1)S(1)}, bf16[256,128]{1,0:T(8,128)(2,1)S(1)}, u32[]{:S(2)}, u32[]{:S(2)}) collective-permute-start(bf16[256,128]{1,0:T(8,128)(2,1)S(1)} %get-tuple-element.67), channel_id=1, source_target_pairs={{0,0},{1,2},{2,1},{3,3},{4,4},{5,6},{6,5},{7,7},{8,8},{9,10},{10,9... | collective-permute-start | bytes 196616 | tf_op jit(solution)/shard_map/ppermute | solution.py:504
  99.0 4.2 %collective-permute-start.21 = (bf16[256,128]{1,0:T(8,128)(2,1)S(1)}, bf16[256,128]{1,0:T(8,128)(2,1)S(1)}, u32[]{:S(2)}, u32[]{:S(2)}) collective-permute-start(bf16[256,128]{1,0:T(8,128)(2,1)S(1)} %get-tuple-element.68), channel_id=1, source_target_pairs={{0,240},{1,242},{2,241},{3,243},{4,244},{5,246},{6,245},{7,247},{8... | collective-permute-start | bytes 196616 | tf_op jit(solution)/shard_map/ppermute | solution.py:504
  103.1 1.8 %collective-permute-start.22 = (bf16[256,128]{1,0:T(8,128)(2,1)S(1)}, bf16[256,128]{1,0:T(8,128)(2,1)S(1)}, u32[]{:S(2)}, u32[]{:S(2)}) collective-permute-start(bf16[256,128]{1,0:T(8,128)(2,1)S(1)} %get-tuple-element.69), channel_id=1, source_target_pairs={{0,224},{1,226},{2,225},{3,227},{4,228},{5,230},{6,229},{7,231},{8... | collective-permute-start | bytes 196616 | tf_op jit(solution)/shard_map/ppermute | solution.py:504
  104.9 0.6 constant_dynamic-slice_fusion.keep_ref
  105.5 0.9 collective-permute-done.21
  106.4 3.7 %collective-permute-done.22 = bf16[256,128]{1,0:T(8,128)(2,1)S(1)} collective-permute-done((bf16[256,128]{1,0:T(8,128)(2,1)S(1)}, bf16[256,128]{1,0:T(8,128)(2,1)S(1)}, u32[]{:S(2)}, u32[]{:S(2)}) %collective-permute-start.22) | collective-permute-done | bytes 65568 | tf_op jit(solution)/shard_map/ppermute | solution.py:504
  110.1 0.7 convert_add_fusion
  110.9 1.3 %adam.1 = (f32[16,128]{1,0:T(8,128)}, f32[16,128]{1,0:T(8,128)}, f32[16,128]{1,0:T(8,128)}, f32[4,128]{1,0:T(4,128)}, f32[4,128]{1,0:T(4,128)}, /*index=5*/f32[4,128]{1,0:T(4,128)}) custom-call(bf16[64,20,128]{2,1,0:T(8,128)(2,1)S(1)} %all-to-all-done.1.got_ref, f32[16,128]{1,0:T(8,128)S(1)} %bitcast.35, f32[16,128]{1,0:T(8,128)S(1)} %bitcast.38, ...), custom_call_target="tpu_custom_call" | custom-call | tf_op jit(solution)/shard_map/adam/pallas_call | solution.py:520
  (34 shorter events, 0.2 us)
Async XLA Ops:
  2.2 41.6 %all-to-all-start = ((bf16[64,20,128]{2,1,0:T(8,128)(2,1)}), bf16[64,20,128]{2,1,0:T(8,128)(2,1)S(1)}, u32[]{:S(2)}, u32[]{:S(2)}) async-start(bf16[64,20,128]{2,1,0:T(8,128)(2,1)} %spread.1), calls=%async_computation | async-start | bytes 786432 | tf_op jit(solution)/shard_map/all_to_all | solution.py:439
  16.4 12.5 %collective-permute-start = (bf16[256,128]{1,0:T(8,128)(2,1)S(1)}, bf16[256,128]{1,0:T(8,128)(2,1)S(1)}, u32[]{:S(2)}, u32[]{:S(2)}) collective-permute-start(bf16[256,128]{1,0:T(8,128)(2,1)S(1)} %get-tuple-element.81.own_ref), channel_id=1, source_target_pairs={{0,16},{4,20},{8,24},{12,28},{16,32},{20,36},{24,40},{28,44},{32,4... | collective-permute-start | bytes 196616 | tf_op jit(solution)/shard_map/ppermute | solution.py:429
  18.0 13.3 %collective-permute-start.1 = (bf16[256,128]{1,0:T(8,128)(2,1)S(1)}, bf16[256,128]{1,0:T(8,128)(2,1)S(1)}, u32[]{:S(2)}, u32[]{:S(2)}) collective-permute-start(bf16[256,128]{1,0:T(8,128)(2,1)S(1)} %get-tuple-element.81.own_ref), channel_id=1, source_target_pairs={{0,32},{4,36},{8,40},{12,44},{16,48},{20,52},{24,56},{28,60},{32,6... | collective-permute-start | bytes 196616 | tf_op jit(solution)/shard_map/ppermute | solution.py:429
  31.8 11.3 %collective-permute-start.2 = (bf16[2,256,128]{2,1,0:T(8,128)(2,1)S(1)}, bf16[2,256,128]{2,1,0:T(8,128)(2,1)S(1)}, u32[]{:S(2)}, u32[]{:S(2)}) collective-permute-start(bf16[2,256,128]{2,1,0:T(8,128)(2,1)S(1)} %get-tuple-element.48), channel_id=1, source_target_pairs={{0,4},{4,8},{8,12},{12,0},{16,20},{20,24},{24,28},{28,16},{32,36},... | collective-permute-start | bytes 393224 | tf_op jit(solution)/shard_map/ppermute | solution.py:433
  33.2 10.0 %collective-permute-start.3 = (bf16[2,256,128]{2,1,0:T(8,128)(2,1)S(1)}, bf16[2,256,128]{2,1,0:T(8,128)(2,1)S(1)}, u32[]{:S(2)}, u32[]{:S(2)}) collective-permute-start(bf16[2,256,128]{2,1,0:T(8,128)(2,1)S(1)} %get-tuple-element.49), channel_id=1, source_target_pairs={{0,8},{4,12},{8,0},{12,4},{16,24},{20,28},{24,16},{28,20},{32,40},... | collective-permute-start | bytes 393224 | tf_op jit(solution)/shard_map/ppermute | solution.py:433
  35.6 8.0 %collective-permute-start.4 = (bf16[2,256,128]{2,1,0:T(8,128)(2,1)S(1)}, bf16[2,256,128]{2,1,0:T(8,128)(2,1)S(1)}, u32[]{:S(2)}, u32[]{:S(2)}) collective-permute-start(bf16[2,256,128]{2,1,0:T(8,128)(2,1)S(1)} %get-tuple-element.50), channel_id=1, source_target_pairs={{0,12},{4,0},{8,4},{12,8},{16,28},{20,16},{24,20},{28,24},{32,44},... | collective-permute-start | bytes 393224 | tf_op jit(solution)/shard_map/ppermute | solution.py:433
  42.5 2.9 %collective-permute-start.5 = (bf16[256,128]{1,0:T(8,128)(2,1)S(1)}, bf16[256,128]{1,0:T(8,128)(2,1)S(1)}, u32[]{:S(2)}, u32[]{:S(2)}) collective-permute-start(bf16[256,128]{1,0:T(8,128)(2,1)S(1)} %collective-permute-done.one_ref.refs_8_), channel_id=1, source_target_pairs={{0,1},{1,0},{2,3},{3,2},{4,5},{5,4},{6,7},{7,6},{8,9},{9,8},{10,11... | collective-permute-start | bytes 196616 | tf_op jit(solution)/shard_map/ppermute | solution.py:443
  42.6 3.3 %collective-permute-start.6 = (bf16[256,128]{1,0:T(8,128)(2,1)S(1)}, bf16[256,128]{1,0:T(8,128)(2,1)S(1)}, u32[]{:S(2)}, u32[]{:S(2)}) collective-permute-start(bf16[256,128]{1,0:T(8,128)(2,1)S(1)} %collective-permute-done.1.two_ref.refs_9_), channel_id=1, source_target_pairs={{0,1},{1,0},{2,3},{3,2},{4,5},{5,4},{6,7},{7,6},{8,9},{9,8},{10,11... | collective-permute-start | bytes 196616 | tf_op jit(solution)/shard_map/ppermute | solution.py:443
  43.1 4.2 %collective-permute-start.7 = (bf16[2,256,128]{2,1,0:T(8,128)(2,1)S(1)}, bf16[2,256,128]{2,1,0:T(8,128)(2,1)S(1)}, u32[]{:S(2)}, u32[]{:S(2)}) collective-permute-start(bf16[2,256,128]{2,1,0:T(8,128)(2,1)S(1)} %collective-permute-done.2.refs_10_), channel_id=1, source_target_pairs={{0,1},{1,0},{2,3},{3,2},{4,5},{5,4},{6,7},{7,6},{8,9},{9,8},{10,11... | collective-permute-start | bytes 393224 | tf_op jit(solution)/shard_map/ppermute | solution.py:443
  43.2 8.6 %collective-permute-start.8 = (bf16[2,256,128]{2,1,0:T(8,128)(2,1)S(1)}, bf16[2,256,128]{2,1,0:T(8,128)(2,1)S(1)}, u32[]{:S(2)}, u32[]{:S(2)}) collective-permute-start(bf16[2,256,128]{2,1,0:T(8,128)(2,1)S(1)} %collective-permute-done.3.refs_11_), channel_id=1, source_target_pairs={{0,1},{1,0},{2,3},{3,2},{4,5},{5,4},{6,7},{7,6},{8,9},{9,8},{10,11... | collective-permute-start | bytes 393224 | tf_op jit(solution)/shard_map/ppermute | solution.py:443
  43.7 8.2 %collective-permute-start.9 = (bf16[2,256,128]{2,1,0:T(8,128)(2,1)S(1)}, bf16[2,256,128]{2,1,0:T(8,128)(2,1)S(1)}, u32[]{:S(2)}, u32[]{:S(2)}) collective-permute-start(bf16[2,256,128]{2,1,0:T(8,128)(2,1)S(1)} %collective-permute-done.4.refs_12_), channel_id=1, source_target_pairs={{0,1},{1,0},{2,3},{3,2},{4,5},{5,4},{6,7},{7,6},{8,9},{9,8},{10,11... | collective-permute-start | bytes 393224 | tf_op jit(solution)/shard_map/ppermute | solution.py:443
  45.5 6.4 %collective-permute-start.10 = (bf16[64,256]{1,0:T(8,128)(2,1)S(1)}, bf16[64,256]{1,0:T(8,128)(2,1)S(1)}, u32[]{:S(2)}, u32[]{:S(2)}) collective-permute-start(bf16[64,256]{1,0:T(8,128)(2,1)S(1)} %convolution_convert_fusion.1.refs_18_), channel_id=1, source_target_pairs={{0,1},{1,0},{2,3},{3,2},{4,5},{5,4},{6,7},{7,6},{8,9},{9,8},{10,11... | collective-permute-start | bytes 98312 | tf_op jit(solution)/shard_map/ppermute | solution.py:450
  46.0 5.9 %collective-permute-start.11 = (bf16[64,256]{1,0:T(8,128)(2,1)S(1)}, bf16[64,256]{1,0:T(8,128)(2,1)S(1)}, u32[]{:S(2)}, u32[]{:S(2)}) collective-permute-start(bf16[64,256]{1,0:T(8,128)(2,1)S(1)} %convolution_convert_fusion.1.refs_18_), channel_id=1, source_target_pairs={{0,2},{1,3},{2,0},{3,1},{4,6},{5,7},{6,4},{7,5},{8,10},{9,11},{10,... | collective-permute-start | bytes 98312 | tf_op jit(solution)/shard_map/ppermute | solution.py:450
  47.4 5.2 %collective-permute-start.12 = (bf16[64,256]{1,0:T(8,128)(2,1)S(1)}, bf16[64,256]{1,0:T(8,128)(2,1)S(1)}, u32[]{:S(2)}, u32[]{:S(2)}) collective-permute-start(bf16[64,256]{1,0:T(8,128)(2,1)S(1)} %convolution_convert_fusion.1.refs_18_), channel_id=1, source_target_pairs={{0,3},{1,2},{2,1},{3,0},{4,7},{5,6},{6,5},{7,4},{8,11},{9,10},{10,... | collective-permute-start | bytes 98312 | tf_op jit(solution)/shard_map/ppermute | solution.py:450
  49.1 1.0 copy-start
  50.0 0.9 copy-start.1
  51.0 0.7 copy-start.6
  62.9 2.1 %copy-start.7 = (s32[2,64]{1,0:T(2,128)S(1)}, s32[2,64]{1,0:T(2,128)}, u32[]{:S(2)}) copy-start(s32[2,64]{1,0:T(2,128)} %mask_ref.1) | copy-start | bytes 1540
  64.9 5.9 %collective-permute-start.13 = (bf16[2304,128]{1,0:T(8,128)(2,1)S(1)}, bf16[2304,128]{1,0:T(8,128)(2,1)S(1)}, u32[]{:S(2)}, u32[]{:S(2)}) collective-permute-start(bf16[2304,128]{1,0:T(8,128)(2,1)S(1)} %kv_send.1), channel_id=1, source_target_pairs={{0,1},{1,0},{2,3},{3,2},{4,5},{5,4},{6,7},{7,6},{8,9},{9,8},{10,11... | collective-permute-start | bytes 1769480 | tf_op jit(solution)/shard_map/ppermute | solution.py:476
  65.1 7.9 %copy-start.10 = (bf16[256,2048]{1,0:T(8,128)(2,1)S(1)}, bf16[256,2048]{1,0:T(8,128)(2,1)}, u32[]{:S(2)}) copy-start(bf16[256,2048]{1,0:T(8,128)(2,1)} %param.16) | copy-start | bytes 3145732
  65.1 5.9 %collective-permute-start.14 = (bf16[64,256]{1,0:T(8,128)(2,1)S(1)}, bf16[64,256]{1,0:T(8,128)(2,1)S(1)}, u32[]{:S(2)}, u32[]{:S(2)}) collective-permute-start(bf16[64,256]{1,0:T(8,128)(2,1)S(1)} %get-tuple-element.70), channel_id=1, source_target_pairs={{0,1},{1,0},{2,3},{3,2},{4,5},{5,4},{6,7},{7,6},{8,9},{9,8},{10,11... | collective-permute-start | bytes 98312 | tf_op jit(solution)/shard_map/ppermute | solution.py:474
  65.6 5.4 %collective-permute-start.15 = (bf16[64,256]{1,0:T(8,128)(2,1)S(1)}, bf16[64,256]{1,0:T(8,128)(2,1)S(1)}, u32[]{:S(2)}, u32[]{:S(2)}) collective-permute-start(bf16[64,256]{1,0:T(8,128)(2,1)S(1)} %get-tuple-element.70), channel_id=1, source_target_pairs={{0,2},{1,3},{2,0},{3,1},{4,6},{5,7},{6,4},{7,5},{8,10},{9,11},{10,... | collective-permute-start | bytes 98312 | tf_op jit(solution)/shard_map/ppermute | solution.py:474
  67.7 5.2 %collective-permute-start.16 = (bf16[64,256]{1,0:T(8,128)(2,1)S(1)}, bf16[64,256]{1,0:T(8,128)(2,1)S(1)}, u32[]{:S(2)}, u32[]{:S(2)}) collective-permute-start(bf16[64,256]{1,0:T(8,128)(2,1)S(1)} %get-tuple-element.70), channel_id=1, source_target_pairs={{0,3},{1,2},{2,1},{3,0},{4,7},{5,6},{6,5},{7,4},{8,11},{9,10},{10,... | collective-permute-start | bytes 98312 | tf_op jit(solution)/shard_map/ppermute | solution.py:474
  70.7 40.1 %copy-start.2 = (f32[1,2048]{1,0:T(1,128)S(1)}, f32[1,2048]{1,0:T(1,128)}, u32[]{:S(2)}) copy-start(f32[1,2048]{1,0:T(1,128)} %param.17) | copy-start | bytes 24580
  70.7 40.1 %copy-start.3 = (f32[1,512]{1,0:T(1,128)S(1)}, f32[1,512]{1,0:T(1,128)}, u32[]{:S(2)}) copy-start(f32[1,512]{1,0:T(1,128)} %param.20) | copy-start | bytes 6148
  70.7 40.1 %copy-start.4 = (f32[1,2048]{1,0:T(1,128)S(1)}, f32[1,2048]{1,0:T(1,128)}, u32[]{:S(2)}) copy-start(f32[1,2048]{1,0:T(1,128)} %param.18) | copy-start | bytes 24580
  70.8 40.1 %copy-start.5 = (f32[1,2048]{1,0:T(1,128)S(1)}, f32[1,2048]{1,0:T(1,128)}, u32[]{:S(2)}) copy-start(f32[1,2048]{1,0:T(1,128)} %param.19) | copy-start | bytes 24580
  70.8 40.1 %copy-start.8 = (f32[1,512]{1,0:T(1,128)S(1)}, f32[1,512]{1,0:T(1,128)}, u32[]{:S(2)}) copy-start(f32[1,512]{1,0:T(1,128)} %param.21) | copy-start | bytes 6148
  70.8 40.1 %copy-start.9 = (f32[1,512]{1,0:T(1,128)S(1)}, f32[1,512]{1,0:T(1,128)}, u32[]{:S(2)}) copy-start(f32[1,512]{1,0:T(1,128)} %param.22) | copy-start | bytes 6148
  74.1 36.7 %all-to-all-start.1 = ((bf16[64,20,128]{2,1,0:T(8,128)(2,1)}), bf16[64,20,128]{2,1,0:T(8,128)(2,1)S(1)}, u32[]{:S(2)}, u32[]{:S(2)}) async-start(bf16[64,20,128]{2,1,0:T(8,128)(2,1)} %pad_maximum_fusion), calls=%async_computation.1 | async-start | bytes 786432 | tf_op jit(solution)/shard_map/all_to_all | solution.py:490
  80.5 11.3 %collective-permute-start.17 = (bf16[2,256,128]{2,1,0:T(8,128)(2,1)S(1)}, bf16[2,256,128]{2,1,0:T(8,128)(2,1)S(1)}, u32[]{:S(2)}, u32[]{:S(2)}) collective-permute-start(bf16[2,256,128]{2,1,0:T(8,128)(2,1)S(1)} %get-tuple-element.64), channel_id=1, source_target_pairs={{0,12},{4,0},{8,4},{12,8},{16,28},{20,16},{24,20},{28,24},{32,44},... | collective-permute-start | bytes 393224 | tf_op jit(solution)/shard_map/ppermute | solution.py:433
  83.3 10.1 %collective-permute-start.18 = (bf16[2,256,128]{2,1,0:T(8,128)(2,1)S(1)}, bf16[2,256,128]{2,1,0:T(8,128)(2,1)S(1)}, u32[]{:S(2)}, u32[]{:S(2)}) collective-permute-start(bf16[2,256,128]{2,1,0:T(8,128)(2,1)S(1)} %get-tuple-element.65), channel_id=1, source_target_pairs={{0,8},{4,12},{8,0},{12,4},{16,24},{20,28},{24,16},{28,20},{32,40},... | collective-permute-start | bytes 393224 | tf_op jit(solution)/shard_map/ppermute | solution.py:433
  84.2 11.2 %collective-permute-start.19 = (bf16[2,256,128]{2,1,0:T(8,128)(2,1)S(1)}, bf16[2,256,128]{2,1,0:T(8,128)(2,1)S(1)}, u32[]{:S(2)}, u32[]{:S(2)}) collective-permute-start(bf16[2,256,128]{2,1,0:T(8,128)(2,1)S(1)} %get-tuple-element.66), channel_id=1, source_target_pairs={{0,4},{4,8},{8,12},{12,0},{16,20},{20,24},{24,28},{28,16},{32,36},... | collective-permute-start | bytes 393224 | tf_op jit(solution)/shard_map/ppermute | solution.py:433
  96.0 9.5 %collective-permute-start.20 = (bf16[256,128]{1,0:T(8,128)(2,1)S(1)}, bf16[256,128]{1,0:T(8,128)(2,1)S(1)}, u32[]{:S(2)}, u32[]{:S(2)}) collective-permute-start(bf16[256,128]{1,0:T(8,128)(2,1)S(1)} %get-tuple-element.67), channel_id=1, source_target_pairs={{0,0},{1,2},{2,1},{3,3},{4,4},{5,6},{6,5},{7,7},{8,8},{9,10},{10,9... | collective-permute-start | bytes 196616 | tf_op jit(solution)/shard_map/ppermute | solution.py:504
  99.0 7.4 %collective-permute-start.21 = (bf16[256,128]{1,0:T(8,128)(2,1)S(1)}, bf16[256,128]{1,0:T(8,128)(2,1)S(1)}, u32[]{:S(2)}, u32[]{:S(2)}) collective-permute-start(bf16[256,128]{1,0:T(8,128)(2,1)S(1)} %get-tuple-element.68), channel_id=1, source_target_pairs={{0,240},{1,242},{2,241},{3,243},{4,244},{5,246},{6,245},{7,247},{8... | collective-permute-start | bytes 196616 | tf_op jit(solution)/shard_map/ppermute | solution.py:504
  103.1 7.0 %collective-permute-start.22 = (bf16[256,128]{1,0:T(8,128)(2,1)S(1)}, bf16[256,128]{1,0:T(8,128)(2,1)S(1)}, u32[]{:S(2)}, u32[]{:S(2)}) collective-permute-start(bf16[256,128]{1,0:T(8,128)(2,1)S(1)} %get-tuple-element.69), channel_id=1, source_target_pairs={{0,224},{1,226},{2,225},{3,227},{4,228},{5,230},{6,229},{7,231},{8... | collective-permute-start | bytes 196616 | tf_op jit(solution)/shard_map/ppermute | solution.py:504

commit v3 on v2

--- a/solution.py
+++ b/solution.py
@@ -30,6 +30,14 @@
     return lax.dot_general(a, b, dims, preferred_element_type=jnp.float32)
 
 
+def core_of():
+    return lax.rem(lax.axis_index("head"), CORES)
+
+
+def column_place():
+    return lax.rem(lax.axis_index("ctx"), COLUMNS)
+
+
 def distance(slot, column):
     if slot < 3:
         return (0, COLUMNS, 2 * COLUMNS)[slot]
@@ -38,8 +46,8 @@
     return jnp.where(near, step + (0 if late else COLUMNS), step + (COLUMNS if late else 0))
 
 
-def pack_kernel(spot_ref, own_ref, one_ref, two_ref, *outs):
-    column = spot_ref[1]
+def pack_kernel(own_ref, one_ref, two_ref, *outs):
+    column = column_place()
     for n, out in enumerate(outs):
         step = n + 1
         out[0] = one_ref[...]
@@ -53,18 +61,29 @@
             out[1] = two_ref[...]
 
 
-def pack(spot, own, one, two):
+def pack(own, one, two):
     vmem = pl.BlockSpec(memory_space=pltpu.VMEM)
     return pl.pallas_call(
         pack_kernel,
-        in_specs=[pl.BlockSpec(memory_space=pltpu.SMEM)] + [vmem] * 3,
+        in_specs=[vmem] * 3,
         out_shape=[jax.ShapeDtypeStruct((2,) + own.shape, own.dtype)] * (COLUMNS - 1),
         compiler_params=pltpu.CompilerParams(vmem_limit_bytes=8 << 20),
         name="pack",
-    )(spot, own, one, two)
-
-
-def stage_kernel(fq_ref, go_ref, mask_ref, fq_out, go_out, mask_out):
+    )(own, one, two)
+
+
+def stage_kernel(
+    length_ref, shift_ref, fq_ref, go_ref, mask_ref, fq_out, go_out, mask_out, low_out, *, seq_total
+):
+    tokens = fq_ref.shape[0]
+    kv_head = lax.axis_index("head") // CORES
+    length = length_ref[kv_head]
+    first = lax.rem(lax.axis_index("ctx") * tokens - shift_ref[kv_head] + seq_total, seq_total)
+    within = lax.broadcasted_iota(jnp.int32, (1, tokens), 1)
+    in_group = within + lax.rem(first, length)
+    in_group = jnp.where(in_group >= length, in_group - length, in_group)
+    rolled = within + first
+    low_out[...] = within - jnp.where(rolled >= seq_total, rolled - seq_total, in_group)
     for h in range(fq_out.shape[0]):
         lanes = pl.ds(h * HEAD_SIZE, HEAD_SIZE)
         fq_out[h] = fq_ref[:, lanes]
@@ -72,15 +91,22 @@
     mask_out[...] = mask_ref[...]
 
 
-def stage(fq, go, masks):
+def stage(length, shift, fq, go, masks, seq_total):
     tokens, width = fq.shape
+    vmem = pl.BlockSpec(memory_space=pltpu.VMEM)
     by_head = jax.ShapeDtypeStruct((width // HEAD_SIZE, tokens, HEAD_SIZE), jnp.bfloat16)
     return pl.pallas_call(
-        stage_kernel,
-        out_shape=[by_head, by_head, jax.ShapeDtypeStruct(masks.shape, masks.dtype)],
+        functools.partial(stage_kernel, seq_total=seq_total),
+        in_specs=[pl.BlockSpec(memory_space=pltpu.SMEM)] * 2 + [vmem] * 3,
+        out_shape=[
+            by_head,
+            by_head,
+            jax.ShapeDtypeStruct(masks.shape, masks.dtype),
+            jax.ShapeDtypeStruct((1, tokens), jnp.int32),
+        ],
         compiler_params=pltpu.CompilerParams(vmem_limit_bytes=8 << 20),
         name="stage",
-    )(fq, go, masks)
+    )(length, shift, fq, go, masks)
 
 
 def column_of(row):
@@ -97,13 +123,13 @@
 
 def attention_kernel(*refs, tokens, heads, score_scale):
     tiles = REACH + 1
-    (spot_ref, fq_ref, go_ref, up_ref, mask_ref, low_ref, own_k_ref, own_v_ref) = refs[:8]
-    direct, swapped = refs[8:13], refs[13:18]
-    parts = refs[18:22]
-    out_ref, gq_ref, low_rank_ref, grad_up_ref, q_ref, w_ref, gs_ref = refs[22:29]
-    (k_s, v_s, kt_s, vt_s, place_s, s_s, gw_s, a_s, acc_s, lr_s) = refs[29:]
-    core = spot_ref[0]
-    column = spot_ref[1]
+    (fq_ref, go_ref, up_ref, low_ref, mask_ref, own_k_ref, own_v_ref) = refs[:7]
+    direct, swapped = refs[7:12], refs[12:17]
+    parts = refs[17:21]
+    out_ref, gq_ref, low_rank_ref, grad_up_ref, q_ref, w_ref, gs_ref = refs[21:28]
+    (k_s, v_s, kt_s, vt_s, place_s, s_s, gw_s, a_s, acc_s, lr_s) = refs[28:]
+    core = core_of()
+    column = column_place()
     exponent = score_scale * math.log2(math.e)
 
     def rows(d):
@@ -215,16 +241,19 @@
     low_rank_ref[...] = lr_s[...].astype(jnp.bfloat16)
 
 
-def attention(spot, fq, go, up, rest):
+def attention(fq, go, up, low, rest):
     heads, tokens, _ = fq.shape
     ranks, width = up.shape
     span = (REACH + 1) * tokens
     vmem = pl.BlockSpec(memory_space=pltpu.VMEM)
     return pl.pallas_call(
         functools.partial(
-            attention_kernel, tokens=tokens, heads=heads, score_scale=1.0 / math.sqrt(HEAD_SIZE)
+            attention_kernel,
+            tokens=tokens,
+            heads=heads,
+            score_scale=1.0 / math.sqrt(HEAD_SIZE),
         ),
-        in_specs=[pl.BlockSpec(memory_space=pltpu.SMEM)] + [vmem] * (3 + len(rest)),
+        in_specs=[vmem] * (4 + len(rest)),
         out_specs=[vmem] * 7,
         scratch_shapes=[
             pltpu.VMEM((span, HEAD_SIZE), jnp.bfloat16),
@@ -254,12 +283,12 @@
             transcendentals=heads * tokens * span,
         ),
         name="attention",
-    )(spot, fq, go, up, *rest)
-
-
-def kv_half_kernel(spot_ref, w_ref, gs_ref, go_ref, q_ref, half_ref, *, keep, score_scale):
+    )(fq, go, up, low, *rest)
+
+
+def kv_half_kernel(w_ref, gs_ref, go_ref, q_ref, half_ref, *, keep, score_scale):
     heads, span, tokens = w_ref.shape
-    values = (spot_ref[0] == 0) != keep
+    values = (core_of() == 0) != keep
 
     def product(left_ref, right_ref, scale):
         right = jnp.concatenate([right_ref[h] for h in range(heads)], 0)
@@ -277,12 +306,12 @@
         product(gs_ref, q_ref, score_scale)
 
 
-def kv_half(spot, weights, grad_scores, go, queries, keep):
+def kv_half(weights, grad_scores, go, queries, keep):
     span = weights.shape[1]
     vmem = pl.BlockSpec(memory_space=pltpu.VMEM)
     return pl.pallas_call(
         functools.partial(kv_half_kernel, keep=keep, score_scale=1.0 / math.sqrt(HEAD_SIZE)),
-        in_specs=[pl.BlockSpec(memory_space=pltpu.SMEM)] + [vmem] * 4,
+        in_specs=[vmem] * 4,
         out_specs=vmem,
         out_shape=jax.ShapeDtypeStruct((span, HEAD_SIZE), jnp.float32 if keep else jnp.bfloat16),
         compiler_params=pltpu.CompilerParams(vmem_limit_bytes=6 << 20),
@@ -290,7 +319,7 @@
             flops=2 * span * queries.size, bytes_accessed=2 << 20, transcendentals=0
         ),
         name="kv_keep" if keep else "kv_send",
-    )(spot, weights, grad_scores, go, queries)
+    )(weights, grad_scores, go, queries)
 
 
 def pair_sum_kernel(keep_ref, got_ref, own_ref, one_ref, two_ref, *packs):
@@ -319,8 +348,8 @@
     )(keep, got)
 
 
-def row_sum_kernel(spot_ref, own_ref, one_ref, two_ref, *rest):
-    column = spot_ref[1]
+def row_sum_kernel(own_ref, one_ref, two_ref, *rest):
+    column = column_place()
     packs, (own_out, one_out, two_out) = rest[: COLUMNS - 1], rest[COLUMNS - 1 :]
     own, one, two = own_ref[...], one_ref[...], two_ref[...]
     for n, pack_ref in enumerate(packs):
@@ -334,27 +363,19 @@
     two_out[...] = two.astype(jnp.bfloat16)
 
 
-def row_sum(spot, own, one, two, packs):
+def row_sum(own, one, two, packs):
     vmem = pl.BlockSpec(memory_space=pltpu.VMEM)
     return pl.pallas_call(
         row_sum_kernel,
-        in_specs=[pl.BlockSpec(memory_space=pltpu.SMEM)] + [vmem] * (2 + COLUMNS),
+        in_specs=[vmem] * (2 + COLUMNS),
         out_shape=[jax.ShapeDtypeStruct(own.shape, jnp.bfloat16)] * 3,
         compiler_params=pltpu.CompilerParams(vmem_limit_bytes=8 << 20),
         name="row_sum",
-    )(spot, own, one, two, *packs)
-
-
-def spread_kernel(down_ref, up_ref, out_ref, down_s, up_s, sems):
-    loads = [
-        pltpu.make_async_copy(down_ref, down_s, sems.at[0]),
-        pltpu.make_async_copy(up_ref, up_s, sems.at[1]),
-    ]
-    for load in loads:
-        load.start()
-    for load in loads:
-        load.wait()
-    row = jnp.concatenate([down_s[...], up_s[...]], 0).astype(jnp.bfloat16)
+    )(own, one, two, *packs)
+
+
+def spread_kernel(down_ref, up_ref, out_ref):
+    row = jnp.concatenate([down_ref[...], up_ref[...]], 0).astype(jnp.bfloat16)
     for n in range(out_ref.shape[0]):
         out_ref[n] = row
 
@@ -362,14 +383,8 @@
 def spread(down, up, copies):
     return pl.pallas_call(
         spread_kernel,
-        in_specs=[pl.BlockSpec(memory_space=pl.ANY)] * 2,
-        scratch_shapes=[
-            pltpu.VMEM(down.shape, down.dtype),
-            pltpu.VMEM(up.shape, up.dtype),
-            pltpu.SemaphoreType.DMA((2,)),
-        ],
         out_shape=jax.ShapeDtypeStruct((copies, down.shape[0] + up.shape[0], 128), jnp.bfloat16),
-        compiler_params=pltpu.CompilerParams(vmem_limit_bytes=63 << 20),
+        compiler_params=pltpu.CompilerParams(vmem_limit_bytes=4 << 20),
         name="spread",
     )(down, up)
 
@@ -416,8 +431,6 @@
     key_width = KVH * HEAD_SIZE
     ranks = rank_keep_mask.shape[1]
 
-    column = ctx_place % COLUMNS
-    spot = jnp.concatenate([core.reshape(1), column.reshape(1)]).astype(jnp.int32)
     own_k = lax.dynamic_slice_in_dim(key_value_rows, kv_head * HEAD_SIZE, HEAD_SIZE, 1)
     own_v = lax.dynamic_slice_in_dim(key_value_rows, key_width + kv_head * HEAD_SIZE, HEAD_SIZE, 1)
     mine = lax.dynamic_slice_in_dim(
@@ -437,9 +450,16 @@
     down_rows, up_rows = model // 128, width // 128
     row = spread(adapter_down.reshape(down_rows, 128), adapter_up.reshape(up_rows, 128), ctx)
     gathered = lax.all_to_all(row, "ctx", split_axis=0, concat_axis=0)
-    packs = pack(spot, mine, one, two)
+    packs = pack(mine, one, two)
     direct = [one, two] + [across(p, n + 1) for n, p in enumerate(packs)]
-    queries_in, grads_in, masks_in = stage(frozen_queries, output_gradient, rank_keep_mask)
+    queries_in, grads_in, masks_in, low = stage(
+        group_length,
+        group_shift,
+        frozen_queries,
+        output_gradient,
+        rank_keep_mask,
+        tokens * ctx,
+    )
     swapped = [lax.ppermute(piece, "head", swap) for piece in direct]
 
     down = gathered[:, :down_rows].reshape(ranks, model)
@@ -449,20 +469,14 @@
     others = [[(h, h ^ k) for h in range(head_count)] for k in range(1, head_count)]
     parts = [part] + [lax.ppermute(part, "head", pairs) for pairs in others]
 
-    length = jnp.where(kv_head == 0, group_length[0:1], group_length[1:2])
-    shift = jnp.where(kv_head == 0, group_shift[0:1], group_shift[1:2])
-    within = jnp.arange(tokens, dtype=jnp.int32)
-    rolled = (ctx_place * tokens + within - shift) % (tokens * ctx)
-    low = (within - rolled % length).reshape(1, tokens)
     keep_masks = rank_keep_mask.astype(jnp.float32)[:, :, None]
     out, query_gradient, low_rank_part, grad_up_part, queries, weights, grad_scores = attention(
-        spot,
         queries_in,
         grads_in,
         up,
+        low,
         [
             masks_in,
-            low,
             own_k,
             own_v,
             *direct,
@@ -472,9 +486,9 @@
     )
 
     low_parts = [low_rank_part] + [lax.ppermute(low_rank_part, "head", pairs) for pairs in others]
-    send = kv_half(spot, weights, grad_scores, grads_in, queries, keep=False)
+    send = kv_half(weights, grad_scores, grads_in, queries, keep=False)
     got = lax.ppermute(send, "head", swap)
-    keep = kv_half(spot, weights, grad_scores, grads_in, queries, keep=True)
+    keep = kv_half(weights, grad_scores, grads_in, queries, keep=True)
     own_sum, one_sum, two_sum, *packs = pair_sum(keep, got, tokens)
     low_parts, grad_up_part, packs = lax.optimization_barrier((low_parts, grad_up_part, packs))
     low_total = sum(p.astype(jnp.float32) for p in low_parts)
@@ -490,7 +504,7 @@
     received = lax.all_to_all(packed, "ctx", split_axis=0, concat_axis=0)
 
     packs = [across(p, -(n + 1)) for n, p in enumerate(packs)]
-    own_sum, one_sum, two_sum = row_sum(spot, own_sum, one_sum, two_sum, packs)
+    own_sum, one_sum, two_sum = row_sum(own_sum, one_sum, two_sum, packs)
 
     def home(piece, back):
         pairs = [

time: 114 us -> 113 us (level)
  the two profiles are of different devices: /device:TPU:6 before, /device:TPU:1 now
where the time goes in v3:
time: 113 us; the launch traced here: 112 us
  starting transfers between devices  56.4 us (50%)
  waiting for transfers between devices  29.6 us (26%)
  Pallas kernels  15.8 us (14%)
  local copies, waits for them, and re-layouts  7.06 us (6%)
  other arithmetic  1.47 us (1%)
    all_to_all x1, starting transfers between devices, on_device(): gathered = lax.all_to_all(row, 'ctx', split_axis=0, concat_axis=0)  13.6 us
    ppermute x2, waiting for transfers between devices, along(): lax.ppermute(piece, 'ctx', [(i, (i + step) % ctx) for i in range(ctx)])  11.9 us
    ppermute x6, waiting for transfers between devices, across(): return lax.ppermute(piece, 'ctx', pairs)  11.7 us
    ppermute x3, starting transfers between devices, home(): return lax.ppermute(piece, ('ctx', 'head'), pairs).astype(jnp.float32)  10.6 us
    pallas_call x1, Pallas kernels, attention(): pl.pallas_call(functools.partial(attention_kernel, tokens=tokens, heads=h...  9.78 us
    ppermute x6, starting transfers between devices, across(): return lax.ppermute(piece, 'ctx', pairs)  8.01 us
    all_to_all x1, starting transfers between devices, on_device(): received = lax.all_to_all(packed, 'ctx', split_axis=0, concat_axis=0)  7.02 us
    ppermute x5, starting transfers between devices, on_device(): swapped = [lax.ppermute(piece, 'head', swap) for piece in direct]  6.24 us
  transfers between devices with their start and end apart: 25, of which 7 were waited for; matrix products, arithmetic and copies ran while one was open for 2% of the time, Pallas kernels for 2%

profile of v3, /device:TPU:1, one launch (start us, length us, event | category | flops | bytes accessed | tf_op | source)
XLA Modules:
  0.0 112.1 jit_solution(17085027201775121904)
XLA Ops:
  0.6 0.0 copy-start
  0.7 0.0 copy-start.3
  0.7 0.8 copy-done.3
  1.4 0.7 copy-done.5
  2.1 0.8 spread.1
  2.9 13.6 %all-to-all-start = ((bf16[64,20,128]{2,1,0:T(8,128)(2,1)}), bf16[64,20,128]{2,1,0:T(8,128)(2,1)S(1)}, u32[]{:S(2)}, u32[]{:S(2)}) async-start(bf16[64,20,128]{2,1,0:T(8,128)(2,1)} %spread.1), calls=%async_computation | async-start | bytes 786432 | tf_op jit(solution)/shard_map/all_to_all | solution.py:452
  16.5 0.9 constant_dynamic-slice_fusion.1
  17.5 1.1 collective-permute-start
  18.5 2.1 %collective-permute-start.1 = (bf16[256,128]{1,0:T(8,128)(2,1)S(1)}, bf16[256,128]{1,0:T(8,128)(2,1)S(1)}, u32[]{:S(2)}, u32[]{:S(2)}) collective-permute-start(bf16[256,128]{1,0:T(8,128)(2,1)S(1)} %get-tuple-element.83.own_ref), channel_id=1, source_target_pairs={{0,32},{4,36},{8,40},{12,44},{16,48},{20,52},{24,56},{28,60},{32,6... | collective-permute-start | bytes 196616 | tf_op jit(solution)/shard_map/ppermute | solution.py:442
  20.6 7.8 %collective-permute-done.one_ref.refs_7_ = bf16[256,128]{1,0:T(8,128)(2,1)S(1)} collective-permute-done((bf16[256,128]{1,0:T(8,128)(2,1)S(1)}, bf16[256,128]{1,0:T(8,128)(2,1)S(1)}, u32[]{:S(2)}, u32[]{:S(2)}) %collective-permute-start) | collective-permute-done | bytes 65568 | tf_op jit(solution)/shard_map/ppermute | solution.py:442
  28.4 4.2 %collective-permute-done.1.two_ref.refs_8_ = bf16[256,128]{1,0:T(8,128)(2,1)S(1)} collective-permute-done((bf16[256,128]{1,0:T(8,128)(2,1)S(1)}, bf16[256,128]{1,0:T(8,128)(2,1)S(1)}, u32[]{:S(2)}, u32[]{:S(2)}) %collective-permute-start.1) | collective-permute-done | bytes 65568 | tf_op jit(solution)/shard_map/ppermute | solution.py:442
  32.6 1.0 collective-permute-start.2
  33.6 2.5 %collective-permute-start.3 = (bf16[2,256,128]{2,1,0:T(8,128)(2,1)S(1)}, bf16[2,256,128]{2,1,0:T(8,128)(2,1)S(1)}, u32[]{:S(2)}, u32[]{:S(2)}) collective-permute-start(bf16[2,256,128]{2,1,0:T(8,128)(2,1)S(1)} %get-tuple-element.51), channel_id=1, source_target_pairs={{0,8},{4,12},{8,0},{12,4},{16,24},{20,28},{24,16},{28,20},{32,40},... | collective-permute-start | bytes 393224 | tf_op jit(solution)/shard_map/ppermute | solution.py:446
  36.1 1.1 collective-permute-start.4
  37.2 2.9 %collective-permute-start.5 = (bf16[256,128]{1,0:T(8,128)(2,1)S(1)}, bf16[256,128]{1,0:T(8,128)(2,1)S(1)}, u32[]{:S(2)}, u32[]{:S(2)}) collective-permute-start(bf16[256,128]{1,0:T(8,128)(2,1)S(1)} %collective-permute-done.one_ref.refs_7_), channel_id=1, source_target_pairs={{0,1},{1,0},{2,3},{3,2},{4,5},{5,4},{6,7},{7,6},{8,9},{9,8},{10,11... | collective-permute-start | bytes 196616 | tf_op jit(solution)/shard_map/ppermute | solution.py:463
  40.1 0.0 collective-permute-start.6
  40.1 0.0 collective-permute-done.2.refs_9_
  40.1 1.9 %collective-permute-start.7 = (bf16[2,256,128]{2,1,0:T(8,128)(2,1)S(1)}, bf16[2,256,128]{2,1,0:T(8,128)(2,1)S(1)}, u32[]{:S(2)}, u32[]{:S(2)}) collective-permute-start(bf16[2,256,128]{2,1,0:T(8,128)(2,1)S(1)} %collective-permute-done.2.refs_9_), channel_id=1, source_target_pairs={{0,1},{1,0},{2,3},{3,2},{4,5},{5,4},{6,7},{7,6},{8,9},{9,8},{10,11... | collective-permute-start | bytes 393224 | tf_op jit(solution)/shard_map/ppermute | solution.py:463
  42.0 1.4 %collective-permute-start.8 = (bf16[2,256,128]{2,1,0:T(8,128)(2,1)S(1)}, bf16[2,256,128]{2,1,0:T(8,128)(2,1)S(1)}, u32[]{:S(2)}, u32[]{:S(2)}) collective-permute-start(bf16[2,256,128]{2,1,0:T(8,128)(2,1)S(1)} %collective-permute-done.3.refs_10_), channel_id=1, source_target_pairs={{0,1},{1,0},{2,3},{3,2},{4,5},{5,4},{6,7},{7,6},{8,9},{9,8},{10,11... | collective-permute-start | bytes 393224 | tf_op jit(solution)/shard_map/ppermute | solution.py:463
  43.4 0.0 collective-permute-done.4.refs_11_
  43.4 0.1 collective-permute-start.9
  43.5 0.4 convolution_convert_fusion.1.refs_17_
  43.9 0.0 collective-permute-done.5.refs_12_
  43.9 0.5 collective-permute-start.10
  44.4 2.5 %collective-permute-start.11 = (bf16[64,256]{1,0:T(8,128)(2,1)S(1)}, bf16[64,256]{1,0:T(8,128)(2,1)S(1)}, u32[]{:S(2)}, u32[]{:S(2)}) collective-permute-start(bf16[64,256]{1,0:T(8,128)(2,1)S(1)} %convolution_convert_fusion.1.refs_17_), channel_id=1, source_target_pairs={{0,2},{1,3},{2,0},{3,1},{4,6},{5,7},{6,4},{7,5},{8,10},{9,11},{10,... | collective-permute-start | bytes 98312 | tf_op jit(solution)/shard_map/ppermute | solution.py:470
  46.9 0.8 collective-permute-start.12
  47.7 0.9 copy-done.1
  48.6 0.9 copy-done.2
  49.6 0.7 copy-done.9
  50.3 0.7 copy-done.13
  50.9 0.7 copy-done.14
  51.6 0.6 stage.1
  52.3 9.8 %attention.1 = (bf16[256,512]{1,0:T(8,128)(2,1)}, bf16[256,512]{1,0:T(8,128)(2,1)}, bf16[64,256]{1,0:T(8,128)(2,1)S(1)}, bf16[64,512]{1,0:T(8,128)(2,1)S(1)}, bf...) custom-call(bf16[4,256,128]{2,1,0:T(8,128)(2,1)S(1)} %get-tuple-element.46.refs_, ...), custom_call_target="tpu_custom_call" | custom-call | flops 2415919104 | bytes 8388608 | tf_op jit(solution)/shard_map/attention/pallas_call | solution.py:249
  62.1 1.4 %kv_send.1 = bf16[2304,128]{1,0:T(8,128)(2,1)S(1)} custom-call(bf16[4,2304,256]{2,1,0:T(8,128)(2,1)S(1)} %get-tuple-element.55.w_ref, bf16[4,2304,256]{2,1,0:T(8,128)(2,1)S(1)} %get-tuple-element.56.gs_ref, bf16[4,256,128]{2,1,0:T(8,128)(2,1)S(1)} %get-tuple-element.47.refs_1_.go_ref, bf16[4,256,128]{2,1,0:T(8,128)(2,1)S(1)} %get-tuple-element.57.q_ref), custom_call_target="tpu_custom_call" | custom-call | flops 603979776 | bytes 2097152 | tf_op jit(solution)/shard_map/kv_send/pallas_call | solution.py:312
  63.5 0.3 collective-permute-start.13
  63.8 0.4 collective-permute-start.14
  64.2 2.4 %collective-permute-start.15 = (bf16[64,256]{1,0:T(8,128)(2,1)S(1)}, bf16[64,256]{1,0:T(8,128)(2,1)S(1)}, u32[]{:S(2)}, u32[]{:S(2)}) collective-permute-start(bf16[64,256]{1,0:T(8,128)(2,1)S(1)} %get-tuple-element.72), channel_id=1, source_target_pairs={{0,2},{1,3},{2,0},{3,1},{4,6},{5,7},{6,4},{7,5},{8,10},{9,11},{10,... | collective-permute-start | bytes 98312 | tf_op jit(solution)/shard_map/ppermute | solution.py:488
  66.6 0.9 collective-permute-start.16
  67.5 1.7 %kv_keep.1.keep_ref = f32[2304,128]{1,0:T(8,128)S(1)} custom-call(bf16[4,2304,256]{2,1,0:T(8,128)(2,1)S(1)} %get-tuple-element.55.w_ref, bf16[4,2304,256]{2,1,0:T(8,128)(2,1)S(1)} %get-tuple-element.56.gs_ref, bf16[4,256,128]{2,1,0:T(8,128)(2,1)S(1)} %get-tuple-element.47.refs_1_.go_ref, bf16[4,256,128]{2,1,0:T(8,128)(2,1)S(1)} %get-tuple-element.57.q_ref), custom_call_target="tpu_custom_call" | custom-call | flops 603979776 | bytes 2097152 | tf_op jit(solution)/shard_map/kv_keep/pallas_call | solution.py:312
  69.2 0.0 copy-start.4
  69.2 0.0 copy-start.6
  69.2 0.0 copy-start.7
  69.2 0.0 copy-start.8
  69.2 0.0 copy-start.11
  69.3 0.0 copy-start.12
  69.3 0.1 pair_sum.1
  69.4 2.3 %collective-permute-done.16 = bf16[64,256]{1,0:T(8,128)(2,1)S(1)} collective-permute-done((bf16[64,256]{1,0:T(8,128)(2,1)S(1)}, bf16[64,256]{1,0:T(8,128)(2,1)S(1)}, u32[]{:S(2)}, u32[]{:S(2)}) %collective-permute-start.16) | collective-permute-done | bytes 32800 | tf_op jit(solution)/shard_map/ppermute | solution.py:488
  71.7 0.3 fusion
  72.1 0.8 pad_maximum_fusion
  72.9 7.0 %all-to-all-start.1 = ((bf16[64,20,128]{2,1,0:T(8,128)(2,1)}), bf16[64,20,128]{2,1,0:T(8,128)(2,1)S(1)}, u32[]{:S(2)}, u32[]{:S(2)}) async-start(bf16[64,20,128]{2,1,0:T(8,128)(2,1)} %pad_maximum_fusion), calls=%async_computation.1 | async-start | bytes 786432 | tf_op jit(solution)/shard_map/all_to_all | solution.py:504
  79.9 2.3 %collective-permute-start.17 = (bf16[2,256,128]{2,1,0:T(8,128)(2,1)S(1)}, bf16[2,256,128]{2,1,0:T(8,128)(2,1)S(1)}, u32[]{:S(2)}, u32[]{:S(2)}) collective-permute-start(bf16[2,256,128]{2,1,0:T(8,128)(2,1)S(1)} %get-tuple-element.66), channel_id=1, source_target_pairs={{0,12},{4,0},{8,4},{12,8},{16,28},{20,16},{24,20},{28,24},{32,44},... | collective-permute-start | bytes 393224 | tf_op jit(solution)/shard_map/ppermute | solution.py:446
  82.2 0.6 collective-permute-start.18
  82.8 0.6 collective-permute-start.19
  83.4 2.4 %collective-permute-done.17.rest_0_ = bf16[2,256,128]{2,1,0:T(8,128)(2,1)S(1)} collective-permute-done((bf16[2,256,128]{2,1,0:T(8,128)(2,1)S(1)}, bf16[2,256,128]{2,1,0:T(8,128)(2,1)S(1)}, u32[]{:S(2)}, u32[]{:S(2)}) %collective-permute-start.17) | collective-permute-done | bytes 131104 | tf_op jit(solution)/shard_map/ppermute | solution.py:446
  85.7 3.6 %collective-permute-done.18.rest_1_ = bf16[2,256,128]{2,1,0:T(8,128)(2,1)S(1)} collective-permute-done((bf16[2,256,128]{2,1,0:T(8,128)(2,1)S(1)}, bf16[2,256,128]{2,1,0:T(8,128)(2,1)S(1)}, u32[]{:S(2)}, u32[]{:S(2)}) %collective-permute-start.18) | collective-permute-done | bytes 131104 | tf_op jit(solution)/shard_map/ppermute | solution.py:446
  89.3 5.7 %collective-permute-done.19.rest_2_ = bf16[2,256,128]{2,1,0:T(8,128)(2,1)S(1)} collective-permute-done((bf16[2,256,128]{2,1,0:T(8,128)(2,1)S(1)}, bf16[2,256,128]{2,1,0:T(8,128)(2,1)S(1)}, u32[]{:S(2)}, u32[]{:S(2)}) %collective-permute-start.19) | collective-permute-done | bytes 131104 | tf_op jit(solution)/shard_map/ppermute | solution.py:446
  95.1 0.1 row_sum.1
  95.2 4.0 %collective-permute-start.20 = (bf16[256,128]{1,0:T(8,128)(2,1)S(1)}, bf16[256,128]{1,0:T(8,128)(2,1)S(1)}, u32[]{:S(2)}, u32[]{:S(2)}) collective-permute-start(bf16[256,128]{1,0:T(8,128)(2,1)S(1)} %get-tuple-element.69), channel_id=1, source_target_pairs={{0,0},{1,2},{2,1},{3,3},{4,4},{5,6},{6,5},{7,7},{8,8},{9,10},{10,9... | collective-permute-start | bytes 196616 | tf_op jit(solution)/shard_map/ppermute | solution.py:518
  99.3 3.8 %collective-permute-start.21 = (bf16[256,128]{1,0:T(8,128)(2,1)S(1)}, bf16[256,128]{1,0:T(8,128)(2,1)S(1)}, u32[]{:S(2)}, u32[]{:S(2)}) collective-permute-start(bf16[256,128]{1,0:T(8,128)(2,1)S(1)} %get-tuple-element.70), channel_id=1, source_target_pairs={{0,240},{1,242},{2,241},{3,243},{4,244},{5,246},{6,245},{7,247},{8... | collective-permute-start | bytes 196616 | tf_op jit(solution)/shard_map/ppermute | solution.py:518
  103.1 2.7 %collective-permute-start.22 = (bf16[256,128]{1,0:T(8,128)(2,1)S(1)}, bf16[256,128]{1,0:T(8,128)(2,1)S(1)}, u32[]{:S(2)}, u32[]{:S(2)}) collective-permute-start(bf16[256,128]{1,0:T(8,128)(2,1)S(1)} %get-tuple-element.71), channel_id=1, source_target_pairs={{0,224},{1,226},{2,225},{3,227},{4,228},{5,230},{6,229},{7,231},{8... | collective-permute-start | bytes 196616 | tf_op jit(solution)/shard_map/ppermute | solution.py:518
  105.8 0.6 constant_dynamic-slice_fusion.keep_ref
  106.4 3.6 %collective-permute-done.22 = bf16[256,128]{1,0:T(8,128)(2,1)S(1)} collective-permute-done((bf16[256,128]{1,0:T(8,128)(2,1)S(1)}, bf16[256,128]{1,0:T(8,128)(2,1)S(1)}, u32[]{:S(2)}, u32[]{:S(2)}) %collective-permute-start.22) | collective-permute-done | bytes 65568 | tf_op jit(solution)/shard_map/ppermute | solution.py:518
  110.1 0.7 convert_add_fusion
  110.8 1.3 %adam.1 = (f32[16,128]{1,0:T(8,128)}, f32[16,128]{1,0:T(8,128)}, f32[16,128]{1,0:T(8,128)}, f32[4,128]{1,0:T(4,128)}, f32[4,128]{1,0:T(4,128)}, /*index=5*/f32[4,128]{1,0:T(4,128)}) custom-call(bf16[64,20,128]{2,1,0:T(8,128)(2,1)S(1)} %all-to-all-done.1.got_ref, f32[16,128]{1,0:T(8,128)S(1)} %bitcast.29, f32[16,128]{1,0:T(8,128)S(1)} %bitcast.32, ...), custom_call_target="tpu_custom_call" | custom-call | tf_op jit(solution)/shard_map/adam/pallas_call | solution.py:534
  (38 shorter events, 0.2 us)
Async XLA Ops:
  0.6 42.8 %copy-start = (bf16[256,2048]{1,0:T(8,128)(2,1)S(1)}, bf16[256,2048]{1,0:T(8,128)(2,1)}, u32[]{:S(2)}) copy-start(bf16[256,2048]{1,0:T(8,128)(2,1)} %param.16) | copy-start | bytes 3145732
  0.7 0.8 copy-start.3
  1.4 0.7 copy-start.5
  2.9 40.5 %all-to-all-start = ((bf16[64,20,128]{2,1,0:T(8,128)(2,1)}), bf16[64,20,128]{2,1,0:T(8,128)(2,1)S(1)}, u32[]{:S(2)}, u32[]{:S(2)}) async-start(bf16[64,20,128]{2,1,0:T(8,128)(2,1)} %spread.1), calls=%async_computation | async-start | bytes 786432 | tf_op jit(solution)/shard_map/all_to_all | solution.py:452
  17.5 10.9 %collective-permute-start = (bf16[256,128]{1,0:T(8,128)(2,1)S(1)}, bf16[256,128]{1,0:T(8,128)(2,1)S(1)}, u32[]{:S(2)}, u32[]{:S(2)}) collective-permute-start(bf16[256,128]{1,0:T(8,128)(2,1)S(1)} %get-tuple-element.83.own_ref), channel_id=1, source_target_pairs={{0,16},{4,20},{8,24},{12,28},{16,32},{20,36},{24,40},{28,44},{32,4... | collective-permute-start | bytes 196616 | tf_op jit(solution)/shard_map/ppermute | solution.py:442
  18.5 14.0 %collective-permute-start.1 = (bf16[256,128]{1,0:T(8,128)(2,1)S(1)}, bf16[256,128]{1,0:T(8,128)(2,1)S(1)}, u32[]{:S(2)}, u32[]{:S(2)}) collective-permute-start(bf16[256,128]{1,0:T(8,128)(2,1)S(1)} %get-tuple-element.83.own_ref), channel_id=1, source_target_pairs={{0,32},{4,36},{8,40},{12,44},{16,48},{20,52},{24,56},{28,60},{32,6... | collective-permute-start | bytes 196616 | tf_op jit(solution)/shard_map/ppermute | solution.py:442
  32.6 7.5 %collective-permute-start.2 = (bf16[2,256,128]{2,1,0:T(8,128)(2,1)S(1)}, bf16[2,256,128]{2,1,0:T(8,128)(2,1)S(1)}, u32[]{:S(2)}, u32[]{:S(2)}) collective-permute-start(bf16[2,256,128]{2,1,0:T(8,128)(2,1)S(1)} %get-tuple-element.50), channel_id=1, source_target_pairs={{0,4},{4,8},{8,12},{12,0},{16,20},{20,24},{24,28},{28,16},{32,36},... | collective-permute-start | bytes 393224 | tf_op jit(solution)/shard_map/ppermute | solution.py:446
  33.6 8.3 %collective-permute-start.3 = (bf16[2,256,128]{2,1,0:T(8,128)(2,1)S(1)}, bf16[2,256,128]{2,1,0:T(8,128)(2,1)S(1)}, u32[]{:S(2)}, u32[]{:S(2)}) collective-permute-start(bf16[2,256,128]{2,1,0:T(8,128)(2,1)S(1)} %get-tuple-element.51), channel_id=1, source_target_pairs={{0,8},{4,12},{8,0},{12,4},{16,24},{20,28},{24,16},{28,20},{32,40},... | collective-permute-start | bytes 393224 | tf_op jit(solution)/shard_map/ppermute | solution.py:446
  36.1 7.3 %collective-permute-start.4 = (bf16[2,256,128]{2,1,0:T(8,128)(2,1)S(1)}, bf16[2,256,128]{2,1,0:T(8,128)(2,1)S(1)}, u32[]{:S(2)}, u32[]{:S(2)}) collective-permute-start(bf16[2,256,128]{2,1,0:T(8,128)(2,1)S(1)} %get-tuple-element.52), channel_id=1, source_target_pairs={{0,12},{4,0},{8,4},{12,8},{16,28},{20,16},{24,20},{28,24},{32,44},... | collective-permute-start | bytes 393224 | tf_op jit(solution)/shard_map/ppermute | solution.py:446
  37.2 6.7 %collective-permute-start.5 = (bf16[256,128]{1,0:T(8,128)(2,1)S(1)}, bf16[256,128]{1,0:T(8,128)(2,1)S(1)}, u32[]{:S(2)}, u32[]{:S(2)}) collective-permute-start(bf16[256,128]{1,0:T(8,128)(2,1)S(1)} %collective-permute-done.one_ref.refs_7_), channel_id=1, source_target_pairs={{0,1},{1,0},{2,3},{3,2},{4,5},{5,4},{6,7},{7,6},{8,9},{9,8},{10,11... | collective-permute-start | bytes 196616 | tf_op jit(solution)/shard_map/ppermute | solution.py:463
  40.1 4.4 %collective-permute-start.6 = (bf16[256,128]{1,0:T(8,128)(2,1)S(1)}, bf16[256,128]{1,0:T(8,128)(2,1)S(1)}, u32[]{:S(2)}, u32[]{:S(2)}) collective-permute-start(bf16[256,128]{1,0:T(8,128)(2,1)S(1)} %collective-permute-done.1.two_ref.refs_8_), channel_id=1, source_target_pairs={{0,1},{1,0},{2,3},{3,2},{4,5},{5,4},{6,7},{7,6},{8,9},{9,8},{10,11... | collective-permute-start | bytes 196616 | tf_op jit(solution)/shard_map/ppermute | solution.py:463
  40.1 6.8 %collective-permute-start.7 = (bf16[2,256,128]{2,1,0:T(8,128)(2,1)S(1)}, bf16[2,256,128]{2,1,0:T(8,128)(2,1)S(1)}, u32[]{:S(2)}, u32[]{:S(2)}) collective-permute-start(bf16[2,256,128]{2,1,0:T(8,128)(2,1)S(1)} %collective-permute-done.2.refs_9_), channel_id=1, source_target_pairs={{0,1},{1,0},{2,3},{3,2},{4,5},{5,4},{6,7},{7,6},{8,9},{9,8},{10,11... | collective-permute-start | bytes 393224 | tf_op jit(solution)/shard_map/ppermute | solution.py:463
  42.0 10.3 %collective-permute-start.8 = (bf16[2,256,128]{2,1,0:T(8,128)(2,1)S(1)}, bf16[2,256,128]{2,1,0:T(8,128)(2,1)S(1)}, u32[]{:S(2)}, u32[]{:S(2)}) collective-permute-start(bf16[2,256,128]{2,1,0:T(8,128)(2,1)S(1)} %collective-permute-done.3.refs_10_), channel_id=1, source_target_pairs={{0,1},{1,0},{2,3},{3,2},{4,5},{5,4},{6,7},{7,6},{8,9},{9,8},{10,11... | collective-permute-start | bytes 393224 | tf_op jit(solution)/shard_map/ppermute | solution.py:463
  43.4 8.9 %collective-permute-start.9 = (bf16[2,256,128]{2,1,0:T(8,128)(2,1)S(1)}, bf16[2,256,128]{2,1,0:T(8,128)(2,1)S(1)}, u32[]{:S(2)}, u32[]{:S(2)}) collective-permute-start(bf16[2,256,128]{2,1,0:T(8,128)(2,1)S(1)} %collective-permute-done.4.refs_11_), channel_id=1, source_target_pairs={{0,1},{1,0},{2,3},{3,2},{4,5},{5,4},{6,7},{7,6},{8,9},{9,8},{10,11... | collective-permute-start | bytes 393224 | tf_op jit(solution)/shard_map/ppermute | solution.py:463
  43.9 8.4 %collective-permute-start.10 = (bf16[64,256]{1,0:T(8,128)(2,1)S(1)}, bf16[64,256]{1,0:T(8,128)(2,1)S(1)}, u32[]{:S(2)}, u32[]{:S(2)}) collective-permute-start(bf16[64,256]{1,0:T(8,128)(2,1)S(1)} %convolution_convert_fusion.1.refs_17_), channel_id=1, source_target_pairs={{0,1},{1,0},{2,3},{3,2},{4,5},{5,4},{6,7},{7,6},{8,9},{9,8},{10,11... | collective-permute-start | bytes 98312 | tf_op jit(solution)/shard_map/ppermute | solution.py:470
  44.4 7.9 %collective-permute-start.11 = (bf16[64,256]{1,0:T(8,128)(2,1)S(1)}, bf16[64,256]{1,0:T(8,128)(2,1)S(1)}, u32[]{:S(2)}, u32[]{:S(2)}) collective-permute-start(bf16[64,256]{1,0:T(8,128)(2,1)S(1)} %convolution_convert_fusion.1.refs_17_), channel_id=1, source_target_pairs={{0,2},{1,3},{2,0},{3,1},{4,6},{5,7},{6,4},{7,5},{8,10},{9,11},{10,... | collective-permute-start | bytes 98312 | tf_op jit(solution)/shard_map/ppermute | solution.py:470
  46.9 5.4 %collective-permute-start.12 = (bf16[64,256]{1,0:T(8,128)(2,1)S(1)}, bf16[64,256]{1,0:T(8,128)(2,1)S(1)}, u32[]{:S(2)}, u32[]{:S(2)}) collective-permute-start(bf16[64,256]{1,0:T(8,128)(2,1)S(1)} %convolution_convert_fusion.1.refs_17_), channel_id=1, source_target_pairs={{0,3},{1,2},{2,1},{3,0},{4,7},{5,6},{6,5},{7,4},{8,11},{9,10},{10,... | collective-permute-start | bytes 98312 | tf_op jit(solution)/shard_map/ppermute | solution.py:470
  47.7 0.9 copy-start.1
  48.6 0.9 copy-start.2
  49.6 0.7 copy-start.9
  50.3 0.7 copy-start.13
  50.9 0.7 copy-start.14
  62.1 1.7 %copy-start.10 = (s32[2,64]{1,0:T(2,128)S(1)}, s32[2,64]{1,0:T(2,128)}, u32[]{:S(2)}) copy-start(s32[2,64]{1,0:T(2,128)} %mask_ref.1) | copy-start | bytes 1540
  63.5 5.8 %collective-permute-start.13 = (bf16[2304,128]{1,0:T(8,128)(2,1)S(1)}, bf16[2304,128]{1,0:T(8,128)(2,1)S(1)}, u32[]{:S(2)}, u32[]{:S(2)}) collective-permute-start(bf16[2304,128]{1,0:T(8,128)(2,1)S(1)} %kv_send.1), channel_id=1, source_target_pairs={{0,1},{1,0},{2,3},{3,2},{4,5},{5,4},{6,7},{7,6},{8,9},{9,8},{10,11... | collective-permute-start | bytes 1769480 | tf_op jit(solution)/shard_map/ppermute | solution.py:490
  63.8 5.6 %collective-permute-start.14 = (bf16[64,256]{1,0:T(8,128)(2,1)S(1)}, bf16[64,256]{1,0:T(8,128)(2,1)S(1)}, u32[]{:S(2)}, u32[]{:S(2)}) collective-permute-start(bf16[64,256]{1,0:T(8,128)(2,1)S(1)} %get-tuple-element.72), channel_id=1, source_target_pairs={{0,1},{1,0},{2,3},{3,2},{4,5},{5,4},{6,7},{7,6},{8,9},{9,8},{10,11... | collective-permute-start | bytes 98312 | tf_op jit(solution)/shard_map/ppermute | solution.py:488
  64.2 5.2 %collective-permute-start.15 = (bf16[64,256]{1,0:T(8,128)(2,1)S(1)}, bf16[64,256]{1,0:T(8,128)(2,1)S(1)}, u32[]{:S(2)}, u32[]{:S(2)}) collective-permute-start(bf16[64,256]{1,0:T(8,128)(2,1)S(1)} %get-tuple-element.72), channel_id=1, source_target_pairs={{0,2},{1,3},{2,0},{3,1},{4,6},{5,7},{6,4},{7,5},{8,10},{9,11},{10,... | collective-permute-start | bytes 98312 | tf_op jit(solution)/shard_map/ppermute | solution.py:488
  66.6 5.1 %collective-permute-start.16 = (bf16[64,256]{1,0:T(8,128)(2,1)S(1)}, bf16[64,256]{1,0:T(8,128)(2,1)S(1)}, u32[]{:S(2)}, u32[]{:S(2)}) collective-permute-start(bf16[64,256]{1,0:T(8,128)(2,1)S(1)} %get-tuple-element.72), channel_id=1, source_target_pairs={{0,3},{1,2},{2,1},{3,0},{4,7},{5,6},{6,5},{7,4},{8,11},{9,10},{10,... | collective-permute-start | bytes 98312 | tf_op jit(solution)/shard_map/ppermute | solution.py:488
  69.2 41.6 %copy-start.4 = (f32[1,2048]{1,0:T(1,128)S(1)}, f32[1,2048]{1,0:T(1,128)}, u32[]{:S(2)}) copy-start(f32[1,2048]{1,0:T(1,128)} %param.17) | copy-start | bytes 24580
  69.2 41.6 %copy-start.6 = (f32[1,512]{1,0:T(1,128)S(1)}, f32[1,512]{1,0:T(1,128)}, u32[]{:S(2)}) copy-start(f32[1,512]{1,0:T(1,128)} %param.20) | copy-start | bytes 6148
  69.2 41.6 %copy-start.7 = (f32[1,2048]{1,0:T(1,128)S(1)}, f32[1,2048]{1,0:T(1,128)}, u32[]{:S(2)}) copy-start(f32[1,2048]{1,0:T(1,128)} %param.18) | copy-start | bytes 24580
  69.2 41.6 %copy-start.8 = (f32[1,2048]{1,0:T(1,128)S(1)}, f32[1,2048]{1,0:T(1,128)}, u32[]{:S(2)}) copy-start(f32[1,2048]{1,0:T(1,128)} %param.19) | copy-start | bytes 24580
  69.2 41.6 %copy-start.11 = (f32[1,512]{1,0:T(1,128)S(1)}, f32[1,512]{1,0:T(1,128)}, u32[]{:S(2)}) copy-start(f32[1,512]{1,0:T(1,128)} %param.21) | copy-start | bytes 6148
  69.3 41.6 %copy-start.12 = (f32[1,512]{1,0:T(1,128)S(1)}, f32[1,512]{1,0:T(1,128)}, u32[]{:S(2)}) copy-start(f32[1,512]{1,0:T(1,128)} %param.22) | copy-start | bytes 6148
  72.9 37.9 %all-to-all-start.1 = ((bf16[64,20,128]{2,1,0:T(8,128)(2,1)}), bf16[64,20,128]{2,1,0:T(8,128)(2,1)S(1)}, u32[]{:S(2)}, u32[]{:S(2)}) async-start(bf16[64,20,128]{2,1,0:T(8,128)(2,1)} %pad_maximum_fusion), calls=%async_computation.1 | async-start | bytes 786432 | tf_op jit(solution)/shard_map/all_to_all | solution.py:504
  79.9 5.8 %collective-permute-start.17 = (bf16[2,256,128]{2,1,0:T(8,128)(2,1)S(1)}, bf16[2,256,128]{2,1,0:T(8,128)(2,1)S(1)}, u32[]{:S(2)}, u32[]{:S(2)}) collective-permute-start(bf16[2,256,128]{2,1,0:T(8,128)(2,1)S(1)} %get-tuple-element.66), channel_id=1, source_target_pairs={{0,12},{4,0},{8,4},{12,8},{16,28},{20,16},{24,20},{28,24},{32,44},... | collective-permute-start | bytes 393224 | tf_op jit(solution)/shard_map/ppermute | solution.py:446
  82.2 7.1 %collective-permute-start.18 = (bf16[2,256,128]{2,1,0:T(8,128)(2,1)S(1)}, bf16[2,256,128]{2,1,0:T(8,128)(2,1)S(1)}, u32[]{:S(2)}, u32[]{:S(2)}) collective-permute-start(bf16[2,256,128]{2,1,0:T(8,128)(2,1)S(1)} %get-tuple-element.67), channel_id=1, source_target_pairs={{0,8},{4,12},{8,0},{12,4},{16,24},{20,28},{24,16},{28,20},{32,40},... | collective-permute-start | bytes 393224 | tf_op jit(solution)/shard_map/ppermute | solution.py:446
  82.8 12.3 %collective-permute-start.19 = (bf16[2,256,128]{2,1,0:T(8,128)(2,1)S(1)}, bf16[2,256,128]{2,1,0:T(8,128)(2,1)S(1)}, u32[]{:S(2)}, u32[]{:S(2)}) collective-permute-start(bf16[2,256,128]{2,1,0:T(8,128)(2,1)S(1)} %get-tuple-element.68), channel_id=1, source_target_pairs={{0,4},{4,8},{8,12},{12,0},{16,20},{20,24},{24,28},{28,16},{32,36},... | collective-permute-start | bytes 393224 | tf_op jit(solution)/shard_map/ppermute | solution.py:446
  95.2 11.2 %collective-permute-start.20 = (bf16[256,128]{1,0:T(8,128)(2,1)S(1)}, bf16[256,128]{1,0:T(8,128)(2,1)S(1)}, u32[]{:S(2)}, u32[]{:S(2)}) collective-permute-start(bf16[256,128]{1,0:T(8,128)(2,1)S(1)} %get-tuple-element.69), channel_id=1, source_target_pairs={{0,0},{1,2},{2,1},{3,3},{4,4},{5,6},{6,5},{7,7},{8,8},{9,10},{10,9... | collective-permute-start | bytes 196616 | tf_op jit(solution)/shard_map/ppermute | solution.py:518
  99.3 7.2 %collective-permute-start.21 = (bf16[256,128]{1,0:T(8,128)(2,1)S(1)}, bf16[256,128]{1,0:T(8,128)(2,1)S(1)}, u32[]{:S(2)}, u32[]{:S(2)}) collective-permute-start(bf16[256,128]{1,0:T(8,128)(2,1)S(1)} %get-tuple-element.70), channel_id=1, source_target_pairs={{0,240},{1,242},{2,241},{3,243},{4,244},{5,246},{6,245},{7,247},{8... | collective-permute-start | bytes 196616 | tf_op jit(solution)/shard_map/ppermute | solution.py:518
  103.1 7.0 %collective-permute-start.22 = (bf16[256,128]{1,0:T(8,128)(2,1)S(1)}, bf16[256,128]{1,0:T(8,128)(2,1)S(1)}, u32[]{:S(2)}, u32[]{:S(2)}) collective-permute-start(bf16[256,128]{1,0:T(8,128)(2,1)S(1)} %get-tuple-element.71), channel_id=1, source_target_pairs={{0,224},{1,226},{2,225},{3,227},{4,228},{5,230},{6,229},{7,231},{8... | collective-permute-start | bytes 196616 | tf_op jit(solution)/shard_map/ppermute | solution.py:518

commit v4 on v3

--- a/solution.py
+++ b/solution.py
@@ -72,10 +72,26 @@
     )(own, one, two)
 
 
-def stage_kernel(
-    length_ref, shift_ref, fq_ref, go_ref, mask_ref, fq_out, go_out, mask_out, low_out, *, seq_total
-):
-    tokens = fq_ref.shape[0]
+def stage_kernel(fq_ref, go_ref, fq_out, go_out):
+    for h in range(fq_out.shape[0]):
+        lanes = pl.ds(h * HEAD_SIZE, HEAD_SIZE)
+        fq_out[h] = fq_ref[:, lanes]
+        go_out[h] = go_ref[:, lanes]
+
+
+def stage(fq, go):
+    tokens, width = fq.shape
+    by_head = jax.ShapeDtypeStruct((width // HEAD_SIZE, tokens, HEAD_SIZE), jnp.bfloat16)
+    return pl.pallas_call(
+        stage_kernel,
+        out_shape=[by_head, by_head],
+        compiler_params=pltpu.CompilerParams(vmem_limit_bytes=8 << 20),
+        name="stage",
+    )(fq, go)
+
+
+def bounds_kernel(length_ref, shift_ref, mask_ref, mask_out, low_out, *, seq_total):
+    tokens = low_out.shape[1]
     kv_head = lax.axis_index("head") // CORES
     length = length_ref[kv_head]
     first = lax.rem(lax.axis_index("ctx") * tokens - shift_ref[kv_head] + seq_total, seq_total)
@@ -84,29 +100,21 @@
     in_group = jnp.where(in_group >= length, in_group - length, in_group)
     rolled = within + first
     low_out[...] = within - jnp.where(rolled >= seq_total, rolled - seq_total, in_group)
-    for h in range(fq_out.shape[0]):
-        lanes = pl.ds(h * HEAD_SIZE, HEAD_SIZE)
-        fq_out[h] = fq_ref[:, lanes]
-        go_out[h] = go_ref[:, lanes]
     mask_out[...] = mask_ref[...]
 
 
-def stage(length, shift, fq, go, masks, seq_total):
-    tokens, width = fq.shape
-    vmem = pl.BlockSpec(memory_space=pltpu.VMEM)
-    by_head = jax.ShapeDtypeStruct((width // HEAD_SIZE, tokens, HEAD_SIZE), jnp.bfloat16)
-    return pl.pallas_call(
-        functools.partial(stage_kernel, seq_total=seq_total),
-        in_specs=[pl.BlockSpec(memory_space=pltpu.SMEM)] * 2 + [vmem] * 3,
+def bounds(length, shift, masks, tokens, seq_total):
+    smem = pl.BlockSpec(memory_space=pltpu.SMEM)
+    return pl.pallas_call(
+        functools.partial(bounds_kernel, seq_total=seq_total),
+        in_specs=[smem, smem, pl.BlockSpec(memory_space=pltpu.VMEM)],
         out_shape=[
-            by_head,
-            by_head,
             jax.ShapeDtypeStruct(masks.shape, masks.dtype),
             jax.ShapeDtypeStruct((1, tokens), jnp.int32),
         ],
         compiler_params=pltpu.CompilerParams(vmem_limit_bytes=8 << 20),
-        name="stage",
-    )(length, shift, fq, go, masks)
+        name="bounds",
+    )(length, shift, masks)
 
 
 def column_of(row):
@@ -452,14 +460,8 @@
     gathered = lax.all_to_all(row, "ctx", split_axis=0, concat_axis=0)
     packs = pack(mine, one, two)
     direct = [one, two] + [across(p, n + 1) for n, p in enumerate(packs)]
-    queries_in, grads_in, masks_in, low = stage(
-        group_length,
-        group_shift,
-        frozen_queries,
-        output_gradient,
-        rank_keep_mask,
-        tokens * ctx,
-    )
+    queries_in, grads_in = stage(frozen_queries, output_gradient)
+    masks_in, low = bounds(group_length, group_shift, rank_keep_mask, tokens, tokens * ctx)
     swapped = [lax.ppermute(piece, "head", swap) for piece in direct]
 
     down = gathered[:, :down_rows].reshape(ranks, model)

time: 113 us -> 113 us (level)
  no operation moved by 1% of the time
where the time goes in v4:
time: 113 us; the launch traced here: 112 us
  starting transfers between devices  56.4 us (50%)
  waiting for transfers between devices  29.6 us (26%)
  Pallas kernels  15.9 us (14%)
  local copies, waits for them, and re-layouts  7.05 us (6%)
  other arithmetic  1.47 us (1%)
    all_to_all x1, starting transfers between devices, on_device(): gathered = lax.all_to_all(row, 'ctx', split_axis=0, concat_axis=0)  13.6 us
    ppermute x2, waiting for transfers between devices, along(): lax.ppermute(piece, 'ctx', [(i, (i + step) % ctx) for i in range(ctx)])  11.9 us
    ppermute x6, waiting for transfers between devices, across(): return lax.ppermute(piece, 'ctx', pairs)  11.7 us
    ppermute x3, starting transfers between devices, home(): return lax.ppermute(piece, ('ctx', 'head'), pairs).astype(jnp.float32)  10.6 us
    pallas_call x1, Pallas kernels, attention(): pl.pallas_call(functools.partial(attention_kernel, tokens=tokens, heads=h...  9.78 us
    ppermute x6, starting transfers between devices, across(): return lax.ppermute(piece, 'ctx', pairs)  8.01 us
    all_to_all x1, starting transfers between devices, on_device(): received = lax.all_to_all(packed, 'ctx', split_axis=0, concat_axis=0)  7.01 us
    ppermute x5, starting transfers between devices, on_device(): swapped = [lax.ppermute(piece, 'head', swap) for piece in direct]  6.24 us
  transfers between devices with their start and end apart: 25, of which 7 were waited for; matrix products, arithmetic and copies ran while one was open for 2% of the time, Pallas kernels for 2%

profile of v4, /device:TPU:1, one launch (start us, length us, event | category | flops | bytes accessed | tf_op | source)
XLA Modules:
  0.0 112.2 jit_solution(10519026190482310149)
XLA Ops:
  0.6 0.0 copy-start
  0.7 0.0 copy-start.3
  0.7 0.8 copy-done.3
  1.4 0.7 copy-done.5
  2.1 0.8 spread.1
  2.9 13.6 %all-to-all-start = ((bf16[64,20,128]{2,1,0:T(8,128)(2,1)}), bf16[64,20,128]{2,1,0:T(8,128)(2,1)S(1)}, u32[]{:S(2)}, u32[]{:S(2)}) async-start(bf16[64,20,128]{2,1,0:T(8,128)(2,1)} %spread.1), calls=%async_computation | async-start | bytes 786432 | tf_op jit(solution)/shard_map/all_to_all | solution.py:460
  16.5 0.9 constant_dynamic-slice_fusion.1
  17.5 1.1 collective-permute-start
  18.6 2.1 %collective-permute-start.1 = (bf16[256,128]{1,0:T(8,128)(2,1)S(1)}, bf16[256,128]{1,0:T(8,128)(2,1)S(1)}, u32[]{:S(2)}, u32[]{:S(2)}) collective-permute-start(bf16[256,128]{1,0:T(8,128)(2,1)S(1)} %get-tuple-element.83.own_ref), channel_id=1, source_target_pairs={{0,32},{4,36},{8,40},{12,44},{16,48},{20,52},{24,56},{28,60},{32,6... | collective-permute-start | bytes 196616 | tf_op jit(solution)/shard_map/ppermute | solution.py:450
  20.6 7.8 %collective-permute-done.one_ref.refs_7_ = bf16[256,128]{1,0:T(8,128)(2,1)S(1)} collective-permute-done((bf16[256,128]{1,0:T(8,128)(2,1)S(1)}, bf16[256,128]{1,0:T(8,128)(2,1)S(1)}, u32[]{:S(2)}, u32[]{:S(2)}) %collective-permute-start) | collective-permute-done | bytes 65568 | tf_op jit(solution)/shard_map/ppermute | solution.py:450
  28.4 4.2 %collective-permute-done.1.two_ref.refs_8_ = bf16[256,128]{1,0:T(8,128)(2,1)S(1)} collective-permute-done((bf16[256,128]{1,0:T(8,128)(2,1)S(1)}, bf16[256,128]{1,0:T(8,128)(2,1)S(1)}, u32[]{:S(2)}, u32[]{:S(2)}) %collective-permute-start.1) | collective-permute-done | bytes 65568 | tf_op jit(solution)/shard_map/ppermute | solution.py:450
  32.6 1.0 collective-permute-start.2
  33.6 2.5 %collective-permute-start.3 = (bf16[2,256,128]{2,1,0:T(8,128)(2,1)S(1)}, bf16[2,256,128]{2,1,0:T(8,128)(2,1)S(1)}, u32[]{:S(2)}, u32[]{:S(2)}) collective-permute-start(bf16[2,256,128]{2,1,0:T(8,128)(2,1)S(1)} %get-tuple-element.51), channel_id=1, source_target_pairs={{0,8},{4,12},{8,0},{12,4},{16,24},{20,28},{24,16},{28,20},{32,40},... | collective-permute-start | bytes 393224 | tf_op jit(solution)/shard_map/ppermute | solution.py:454
  36.1 1.1 collective-permute-start.4
  37.2 2.9 %collective-permute-start.5 = (bf16[256,128]{1,0:T(8,128)(2,1)S(1)}, bf16[256,128]{1,0:T(8,128)(2,1)S(1)}, u32[]{:S(2)}, u32[]{:S(2)}) collective-permute-start(bf16[256,128]{1,0:T(8,128)(2,1)S(1)} %collective-permute-done.one_ref.refs_7_), channel_id=1, source_target_pairs={{0,1},{1,0},{2,3},{3,2},{4,5},{5,4},{6,7},{7,6},{8,9},{9,8},{10,11... | collective-permute-start | bytes 196616 | tf_op jit(solution)/shard_map/ppermute | solution.py:465
  40.1 0.0 collective-permute-done.2.refs_9_
  40.1 1.9 %collective-permute-start.7 = (bf16[2,256,128]{2,1,0:T(8,128)(2,1)S(1)}, bf16[2,256,128]{2,1,0:T(8,128)(2,1)S(1)}, u32[]{:S(2)}, u32[]{:S(2)}) collective-permute-start(bf16[2,256,128]{2,1,0:T(8,128)(2,1)S(1)} %collective-permute-done.2.refs_9_), channel_id=1, source_target_pairs={{0,1},{1,0},{2,3},{3,2},{4,5},{5,4},{6,7},{7,6},{8,9},{9,8},{10,11... | collective-permute-start | bytes 393224 | tf_op jit(solution)/shard_map/ppermute | solution.py:465
  42.0 0.0 collective-permute-done.3.refs_10_
  42.0 1.4 %collective-permute-start.8 = (bf16[2,256,128]{2,1,0:T(8,128)(2,1)S(1)}, bf16[2,256,128]{2,1,0:T(8,128)(2,1)S(1)}, u32[]{:S(2)}, u32[]{:S(2)}) collective-permute-start(bf16[2,256,128]{2,1,0:T(8,128)(2,1)S(1)} %collective-permute-done.3.refs_10_), channel_id=1, source_target_pairs={{0,1},{1,0},{2,3},{3,2},{4,5},{5,4},{6,7},{7,6},{8,9},{9,8},{10,11... | collective-permute-start | bytes 393224 | tf_op jit(solution)/shard_map/ppermute | solution.py:465
  43.4 0.1 collective-permute-start.9
  43.5 0.4 convolution_convert_fusion.1.refs_17_
  43.9 0.5 collective-permute-start.10
  44.5 2.5 %collective-permute-start.11 = (bf16[64,256]{1,0:T(8,128)(2,1)S(1)}, bf16[64,256]{1,0:T(8,128)(2,1)S(1)}, u32[]{:S(2)}, u32[]{:S(2)}) collective-permute-start(bf16[64,256]{1,0:T(8,128)(2,1)S(1)} %convolution_convert_fusion.1.refs_17_), channel_id=1, source_target_pairs={{0,2},{1,3},{2,0},{3,1},{4,6},{5,7},{6,4},{7,5},{8,10},{9,11},{10,... | collective-permute-start | bytes 98312 | tf_op jit(solution)/shard_map/ppermute | solution.py:472
  46.9 0.8 collective-permute-start.12
  47.7 0.9 copy-done.1
  48.7 0.9 copy-done.2
  49.6 0.1 stage.1
  49.7 0.0 copy-start.9
  49.7 0.7 copy-done.9
  50.4 0.7 copy-done.13
  51.0 0.7 copy-done.14
  51.7 0.6 bounds.1
  52.4 9.8 %attention.1 = (bf16[256,512]{1,0:T(8,128)(2,1)}, bf16[256,512]{1,0:T(8,128)(2,1)}, bf16[64,256]{1,0:T(8,128)(2,1)S(1)}, bf16[64,512]{1,0:T(8,128)(2,1)S(1)}, bf...) custom-call(bf16[4,256,128]{2,1,0:T(8,128)(2,1)S(1)} %get-tuple-element.46.refs_, ...), custom_call_target="tpu_custom_call" | custom-call | flops 2415919104 | bytes 8388608 | tf_op jit(solution)/shard_map/attention/pallas_call | solution.py:257
  62.2 1.4 %kv_send.1 = bf16[2304,128]{1,0:T(8,128)(2,1)S(1)} custom-call(bf16[4,2304,256]{2,1,0:T(8,128)(2,1)S(1)} %get-tuple-element.55.w_ref, bf16[4,2304,256]{2,1,0:T(8,128)(2,1)S(1)} %get-tuple-element.56.gs_ref, bf16[4,256,128]{2,1,0:T(8,128)(2,1)S(1)} %get-tuple-element.47.refs_1_.go_ref, bf16[4,256,128]{2,1,0:T(8,128)(2,1)S(1)} %get-tuple-element.57.q_ref), custom_call_target="tpu_custom_call" | custom-call | flops 603979776 | bytes 2097152 | tf_op jit(solution)/shard_map/kv_send/pallas_call | solution.py:320
  63.5 0.3 collective-permute-start.13
  63.8 0.4 collective-permute-start.14
  64.2 2.5 %collective-permute-start.15 = (bf16[64,256]{1,0:T(8,128)(2,1)S(1)}, bf16[64,256]{1,0:T(8,128)(2,1)S(1)}, u32[]{:S(2)}, u32[]{:S(2)}) collective-permute-start(bf16[64,256]{1,0:T(8,128)(2,1)S(1)} %get-tuple-element.72), channel_id=1, source_target_pairs={{0,2},{1,3},{2,0},{3,1},{4,6},{5,7},{6,4},{7,5},{8,10},{9,11},{10,... | collective-permute-start | bytes 98312 | tf_op jit(solution)/shard_map/ppermute | solution.py:490
  66.7 0.9 collective-permute-start.16
  67.6 1.7 %kv_keep.1.keep_ref = f32[2304,128]{1,0:T(8,128)S(1)} custom-call(bf16[4,2304,256]{2,1,0:T(8,128)(2,1)S(1)} %get-tuple-element.55.w_ref, bf16[4,2304,256]{2,1,0:T(8,128)(2,1)S(1)} %get-tuple-element.56.gs_ref, bf16[4,256,128]{2,1,0:T(8,128)(2,1)S(1)} %get-tuple-element.47.refs_1_.go_ref, bf16[4,256,128]{2,1,0:T(8,128)(2,1)S(1)} %get-tuple-element.57.q_ref), custom_call_target="tpu_custom_call" | custom-call | flops 603979776 | bytes 2097152 | tf_op jit(solution)/shard_map/kv_keep/pallas_call | solution.py:320
  69.2 0.0 copy-start.4
  69.2 0.0 copy-start.6
  69.3 0.0 copy-start.7
  69.3 0.0 copy-start.8
  69.3 0.0 copy-start.11
  69.3 0.0 copy-start.12
  69.3 0.1 pair_sum.1
  69.4 2.3 %collective-permute-done.16 = bf16[64,256]{1,0:T(8,128)(2,1)S(1)} collective-permute-done((bf16[64,256]{1,0:T(8,128)(2,1)S(1)}, bf16[64,256]{1,0:T(8,128)(2,1)S(1)}, u32[]{:S(2)}, u32[]{:S(2)}) %collective-permute-start.16) | collective-permute-done | bytes 32800 | tf_op jit(solution)/shard_map/ppermute | solution.py:490
  71.7 0.3 fusion
  72.2 0.8 pad_maximum_fusion
  72.9 7.0 %all-to-all-start.1 = ((bf16[64,20,128]{2,1,0:T(8,128)(2,1)}), bf16[64,20,128]{2,1,0:T(8,128)(2,1)S(1)}, u32[]{:S(2)}, u32[]{:S(2)}) async-start(bf16[64,20,128]{2,1,0:T(8,128)(2,1)} %pad_maximum_fusion), calls=%async_computation.1 | async-start | bytes 786432 | tf_op jit(solution)/shard_map/all_to_all | solution.py:506
  80.0 2.3 %collective-permute-start.17 = (bf16[2,256,128]{2,1,0:T(8,128)(2,1)S(1)}, bf16[2,256,128]{2,1,0:T(8,128)(2,1)S(1)}, u32[]{:S(2)}, u32[]{:S(2)}) collective-permute-start(bf16[2,256,128]{2,1,0:T(8,128)(2,1)S(1)} %get-tuple-element.66), channel_id=1, source_target_pairs={{0,12},{4,0},{8,4},{12,8},{16,28},{20,16},{24,20},{28,24},{32,44},... | collective-permute-start | bytes 393224 | tf_op jit(solution)/shard_map/ppermute | solution.py:454
  82.3 0.6 collective-permute-start.18
  82.8 0.6 collective-permute-start.19
  83.4 2.4 %collective-permute-done.17.rest_0_ = bf16[2,256,128]{2,1,0:T(8,128)(2,1)S(1)} collective-permute-done((bf16[2,256,128]{2,1,0:T(8,128)(2,1)S(1)}, bf16[2,256,128]{2,1,0:T(8,128)(2,1)S(1)}, u32[]{:S(2)}, u32[]{:S(2)}) %collective-permute-start.17) | collective-permute-done | bytes 131104 | tf_op jit(solution)/shard_map/ppermute | solution.py:454
  85.8 3.6 %collective-permute-done.18.rest_1_ = bf16[2,256,128]{2,1,0:T(8,128)(2,1)S(1)} collective-permute-done((bf16[2,256,128]{2,1,0:T(8,128)(2,1)S(1)}, bf16[2,256,128]{2,1,0:T(8,128)(2,1)S(1)}, u32[]{:S(2)}, u32[]{:S(2)}) %collective-permute-start.18) | collective-permute-done | bytes 131104 | tf_op jit(solution)/shard_map/ppermute | solution.py:454
  89.4 5.7 %collective-permute-done.19.rest_2_ = bf16[2,256,128]{2,1,0:T(8,128)(2,1)S(1)} collective-permute-done((bf16[2,256,128]{2,1,0:T(8,128)(2,1)S(1)}, bf16[2,256,128]{2,1,0:T(8,128)(2,1)S(1)}, u32[]{:S(2)}, u32[]{:S(2)}) %collective-permute-start.19) | collective-permute-done | bytes 131104 | tf_op jit(solution)/shard_map/ppermute | solution.py:454
  95.1 0.1 row_sum.1
  95.3 4.1 %collective-permute-start.20 = (bf16[256,128]{1,0:T(8,128)(2,1)S(1)}, bf16[256,128]{1,0:T(8,128)(2,1)S(1)}, u32[]{:S(2)}, u32[]{:S(2)}) collective-permute-start(bf16[256,128]{1,0:T(8,128)(2,1)S(1)} %get-tuple-element.69), channel_id=1, source_target_pairs={{0,0},{1,2},{2,1},{3,3},{4,4},{5,6},{6,5},{7,7},{8,8},{9,10},{10,9... | collective-permute-start | bytes 196616 | tf_op jit(solution)/shard_map/ppermute | solution.py:520
  99.3 3.8 %collective-permute-start.21 = (bf16[256,128]{1,0:T(8,128)(2,1)S(1)}, bf16[256,128]{1,0:T(8,128)(2,1)S(1)}, u32[]{:S(2)}, u32[]{:S(2)}) collective-permute-start(bf16[256,128]{1,0:T(8,128)(2,1)S(1)} %get-tuple-element.70), channel_id=1, source_target_pairs={{0,240},{1,242},{2,241},{3,243},{4,244},{5,246},{6,245},{7,247},{8... | collective-permute-start | bytes 196616 | tf_op jit(solution)/shard_map/ppermute | solution.py:520
  103.1 2.7 %collective-permute-start.22 = (bf16[256,128]{1,0:T(8,128)(2,1)S(1)}, bf16[256,128]{1,0:T(8,128)(2,1)S(1)}, u32[]{:S(2)}, u32[]{:S(2)}) collective-permute-start(bf16[256,128]{1,0:T(8,128)(2,1)S(1)} %get-tuple-element.71), channel_id=1, source_target_pairs={{0,224},{1,226},{2,225},{3,227},{4,228},{5,230},{6,229},{7,231},{8... | collective-permute-start | bytes 196616 | tf_op jit(solution)/shard_map/ppermute | solution.py:520
  105.9 0.6 constant_dynamic-slice_fusion.keep_ref
  106.5 3.6 %collective-permute-done.22 = bf16[256,128]{1,0:T(8,128)(2,1)S(1)} collective-permute-done((bf16[256,128]{1,0:T(8,128)(2,1)S(1)}, bf16[256,128]{1,0:T(8,128)(2,1)S(1)}, u32[]{:S(2)}, u32[]{:S(2)}) %collective-permute-start.22) | collective-permute-done | bytes 65568 | tf_op jit(solution)/shard_map/ppermute | solution.py:520
  110.1 0.7 convert_add_fusion
  110.9 1.3 %adam.1 = (f32[16,128]{1,0:T(8,128)}, f32[16,128]{1,0:T(8,128)}, f32[16,128]{1,0:T(8,128)}, f32[4,128]{1,0:T(4,128)}, f32[4,128]{1,0:T(4,128)}, /*index=5*/f32[4,128]{1,0:T(4,128)}) custom-call(bf16[64,20,128]{2,1,0:T(8,128)(2,1)S(1)} %all-to-all-done.1.got_ref, f32[16,128]{1,0:T(8,128)S(1)} %bitcast.29, f32[16,128]{1,0:T(8,128)S(1)} %bitcast.32, ...), custom_call_target="tpu_custom_call" | custom-call | tf_op jit(solution)/shard_map/adam/pallas_call | solution.py:536
  (39 shorter events, 0.2 us)
Async XLA Ops:
  0.6 42.8 %copy-start = (bf16[256,2048]{1,0:T(8,128)(2,1)S(1)}, bf16[256,2048]{1,0:T(8,128)(2,1)}, u32[]{:S(2)}) copy-start(bf16[256,2048]{1,0:T(8,128)(2,1)} %param.16) | copy-start | bytes 3145732
  0.7 0.8 copy-start.3
  1.4 0.7 copy-start.5
  2.9 40.5 %all-to-all-start = ((bf16[64,20,128]{2,1,0:T(8,128)(2,1)}), bf16[64,20,128]{2,1,0:T(8,128)(2,1)S(1)}, u32[]{:S(2)}, u32[]{:S(2)}) async-start(bf16[64,20,128]{2,1,0:T(8,128)(2,1)} %spread.1), calls=%async_computation | async-start | bytes 786432 | tf_op jit(solution)/shard_map/all_to_all | solution.py:460
  17.5 10.9 %collective-permute-start = (bf16[256,128]{1,0:T(8,128)(2,1)S(1)}, bf16[256,128]{1,0:T(8,128)(2,1)S(1)}, u32[]{:S(2)}, u32[]{:S(2)}) collective-permute-start(bf16[256,128]{1,0:T(8,128)(2,1)S(1)} %get-tuple-element.83.own_ref), channel_id=1, source_target_pairs={{0,16},{4,20},{8,24},{12,28},{16,32},{20,36},{24,40},{28,44},{32,4... | collective-permute-start | bytes 196616 | tf_op jit(solution)/shard_map/ppermute | solution.py:450
  18.6 14.0 %collective-permute-start.1 = (bf16[256,128]{1,0:T(8,128)(2,1)S(1)}, bf16[256,128]{1,0:T(8,128)(2,1)S(1)}, u32[]{:S(2)}, u32[]{:S(2)}) collective-permute-start(bf16[256,128]{1,0:T(8,128)(2,1)S(1)} %get-tuple-element.83.own_ref), channel_id=1, source_target_pairs={{0,32},{4,36},{8,40},{12,44},{16,48},{20,52},{24,56},{28,60},{32,6... | collective-permute-start | bytes 196616 | tf_op jit(solution)/shard_map/ppermute | solution.py:450
  32.6 7.5 %collective-permute-start.2 = (bf16[2,256,128]{2,1,0:T(8,128)(2,1)S(1)}, bf16[2,256,128]{2,1,0:T(8,128)(2,1)S(1)}, u32[]{:S(2)}, u32[]{:S(2)}) collective-permute-start(bf16[2,256,128]{2,1,0:T(8,128)(2,1)S(1)} %get-tuple-element.50), channel_id=1, source_target_pairs={{0,4},{4,8},{8,12},{12,0},{16,20},{20,24},{24,28},{28,16},{32,36},... | collective-permute-start | bytes 393224 | tf_op jit(solution)/shard_map/ppermute | solution.py:454
  33.6 8.3 %collective-permute-start.3 = (bf16[2,256,128]{2,1,0:T(8,128)(2,1)S(1)}, bf16[2,256,128]{2,1,0:T(8,128)(2,1)S(1)}, u32[]{:S(2)}, u32[]{:S(2)}) collective-permute-start(bf16[2,256,128]{2,1,0:T(8,128)(2,1)S(1)} %get-tuple-element.51), channel_id=1, source_target_pairs={{0,8},{4,12},{8,0},{12,4},{16,24},{20,28},{24,16},{28,20},{32,40},... | collective-permute-start | bytes 393224 | tf_op jit(solution)/shard_map/ppermute | solution.py:454
  36.1 7.3 %collective-permute-start.4 = (bf16[2,256,128]{2,1,0:T(8,128)(2,1)S(1)}, bf16[2,256,128]{2,1,0:T(8,128)(2,1)S(1)}, u32[]{:S(2)}, u32[]{:S(2)}) collective-permute-start(bf16[2,256,128]{2,1,0:T(8,128)(2,1)S(1)} %get-tuple-element.52), channel_id=1, source_target_pairs={{0,12},{4,0},{8,4},{12,8},{16,28},{20,16},{24,20},{28,24},{32,44},... | collective-permute-start | bytes 393224 | tf_op jit(solution)/shard_map/ppermute | solution.py:454
  37.2 6.7 %collective-permute-start.5 = (bf16[256,128]{1,0:T(8,128)(2,1)S(1)}, bf16[256,128]{1,0:T(8,128)(2,1)S(1)}, u32[]{:S(2)}, u32[]{:S(2)}) collective-permute-start(bf16[256,128]{1,0:T(8,128)(2,1)S(1)} %collective-permute-done.one_ref.refs_7_), channel_id=1, source_target_pairs={{0,1},{1,0},{2,3},{3,2},{4,5},{5,4},{6,7},{7,6},{8,9},{9,8},{10,11... | collective-permute-start | bytes 196616 | tf_op jit(solution)/shard_map/ppermute | solution.py:465
  40.1 4.4 %collective-permute-start.6 = (bf16[256,128]{1,0:T(8,128)(2,1)S(1)}, bf16[256,128]{1,0:T(8,128)(2,1)S(1)}, u32[]{:S(2)}, u32[]{:S(2)}) collective-permute-start(bf16[256,128]{1,0:T(8,128)(2,1)S(1)} %collective-permute-done.1.two_ref.refs_8_), channel_id=1, source_target_pairs={{0,1},{1,0},{2,3},{3,2},{4,5},{5,4},{6,7},{7,6},{8,9},{9,8},{10,11... | collective-permute-start | bytes 196616 | tf_op jit(solution)/shard_map/ppermute | solution.py:465
  40.1 6.8 %collective-permute-start.7 = (bf16[2,256,128]{2,1,0:T(8,128)(2,1)S(1)}, bf16[2,256,128]{2,1,0:T(8,128)(2,1)S(1)}, u32[]{:S(2)}, u32[]{:S(2)}) collective-permute-start(bf16[2,256,128]{2,1,0:T(8,128)(2,1)S(1)} %collective-permute-done.2.refs_9_), channel_id=1, source_target_pairs={{0,1},{1,0},{2,3},{3,2},{4,5},{5,4},{6,7},{7,6},{8,9},{9,8},{10,11... | collective-permute-start | bytes 393224 | tf_op jit(solution)/shard_map/ppermute | solution.py:465
  42.0 10.4 %collective-permute-start.8 = (bf16[2,256,128]{2,1,0:T(8,128)(2,1)S(1)}, bf16[2,256,128]{2,1,0:T(8,128)(2,1)S(1)}, u32[]{:S(2)}, u32[]{:S(2)}) collective-permute-start(bf16[2,256,128]{2,1,0:T(8,128)(2,1)S(1)} %collective-permute-done.3.refs_10_), channel_id=1, source_target_pairs={{0,1},{1,0},{2,3},{3,2},{4,5},{5,4},{6,7},{7,6},{8,9},{9,8},{10,11... | collective-permute-start | bytes 393224 | tf_op jit(solution)/shard_map/ppermute | solution.py:465
  43.4 9.0 %collective-permute-start.9 = (bf16[2,256,128]{2,1,0:T(8,128)(2,1)S(1)}, bf16[2,256,128]{2,1,0:T(8,128)(2,1)S(1)}, u32[]{:S(2)}, u32[]{:S(2)}) collective-permute-start(bf16[2,256,128]{2,1,0:T(8,128)(2,1)S(1)} %collective-permute-done.4.refs_11_), channel_id=1, source_target_pairs={{0,1},{1,0},{2,3},{3,2},{4,5},{5,4},{6,7},{7,6},{8,9},{9,8},{10,11... | collective-permute-start | bytes 393224 | tf_op jit(solution)/shard_map/ppermute | solution.py:465
  43.9 8.4 %collective-permute-start.10 = (bf16[64,256]{1,0:T(8,128)(2,1)S(1)}, bf16[64,256]{1,0:T(8,128)(2,1)S(1)}, u32[]{:S(2)}, u32[]{:S(2)}) collective-permute-start(bf16[64,256]{1,0:T(8,128)(2,1)S(1)} %convolution_convert_fusion.1.refs_17_), channel_id=1, source_target_pairs={{0,1},{1,0},{2,3},{3,2},{4,5},{5,4},{6,7},{7,6},{8,9},{9,8},{10,11... | collective-permute-start | bytes 98312 | tf_op jit(solution)/shard_map/ppermute | solution.py:472
  44.5 7.9 %collective-permute-start.11 = (bf16[64,256]{1,0:T(8,128)(2,1)S(1)}, bf16[64,256]{1,0:T(8,128)(2,1)S(1)}, u32[]{:S(2)}, u32[]{:S(2)}) collective-permute-start(bf16[64,256]{1,0:T(8,128)(2,1)S(1)} %convolution_convert_fusion.1.refs_17_), channel_id=1, source_target_pairs={{0,2},{1,3},{2,0},{3,1},{4,6},{5,7},{6,4},{7,5},{8,10},{9,11},{10,... | collective-permute-start | bytes 98312 | tf_op jit(solution)/shard_map/ppermute | solution.py:472
  46.9 5.5 %collective-permute-start.12 = (bf16[64,256]{1,0:T(8,128)(2,1)S(1)}, bf16[64,256]{1,0:T(8,128)(2,1)S(1)}, u32[]{:S(2)}, u32[]{:S(2)}) collective-permute-start(bf16[64,256]{1,0:T(8,128)(2,1)S(1)} %convolution_convert_fusion.1.refs_17_), channel_id=1, source_target_pairs={{0,3},{1,2},{2,1},{3,0},{4,7},{5,6},{6,5},{7,4},{8,11},{9,10},{10,... | collective-permute-start | bytes 98312 | tf_op jit(solution)/shard_map/ppermute | solution.py:472
  47.7 0.9 copy-start.1
  48.6 0.9 copy-start.2
  49.7 0.7 copy-start.9
  50.4 0.7 copy-start.13
  51.0 0.7 copy-start.14
  62.1 1.7 %copy-start.10 = (s32[2,64]{1,0:T(2,128)S(1)}, s32[2,64]{1,0:T(2,128)}, u32[]{:S(2)}) copy-start(s32[2,64]{1,0:T(2,128)} %mask_ref.1) | copy-start | bytes 1540
  63.5 5.8 %collective-permute-start.13 = (bf16[2304,128]{1,0:T(8,128)(2,1)S(1)}, bf16[2304,128]{1,0:T(8,128)(2,1)S(1)}, u32[]{:S(2)}, u32[]{:S(2)}) collective-permute-start(bf16[2304,128]{1,0:T(8,128)(2,1)S(1)} %kv_send.1), channel_id=1, source_target_pairs={{0,1},{1,0},{2,3},{3,2},{4,5},{5,4},{6,7},{7,6},{8,9},{9,8},{10,11... | collective-permute-start | bytes 1769480 | tf_op jit(solution)/shard_map/ppermute | solution.py:492
  63.8 5.6 %collective-permute-start.14 = (bf16[64,256]{1,0:T(8,128)(2,1)S(1)}, bf16[64,256]{1,0:T(8,128)(2,1)S(1)}, u32[]{:S(2)}, u32[]{:S(2)}) collective-permute-start(bf16[64,256]{1,0:T(8,128)(2,1)S(1)} %get-tuple-element.72), channel_id=1, source_target_pairs={{0,1},{1,0},{2,3},{3,2},{4,5},{5,4},{6,7},{7,6},{8,9},{9,8},{10,11... | collective-permute-start | bytes 98312 | tf_op jit(solution)/shard_map/ppermute | solution.py:490
  64.2 5.2 %collective-permute-start.15 = (bf16[64,256]{1,0:T(8,128)(2,1)S(1)}, bf16[64,256]{1,0:T(8,128)(2,1)S(1)}, u32[]{:S(2)}, u32[]{:S(2)}) collective-permute-start(bf16[64,256]{1,0:T(8,128)(2,1)S(1)} %get-tuple-element.72), channel_id=1, source_target_pairs={{0,2},{1,3},{2,0},{3,1},{4,6},{5,7},{6,4},{7,5},{8,10},{9,11},{10,... | collective-permute-start | bytes 98312 | tf_op jit(solution)/shard_map/ppermute | solution.py:490
  66.7 5.1 %collective-permute-start.16 = (bf16[64,256]{1,0:T(8,128)(2,1)S(1)}, bf16[64,256]{1,0:T(8,128)(2,1)S(1)}, u32[]{:S(2)}, u32[]{:S(2)}) collective-permute-start(bf16[64,256]{1,0:T(8,128)(2,1)S(1)} %get-tuple-element.72), channel_id=1, source_target_pairs={{0,3},{1,2},{2,1},{3,0},{4,7},{5,6},{6,5},{7,4},{8,11},{9,10},{10,... | collective-permute-start | bytes 98312 | tf_op jit(solution)/shard_map/ppermute | solution.py:490
  69.2 41.6 %copy-start.4 = (f32[1,2048]{1,0:T(1,128)S(1)}, f32[1,2048]{1,0:T(1,128)}, u32[]{:S(2)}) copy-start(f32[1,2048]{1,0:T(1,128)} %param.17) | copy-start | bytes 24580
  69.2 41.6 %copy-start.6 = (f32[1,512]{1,0:T(1,128)S(1)}, f32[1,512]{1,0:T(1,128)}, u32[]{:S(2)}) copy-start(f32[1,512]{1,0:T(1,128)} %param.20) | copy-start | bytes 6148
  69.3 41.6 %copy-start.7 = (f32[1,2048]{1,0:T(1,128)S(1)}, f32[1,2048]{1,0:T(1,128)}, u32[]{:S(2)}) copy-start(f32[1,2048]{1,0:T(1,128)} %param.18) | copy-start | bytes 24580
  69.3 41.6 %copy-start.8 = (f32[1,2048]{1,0:T(1,128)S(1)}, f32[1,2048]{1,0:T(1,128)}, u32[]{:S(2)}) copy-start(f32[1,2048]{1,0:T(1,128)} %param.19) | copy-start | bytes 24580
  69.3 41.6 %copy-start.11 = (f32[1,512]{1,0:T(1,128)S(1)}, f32[1,512]{1,0:T(1,128)}, u32[]{:S(2)}) copy-start(f32[1,512]{1,0:T(1,128)} %param.21) | copy-start | bytes 6148
  69.3 41.6 %copy-start.12 = (f32[1,512]{1,0:T(1,128)S(1)}, f32[1,512]{1,0:T(1,128)}, u32[]{:S(2)}) copy-start(f32[1,512]{1,0:T(1,128)} %param.22) | copy-start | bytes 6148
  72.9 37.9 %all-to-all-start.1 = ((bf16[64,20,128]{2,1,0:T(8,128)(2,1)}), bf16[64,20,128]{2,1,0:T(8,128)(2,1)S(1)}, u32[]{:S(2)}, u32[]{:S(2)}) async-start(bf16[64,20,128]{2,1,0:T(8,128)(2,1)} %pad_maximum_fusion), calls=%async_computation.1 | async-start | bytes 786432 | tf_op jit(solution)/shard_map/all_to_all | solution.py:506
  80.0 5.8 %collective-permute-start.17 = (bf16[2,256,128]{2,1,0:T(8,128)(2,1)S(1)}, bf16[2,256,128]{2,1,0:T(8,128)(2,1)S(1)}, u32[]{:S(2)}, u32[]{:S(2)}) collective-permute-start(bf16[2,256,128]{2,1,0:T(8,128)(2,1)S(1)} %get-tuple-element.66), channel_id=1, source_target_pairs={{0,12},{4,0},{8,4},{12,8},{16,28},{20,16},{24,20},{28,24},{32,44},... | collective-permute-start | bytes 393224 | tf_op jit(solution)/shard_map/ppermute | solution.py:454
  82.3 7.1 %collective-permute-start.18 = (bf16[2,256,128]{2,1,0:T(8,128)(2,1)S(1)}, bf16[2,256,128]{2,1,0:T(8,128)(2,1)S(1)}, u32[]{:S(2)}, u32[]{:S(2)}) collective-permute-start(bf16[2,256,128]{2,1,0:T(8,128)(2,1)S(1)} %get-tuple-element.67), channel_id=1, source_target_pairs={{0,8},{4,12},{8,0},{12,4},{16,24},{20,28},{24,16},{28,20},{32,40},... | collective-permute-start | bytes 393224 | tf_op jit(solution)/shard_map/ppermute | solution.py:454
  82.8 12.3 %collective-permute-start.19 = (bf16[2,256,128]{2,1,0:T(8,128)(2,1)S(1)}, bf16[2,256,128]{2,1,0:T(8,128)(2,1)S(1)}, u32[]{:S(2)}, u32[]{:S(2)}) collective-permute-start(bf16[2,256,128]{2,1,0:T(8,128)(2,1)S(1)} %get-tuple-element.68), channel_id=1, source_target_pairs={{0,4},{4,8},{8,12},{12,0},{16,20},{20,24},{24,28},{28,16},{32,36},... | collective-permute-start | bytes 393224 | tf_op jit(solution)/shard_map/ppermute | solution.py:454
  95.3 11.2 %collective-permute-start.20 = (bf16[256,128]{1,0:T(8,128)(2,1)S(1)}, bf16[256,128]{1,0:T(8,128)(2,1)S(1)}, u32[]{:S(2)}, u32[]{:S(2)}) collective-permute-start(bf16[256,128]{1,0:T(8,128)(2,1)S(1)} %get-tuple-element.69), channel_id=1, source_target_pairs={{0,0},{1,2},{2,1},{3,3},{4,4},{5,6},{6,5},{7,7},{8,8},{9,10},{10,9... | collective-permute-start | bytes 196616 | tf_op jit(solution)/shard_map/ppermute | solution.py:520
  99.3 7.2 %collective-permute-start.21 = (bf16[256,128]{1,0:T(8,128)(2,1)S(1)}, bf16[256,128]{1,0:T(8,128)(2,1)S(1)}, u32[]{:S(2)}, u32[]{:S(2)}) collective-permute-start(bf16[256,128]{1,0:T(8,128)(2,1)S(1)} %get-tuple-element.70), channel_id=1, source_target_pairs={{0,240},{1,242},{2,241},{3,243},{4,244},{5,246},{6,245},{7,247},{8... | collective-permute-start | bytes 196616 | tf_op jit(solution)/shard_map/ppermute | solution.py:520
  103.1 7.0 %collective-permute-start.22 = (bf16[256,128]{1,0:T(8,128)(2,1)S(1)}, bf16[256,128]{1,0:T(8,128)(2,1)S(1)}, u32[]{:S(2)}, u32[]{:S(2)}) collective-permute-start(bf16[256,128]{1,0:T(8,128)(2,1)S(1)} %get-tuple-element.71), channel_id=1, source_target_pairs={{0,224},{1,226},{2,225},{3,227},{4,228},{5,230},{6,229},{7,231},{8... | collective-permute-start | bytes 196616 | tf_op jit(solution)/shard_map/ppermute | solution.py:520

commit v5 on v4

--- a/solution.py
+++ b/solution.py
@@ -382,19 +382,19 @@
     )(own, one, two, *packs)
 
 
-def spread_kernel(down_ref, up_ref, out_ref):
-    row = jnp.concatenate([down_ref[...], up_ref[...]], 0).astype(jnp.bfloat16)
+def spread_kernel(row_ref, out_ref):
+    row = row_ref[...].astype(jnp.bfloat16)
     for n in range(out_ref.shape[0]):
         out_ref[n] = row
 
 
-def spread(down, up, copies):
+def spread(row, copies):
     return pl.pallas_call(
         spread_kernel,
-        out_shape=jax.ShapeDtypeStruct((copies, down.shape[0] + up.shape[0], 128), jnp.bfloat16),
+        out_shape=jax.ShapeDtypeStruct((copies,) + row.shape, jnp.bfloat16),
         compiler_params=pltpu.CompilerParams(vmem_limit_bytes=4 << 20),
         name="spread",
-    )(down, up)
+    )(row)
 
 
 def adam_kernel(got_ref, pd, md, vd, pu, mu, vu, keep_ref, opd, omd, ovd, opu, omu, ovu):
@@ -456,7 +456,10 @@
     one, two = along(mine, COLUMNS), along(mine, 2 * COLUMNS)
 
     down_rows, up_rows = model // 128, width // 128
-    row = spread(adapter_down.reshape(down_rows, 128), adapter_up.reshape(up_rows, 128), ctx)
+    row = jnp.concatenate(
+        [adapter_down.reshape(down_rows, 128), adapter_up.reshape(up_rows, 128)], 0
+    )
+    row = spread(row, ctx)
     gathered = lax.all_to_all(row, "ctx", split_axis=0, concat_axis=0)
     packs = pack(mine, one, two)
     direct = [one, two] + [across(p, n + 1) for n, p in enumerate(packs)]
@@ -517,7 +520,8 @@
             for i in range(ctx)
             for h in range(head_count)
         ]
-        return lax.ppermute(piece, ("ctx", "head"), pairs).astype(jnp.float32)
+        piece = lax.ppermute(piece, ("ctx", "head"), pairs)
+        return piece.astype(jnp.float32)
 
     kv_grad = home(own_sum, 0) + home(one_sum, COLUMNS) + home(two_sum, 2 * COLUMNS)
 

time: 113 us -> 112 us (level)
  local copies, waits for them, and re-layouts: 7.05 us -> 5.59 us
    unnamed x32 -> x28, local copies, waits for them, and re-layouts: 5.44 us -> 3.98 us
where the time goes in v5:
time: 112 us
  starting transfers between devices  56.4 us (50%)
  waiting for transfers between devices  29.6 us (26%)
  Pallas kernels  15.8 us (14%)
  local copies, waits for them, and re-layouts  5.59 us (5%)
  other arithmetic  2.28 us (2%)
    all_to_all x1, starting transfers between devices, on_device(): gathered = lax.all_to_all(row, 'ctx', split_axis=0, concat_axis=0)  13.6 us
    ppermute x2, waiting for transfers between devices, along(): lax.ppermute(piece, 'ctx', [(i, (i + step) % ctx) for i in range(ctx)])  11.9 us
    ppermute x6, waiting for transfers between devices, across(): return lax.ppermute(piece, 'ctx', pairs)  11.7 us
    ppermute x3, starting transfers between devices, home(): piece = lax.ppermute(piece, ('ctx', 'head'), pairs)  10.6 us
    pallas_call x1, Pallas kernels, attention(): pl.pallas_call(functools.partial(attention_kernel, tokens=tokens, heads=h...  9.78 us
    ppermute x6, starting transfers between devices, across(): return lax.ppermute(piece, 'ctx', pairs)  8.01 us
    all_to_all x1, starting transfers between devices, on_device(): received = lax.all_to_all(packed, 'ctx', split_axis=0, concat_axis=0)  7.03 us
    ppermute x5, starting transfers between devices, on_device(): swapped = [lax.ppermute(piece, 'head', swap) for piece in direct]  6.24 us
  transfers between devices with their start and end apart: 25, of which 7 were waited for; matrix products, arithmetic and copies ran while one was open for 2% of the time, Pallas kernels for 2%

profile of v5, /device:TPU:1, one launch (start us, length us, event | category | flops | bytes accessed | tf_op | source)
XLA Modules:
  0.0 111.5 jit_solution(8874090586393812016)
XLA Ops:
  0.6 0.0 copy-start
  0.7 0.8 pad_maximum_fusion.1.row_ref
  1.5 0.8 spread.1
  2.3 13.6 %all-to-all-start = ((bf16[64,20,128]{2,1,0:T(8,128)(2,1)}), bf16[64,20,128]{2,1,0:T(8,128)(2,1)S(1)}, u32[]{:S(2)}, u32[]{:S(2)}) async-start(bf16[64,20,128]{2,1,0:T(8,128)(2,1)} %spread.1), calls=%async_computation | async-start | bytes 786432 | tf_op jit(solution)/shard_map/all_to_all | solution.py:463
  15.9 0.9 constant_dynamic-slice_fusion.1
  16.8 1.1 collective-permute-start
  17.9 2.1 %collective-permute-start.1 = (bf16[256,128]{1,0:T(8,128)(2,1)S(1)}, bf16[256,128]{1,0:T(8,128)(2,1)S(1)}, u32[]{:S(2)}, u32[]{:S(2)}) collective-permute-start(bf16[256,128]{1,0:T(8,128)(2,1)S(1)} %get-tuple-element.83.own_ref), channel_id=1, source_target_pairs={{0,32},{4,36},{8,40},{12,44},{16,48},{20,52},{24,56},{28,60},{32,6... | collective-permute-start | bytes 196616 | tf_op jit(solution)/shard_map/ppermute | solution.py:450
  20.0 7.8 %collective-permute-done.one_ref.refs_7_ = bf16[256,128]{1,0:T(8,128)(2,1)S(1)} collective-permute-done((bf16[256,128]{1,0:T(8,128)(2,1)S(1)}, bf16[256,128]{1,0:T(8,128)(2,1)S(1)}, u32[]{:S(2)}, u32[]{:S(2)}) %collective-permute-start) | collective-permute-done | bytes 65568 | tf_op jit(solution)/shard_map/ppermute | solution.py:450
  27.8 4.2 %collective-permute-done.1.two_ref.refs_8_ = bf16[256,128]{1,0:T(8,128)(2,1)S(1)} collective-permute-done((bf16[256,128]{1,0:T(8,128)(2,1)S(1)}, bf16[256,128]{1,0:T(8,128)(2,1)S(1)}, u32[]{:S(2)}, u32[]{:S(2)}) %collective-permute-start.1) | collective-permute-done | bytes 65568 | tf_op jit(solution)/shard_map/ppermute | solution.py:450
  32.0 1.0 collective-permute-start.2
  33.0 2.5 %collective-permute-start.3 = (bf16[2,256,128]{2,1,0:T(8,128)(2,1)S(1)}, bf16[2,256,128]{2,1,0:T(8,128)(2,1)S(1)}, u32[]{:S(2)}, u32[]{:S(2)}) collective-permute-start(bf16[2,256,128]{2,1,0:T(8,128)(2,1)S(1)} %get-tuple-element.51), channel_id=1, source_target_pairs={{0,8},{4,12},{8,0},{12,4},{16,24},{20,28},{24,16},{28,20},{32,40},... | collective-permute-start | bytes 393224 | tf_op jit(solution)/shard_map/ppermute | solution.py:454
  35.4 1.1 collective-permute-start.4
  36.5 2.9 %collective-permute-start.5 = (bf16[256,128]{1,0:T(8,128)(2,1)S(1)}, bf16[256,128]{1,0:T(8,128)(2,1)S(1)}, u32[]{:S(2)}, u32[]{:S(2)}) collective-permute-start(bf16[256,128]{1,0:T(8,128)(2,1)S(1)} %collective-permute-done.one_ref.refs_7_), channel_id=1, source_target_pairs={{0,1},{1,0},{2,3},{3,2},{4,5},{5,4},{6,7},{7,6},{8,9},{9,8},{10,11... | collective-permute-start | bytes 196616 | tf_op jit(solution)/shard_map/ppermute | solution.py:468
  39.4 0.0 collective-permute-start.6
  39.4 0.0 collective-permute-done.2.refs_9_
  39.4 1.9 %collective-permute-start.7 = (bf16[2,256,128]{2,1,0:T(8,128)(2,1)S(1)}, bf16[2,256,128]{2,1,0:T(8,128)(2,1)S(1)}, u32[]{:S(2)}, u32[]{:S(2)}) collective-permute-start(bf16[2,256,128]{2,1,0:T(8,128)(2,1)S(1)} %collective-permute-done.2.refs_9_), channel_id=1, source_target_pairs={{0,1},{1,0},{2,3},{3,2},{4,5},{5,4},{6,7},{7,6},{8,9},{9,8},{10,11... | collective-permute-start | bytes 393224 | tf_op jit(solution)/shard_map/ppermute | solution.py:468
  41.3 1.4 %collective-permute-start.8 = (bf16[2,256,128]{2,1,0:T(8,128)(2,1)S(1)}, bf16[2,256,128]{2,1,0:T(8,128)(2,1)S(1)}, u32[]{:S(2)}, u32[]{:S(2)}) collective-permute-start(bf16[2,256,128]{2,1,0:T(8,128)(2,1)S(1)} %collective-permute-done.3.refs_10_), channel_id=1, source_target_pairs={{0,1},{1,0},{2,3},{3,2},{4,5},{5,4},{6,7},{7,6},{8,9},{9,8},{10,11... | collective-permute-start | bytes 393224 | tf_op jit(solution)/shard_map/ppermute | solution.py:468
  42.7 0.0 collective-permute-done.4.refs_11_
  42.7 0.1 collective-permute-start.9
  42.8 0.0 all-to-all-done
  42.8 0.4 convolution_convert_fusion.1.refs_17_
  43.3 0.5 collective-permute-start.10
  43.8 2.5 %collective-permute-start.11 = (bf16[64,256]{1,0:T(8,128)(2,1)S(1)}, bf16[64,256]{1,0:T(8,128)(2,1)S(1)}, u32[]{:S(2)}, u32[]{:S(2)}) collective-permute-start(bf16[64,256]{1,0:T(8,128)(2,1)S(1)} %convolution_convert_fusion.1.refs_17_), channel_id=1, source_target_pairs={{0,2},{1,3},{2,0},{3,1},{4,6},{5,7},{6,4},{7,5},{8,10},{9,11},{10,... | collective-permute-start | bytes 98312 | tf_op jit(solution)/shard_map/ppermute | solution.py:475
  46.2 0.8 collective-permute-start.12
  47.0 0.9 copy-done.1
  48.0 0.9 copy-done.2
  48.9 0.1 stage.1
  49.0 0.0 copy-start.7
  49.0 0.7 copy-done.7
  49.7 0.7 copy-done.11
  50.4 0.7 copy-done.12
  51.0 0.6 bounds.1
  51.7 9.8 %attention.1 = (bf16[256,512]{1,0:T(8,128)(2,1)}, bf16[256,512]{1,0:T(8,128)(2,1)}, bf16[64,256]{1,0:T(8,128)(2,1)S(1)}, bf16[64,512]{1,0:T(8,128)(2,1)S(1)}, bf...) custom-call(bf16[4,256,128]{2,1,0:T(8,128)(2,1)S(1)} %get-tuple-element.46.refs_, ...), custom_call_target="tpu_custom_call" | custom-call | flops 2415919104 | bytes 8388608 | tf_op jit(solution)/shard_map/attention/pallas_call | solution.py:257
  61.5 1.4 %kv_send.1 = bf16[2304,128]{1,0:T(8,128)(2,1)S(1)} custom-call(bf16[4,2304,256]{2,1,0:T(8,128)(2,1)S(1)} %get-tuple-element.55.w_ref, bf16[4,2304,256]{2,1,0:T(8,128)(2,1)S(1)} %get-tuple-element.56.gs_ref, bf16[4,256,128]{2,1,0:T(8,128)(2,1)S(1)} %get-tuple-element.47.refs_1_.go_ref, bf16[4,256,128]{2,1,0:T(8,128)(2,1)S(1)} %get-tuple-element.57.q_ref), custom_call_target="tpu_custom_call" | custom-call | flops 603979776 | bytes 2097152 | tf_op jit(solution)/shard_map/kv_send/pallas_call | solution.py:320
  62.9 0.3 collective-permute-start.13
  63.2 0.4 collective-permute-start.14
  63.6 2.5 %collective-permute-start.15 = (bf16[64,256]{1,0:T(8,128)(2,1)S(1)}, bf16[64,256]{1,0:T(8,128)(2,1)S(1)}, u32[]{:S(2)}, u32[]{:S(2)}) collective-permute-start(bf16[64,256]{1,0:T(8,128)(2,1)S(1)} %get-tuple-element.72), channel_id=1, source_target_pairs={{0,2},{1,3},{2,0},{3,1},{4,6},{5,7},{6,4},{7,5},{8,10},{9,11},{10,... | collective-permute-start | bytes 98312 | tf_op jit(solution)/shard_map/ppermute | solution.py:493
  66.0 0.9 collective-permute-start.16
  66.9 1.7 %kv_keep.1.keep_ref = f32[2304,128]{1,0:T(8,128)S(1)} custom-call(bf16[4,2304,256]{2,1,0:T(8,128)(2,1)S(1)} %get-tuple-element.55.w_ref, bf16[4,2304,256]{2,1,0:T(8,128)(2,1)S(1)} %get-tuple-element.56.gs_ref, bf16[4,256,128]{2,1,0:T(8,128)(2,1)S(1)} %get-tuple-element.47.refs_1_.go_ref, bf16[4,256,128]{2,1,0:T(8,128)(2,1)S(1)} %get-tuple-element.57.q_ref), custom_call_target="tpu_custom_call" | custom-call | flops 603979776 | bytes 2097152 | tf_op jit(solution)/shard_map/kv_keep/pallas_call | solution.py:320
  68.6 0.0 copy-start.3
  68.6 0.0 copy-start.4
  68.6 0.0 copy-start.5
  68.6 0.0 copy-start.6
  68.6 0.0 copy-start.9
  68.6 0.0 copy-start.10
  68.7 0.1 pair_sum.1
  68.8 2.3 %collective-permute-done.16 = bf16[64,256]{1,0:T(8,128)(2,1)S(1)} collective-permute-done((bf16[64,256]{1,0:T(8,128)(2,1)S(1)}, bf16[64,256]{1,0:T(8,128)(2,1)S(1)}, u32[]{:S(2)}, u32[]{:S(2)}) %collective-permute-start.16) | collective-permute-done | bytes 32800 | tf_op jit(solution)/shard_map/ppermute | solution.py:493
  71.1 0.3 fusion
  71.5 0.8 pad_maximum_fusion
  72.3 7.0 %all-to-all-start.1 = ((bf16[64,20,128]{2,1,0:T(8,128)(2,1)}), bf16[64,20,128]{2,1,0:T(8,128)(2,1)S(1)}, u32[]{:S(2)}, u32[]{:S(2)}) async-start(bf16[64,20,128]{2,1,0:T(8,128)(2,1)} %pad_maximum_fusion), calls=%async_computation.1 | async-start | bytes 786432 | tf_op jit(solution)/shard_map/all_to_all | solution.py:509
  79.3 2.3 %collective-permute-start.17 = (bf16[2,256,128]{2,1,0:T(8,128)(2,1)S(1)}, bf16[2,256,128]{2,1,0:T(8,128)(2,1)S(1)}, u32[]{:S(2)}, u32[]{:S(2)}) collective-permute-start(bf16[2,256,128]{2,1,0:T(8,128)(2,1)S(1)} %get-tuple-element.66), channel_id=1, source_target_pairs={{0,12},{4,0},{8,4},{12,8},{16,28},{20,16},{24,20},{28,24},{32,44},... | collective-permute-start | bytes 393224 | tf_op jit(solution)/shard_map/ppermute | solution.py:454
  81.6 0.6 collective-permute-start.18
  82.2 0.6 collective-permute-start.19
  82.8 2.4 %collective-permute-done.17.rest_0_ = bf16[2,256,128]{2,1,0:T(8,128)(2,1)S(1)} collective-permute-done((bf16[2,256,128]{2,1,0:T(8,128)(2,1)S(1)}, bf16[2,256,128]{2,1,0:T(8,128)(2,1)S(1)}, u32[]{:S(2)}, u32[]{:S(2)}) %collective-permute-start.17) | collective-permute-done | bytes 131104 | tf_op jit(solution)/shard_map/ppermute | solution.py:454
  85.1 3.6 %collective-permute-done.18.rest_1_ = bf16[2,256,128]{2,1,0:T(8,128)(2,1)S(1)} collective-permute-done((bf16[2,256,128]{2,1,0:T(8,128)(2,1)S(1)}, bf16[2,256,128]{2,1,0:T(8,128)(2,1)S(1)}, u32[]{:S(2)}, u32[]{:S(2)}) %collective-permute-start.18) | collective-permute-done | bytes 131104 | tf_op jit(solution)/shard_map/ppermute | solution.py:454
  88.7 5.7 %collective-permute-done.19.rest_2_ = bf16[2,256,128]{2,1,0:T(8,128)(2,1)S(1)} collective-permute-done((bf16[2,256,128]{2,1,0:T(8,128)(2,1)S(1)}, bf16[2,256,128]{2,1,0:T(8,128)(2,1)S(1)}, u32[]{:S(2)}, u32[]{:S(2)}) %collective-permute-start.19) | collective-permute-done | bytes 131104 | tf_op jit(solution)/shard_map/ppermute | solution.py:454
  94.5 0.1 row_sum.1
  94.6 4.1 %collective-permute-start.20 = (bf16[256,128]{1,0:T(8,128)(2,1)S(1)}, bf16[256,128]{1,0:T(8,128)(2,1)S(1)}, u32[]{:S(2)}, u32[]{:S(2)}) collective-permute-start(bf16[256,128]{1,0:T(8,128)(2,1)S(1)} %get-tuple-element.69), channel_id=1, source_target_pairs={{0,0},{1,2},{2,1},{3,3},{4,4},{5,6},{6,5},{7,7},{8,8},{9,10},{10,9... | collective-permute-start | bytes 196616 | tf_op jit(solution)/shard_map/ppermute | solution.py:523
  98.7 3.8 %collective-permute-start.21 = (bf16[256,128]{1,0:T(8,128)(2,1)S(1)}, bf16[256,128]{1,0:T(8,128)(2,1)S(1)}, u32[]{:S(2)}, u32[]{:S(2)}) collective-permute-start(bf16[256,128]{1,0:T(8,128)(2,1)S(1)} %get-tuple-element.70), channel_id=1, source_target_pairs={{0,240},{1,242},{2,241},{3,243},{4,244},{5,246},{6,245},{7,247},{8... | collective-permute-start | bytes 196616 | tf_op jit(solution)/shard_map/ppermute | solution.py:523
  102.5 2.7 %collective-permute-start.22 = (bf16[256,128]{1,0:T(8,128)(2,1)S(1)}, bf16[256,128]{1,0:T(8,128)(2,1)S(1)}, u32[]{:S(2)}, u32[]{:S(2)}) collective-permute-start(bf16[256,128]{1,0:T(8,128)(2,1)S(1)} %get-tuple-element.71), channel_id=1, source_target_pairs={{0,224},{1,226},{2,225},{3,227},{4,228},{5,230},{6,229},{7,231},{8... | collective-permute-start | bytes 196616 | tf_op jit(solution)/shard_map/ppermute | solution.py:523
  105.2 0.6 constant_dynamic-slice_fusion.keep_ref
  105.8 3.7 %collective-permute-done.22 = bf16[256,128]{1,0:T(8,128)(2,1)S(1)} collective-permute-done((bf16[256,128]{1,0:T(8,128)(2,1)S(1)}, bf16[256,128]{1,0:T(8,128)(2,1)S(1)}, u32[]{:S(2)}, u32[]{:S(2)}) %collective-permute-start.22) | collective-permute-done | bytes 65568 | tf_op jit(solution)/shard_map/ppermute | solution.py:523
  109.5 0.7 convert_add_fusion
  110.2 1.3 %adam.1 = (f32[16,128]{1,0:T(8,128)}, f32[16,128]{1,0:T(8,128)}, f32[16,128]{1,0:T(8,128)}, f32[4,128]{1,0:T(4,128)}, f32[4,128]{1,0:T(4,128)}, /*index=5*/f32[4,128]{1,0:T(4,128)}) custom-call(bf16[64,20,128]{2,1,0:T(8,128)(2,1)S(1)} %all-to-all-done.1.got_ref, f32[16,128]{1,0:T(8,128)S(1)} %bitcast.29, f32[16,128]{1,0:T(8,128)S(1)} %bitcast.32, ...), custom_call_target="tpu_custom_call" | custom-call | tf_op jit(solution)/shard_map/adam/pallas_call | solution.py:540
  (36 shorter events, 0.2 us)
Async XLA Ops:
  0.6 42.2 %copy-start = (bf16[256,2048]{1,0:T(8,128)(2,1)S(1)}, bf16[256,2048]{1,0:T(8,128)(2,1)}, u32[]{:S(2)}) copy-start(bf16[256,2048]{1,0:T(8,128)(2,1)} %param.16) | copy-start | bytes 3145732
  2.3 40.5 %all-to-all-start = ((bf16[64,20,128]{2,1,0:T(8,128)(2,1)}), bf16[64,20,128]{2,1,0:T(8,128)(2,1)S(1)}, u32[]{:S(2)}, u32[]{:S(2)}) async-start(bf16[64,20,128]{2,1,0:T(8,128)(2,1)} %spread.1), calls=%async_computation | async-start | bytes 786432 | tf_op jit(solution)/shard_map/all_to_all | solution.py:463
  16.8 10.9 %collective-permute-start = (bf16[256,128]{1,0:T(8,128)(2,1)S(1)}, bf16[256,128]{1,0:T(8,128)(2,1)S(1)}, u32[]{:S(2)}, u32[]{:S(2)}) collective-permute-start(bf16[256,128]{1,0:T(8,128)(2,1)S(1)} %get-tuple-element.83.own_ref), channel_id=1, source_target_pairs={{0,16},{4,20},{8,24},{12,28},{16,32},{20,36},{24,40},{28,44},{32,4... | collective-permute-start | bytes 196616 | tf_op jit(solution)/shard_map/ppermute | solution.py:450
  17.9 14.0 %collective-permute-start.1 = (bf16[256,128]{1,0:T(8,128)(2,1)S(1)}, bf16[256,128]{1,0:T(8,128)(2,1)S(1)}, u32[]{:S(2)}, u32[]{:S(2)}) collective-permute-start(bf16[256,128]{1,0:T(8,128)(2,1)S(1)} %get-tuple-element.83.own_ref), channel_id=1, source_target_pairs={{0,32},{4,36},{8,40},{12,44},{16,48},{20,52},{24,56},{28,60},{32,6... | collective-permute-start | bytes 196616 | tf_op jit(solution)/shard_map/ppermute | solution.py:450
  32.0 7.5 %collective-permute-start.2 = (bf16[2,256,128]{2,1,0:T(8,128)(2,1)S(1)}, bf16[2,256,128]{2,1,0:T(8,128)(2,1)S(1)}, u32[]{:S(2)}, u32[]{:S(2)}) collective-permute-start(bf16[2,256,128]{2,1,0:T(8,128)(2,1)S(1)} %get-tuple-element.50), channel_id=1, source_target_pairs={{0,4},{4,8},{8,12},{12,0},{16,20},{20,24},{24,28},{28,16},{32,36},... | collective-permute-start | bytes 393224 | tf_op jit(solution)/shard_map/ppermute | solution.py:454
  33.0 8.3 %collective-permute-start.3 = (bf16[2,256,128]{2,1,0:T(8,128)(2,1)S(1)}, bf16[2,256,128]{2,1,0:T(8,128)(2,1)S(1)}, u32[]{:S(2)}, u32[]{:S(2)}) collective-permute-start(bf16[2,256,128]{2,1,0:T(8,128)(2,1)S(1)} %get-tuple-element.51), channel_id=1, source_target_pairs={{0,8},{4,12},{8,0},{12,4},{16,24},{20,28},{24,16},{28,20},{32,40},... | collective-permute-start | bytes 393224 | tf_op jit(solution)/shard_map/ppermute | solution.py:454
  35.4 7.3 %collective-permute-start.4 = (bf16[2,256,128]{2,1,0:T(8,128)(2,1)S(1)}, bf16[2,256,128]{2,1,0:T(8,128)(2,1)S(1)}, u32[]{:S(2)}, u32[]{:S(2)}) collective-permute-start(bf16[2,256,128]{2,1,0:T(8,128)(2,1)S(1)} %get-tuple-element.52), channel_id=1, source_target_pairs={{0,12},{4,0},{8,4},{12,8},{16,28},{20,16},{24,20},{28,24},{32,44},... | collective-permute-start | bytes 393224 | tf_op jit(solution)/shard_map/ppermute | solution.py:454
  36.5 6.7 %collective-permute-start.5 = (bf16[256,128]{1,0:T(8,128)(2,1)S(1)}, bf16[256,128]{1,0:T(8,128)(2,1)S(1)}, u32[]{:S(2)}, u32[]{:S(2)}) collective-permute-start(bf16[256,128]{1,0:T(8,128)(2,1)S(1)} %collective-permute-done.one_ref.refs_7_), channel_id=1, source_target_pairs={{0,1},{1,0},{2,3},{3,2},{4,5},{5,4},{6,7},{7,6},{8,9},{9,8},{10,11... | collective-permute-start | bytes 196616 | tf_op jit(solution)/shard_map/ppermute | solution.py:468
  39.4 4.4 %collective-permute-start.6 = (bf16[256,128]{1,0:T(8,128)(2,1)S(1)}, bf16[256,128]{1,0:T(8,128)(2,1)S(1)}, u32[]{:S(2)}, u32[]{:S(2)}) collective-permute-start(bf16[256,128]{1,0:T(8,128)(2,1)S(1)} %collective-permute-done.1.two_ref.refs_8_), channel_id=1, source_target_pairs={{0,1},{1,0},{2,3},{3,2},{4,5},{5,4},{6,7},{7,6},{8,9},{9,8},{10,11... | collective-permute-start | bytes 196616 | tf_op jit(solution)/shard_map/ppermute | solution.py:468
  39.4 6.8 %collective-permute-start.7 = (bf16[2,256,128]{2,1,0:T(8,128)(2,1)S(1)}, bf16[2,256,128]{2,1,0:T(8,128)(2,1)S(1)}, u32[]{:S(2)}, u32[]{:S(2)}) collective-permute-start(bf16[2,256,128]{2,1,0:T(8,128)(2,1)S(1)} %collective-permute-done.2.refs_9_), channel_id=1, source_target_pairs={{0,1},{1,0},{2,3},{3,2},{4,5},{5,4},{6,7},{7,6},{8,9},{9,8},{10,11... | collective-permute-start | bytes 393224 | tf_op jit(solution)/shard_map/ppermute | solution.py:468
  41.3 10.4 %collective-permute-start.8 = (bf16[2,256,128]{2,1,0:T(8,128)(2,1)S(1)}, bf16[2,256,128]{2,1,0:T(8,128)(2,1)S(1)}, u32[]{:S(2)}, u32[]{:S(2)}) collective-permute-start(bf16[2,256,128]{2,1,0:T(8,128)(2,1)S(1)} %collective-permute-done.3.refs_10_), channel_id=1, source_target_pairs={{0,1},{1,0},{2,3},{3,2},{4,5},{5,4},{6,7},{7,6},{8,9},{9,8},{10,11... | collective-permute-start | bytes 393224 | tf_op jit(solution)/shard_map/ppermute | solution.py:468
  42.7 9.0 %collective-permute-start.9 = (bf16[2,256,128]{2,1,0:T(8,128)(2,1)S(1)}, bf16[2,256,128]{2,1,0:T(8,128)(2,1)S(1)}, u32[]{:S(2)}, u32[]{:S(2)}) collective-permute-start(bf16[2,256,128]{2,1,0:T(8,128)(2,1)S(1)} %collective-permute-done.4.refs_11_), channel_id=1, source_target_pairs={{0,1},{1,0},{2,3},{3,2},{4,5},{5,4},{6,7},{7,6},{8,9},{9,8},{10,11... | collective-permute-start | bytes 393224 | tf_op jit(solution)/shard_map/ppermute | solution.py:468
  43.3 8.4 %collective-permute-start.10 = (bf16[64,256]{1,0:T(8,128)(2,1)S(1)}, bf16[64,256]{1,0:T(8,128)(2,1)S(1)}, u32[]{:S(2)}, u32[]{:S(2)}) collective-permute-start(bf16[64,256]{1,0:T(8,128)(2,1)S(1)} %convolution_convert_fusion.1.refs_17_), channel_id=1, source_target_pairs={{0,1},{1,0},{2,3},{3,2},{4,5},{5,4},{6,7},{7,6},{8,9},{9,8},{10,11... | collective-permute-start | bytes 98312 | tf_op jit(solution)/shard_map/ppermute | solution.py:475
  43.8 7.9 %collective-permute-start.11 = (bf16[64,256]{1,0:T(8,128)(2,1)S(1)}, bf16[64,256]{1,0:T(8,128)(2,1)S(1)}, u32[]{:S(2)}, u32[]{:S(2)}) collective-permute-start(bf16[64,256]{1,0:T(8,128)(2,1)S(1)} %convolution_convert_fusion.1.refs_17_), channel_id=1, source_target_pairs={{0,2},{1,3},{2,0},{3,1},{4,6},{5,7},{6,4},{7,5},{8,10},{9,11},{10,... | collective-permute-start | bytes 98312 | tf_op jit(solution)/shard_map/ppermute | solution.py:475
  46.2 5.5 %collective-permute-start.12 = (bf16[64,256]{1,0:T(8,128)(2,1)S(1)}, bf16[64,256]{1,0:T(8,128)(2,1)S(1)}, u32[]{:S(2)}, u32[]{:S(2)}) collective-permute-start(bf16[64,256]{1,0:T(8,128)(2,1)S(1)} %convolution_convert_fusion.1.refs_17_), channel_id=1, source_target_pairs={{0,3},{1,2},{2,1},{3,0},{4,7},{5,6},{6,5},{7,4},{8,11},{9,10},{10,... | collective-permute-start | bytes 98312 | tf_op jit(solution)/shard_map/ppermute | solution.py:475
  47.0 0.9 copy-start.1
  48.0 0.9 copy-start.2
  49.0 0.7 copy-start.7
  49.7 0.7 copy-start.11
  50.4 0.7 copy-start.12
  61.5 1.7 %copy-start.8 = (s32[2,64]{1,0:T(2,128)S(1)}, s32[2,64]{1,0:T(2,128)}, u32[]{:S(2)}) copy-start(s32[2,64]{1,0:T(2,128)} %mask_ref.1) | copy-start | bytes 1540
  62.9 5.8 %collective-permute-start.13 = (bf16[2304,128]{1,0:T(8,128)(2,1)S(1)}, bf16[2304,128]{1,0:T(8,128)(2,1)S(1)}, u32[]{:S(2)}, u32[]{:S(2)}) collective-permute-start(bf16[2304,128]{1,0:T(8,128)(2,1)S(1)} %kv_send.1), channel_id=1, source_target_pairs={{0,1},{1,0},{2,3},{3,2},{4,5},{5,4},{6,7},{7,6},{8,9},{9,8},{10,11... | collective-permute-start | bytes 1769480 | tf_op jit(solution)/shard_map/ppermute | solution.py:495
  63.2 5.6 %collective-permute-start.14 = (bf16[64,256]{1,0:T(8,128)(2,1)S(1)}, bf16[64,256]{1,0:T(8,128)(2,1)S(1)}, u32[]{:S(2)}, u32[]{:S(2)}) collective-permute-start(bf16[64,256]{1,0:T(8,128)(2,1)S(1)} %get-tuple-element.72), channel_id=1, source_target_pairs={{0,1},{1,0},{2,3},{3,2},{4,5},{5,4},{6,7},{7,6},{8,9},{9,8},{10,11... | collective-permute-start | bytes 98312 | tf_op jit(solution)/shard_map/ppermute | solution.py:493
  63.6 5.2 %collective-permute-start.15 = (bf16[64,256]{1,0:T(8,128)(2,1)S(1)}, bf16[64,256]{1,0:T(8,128)(2,1)S(1)}, u32[]{:S(2)}, u32[]{:S(2)}) collective-permute-start(bf16[64,256]{1,0:T(8,128)(2,1)S(1)} %get-tuple-element.72), channel_id=1, source_target_pairs={{0,2},{1,3},{2,0},{3,1},{4,6},{5,7},{6,4},{7,5},{8,10},{9,11},{10,... | collective-permute-start | bytes 98312 | tf_op jit(solution)/shard_map/ppermute | solution.py:493
  66.0 5.0 %collective-permute-start.16 = (bf16[64,256]{1,0:T(8,128)(2,1)S(1)}, bf16[64,256]{1,0:T(8,128)(2,1)S(1)}, u32[]{:S(2)}, u32[]{:S(2)}) collective-permute-start(bf16[64,256]{1,0:T(8,128)(2,1)S(1)} %get-tuple-element.72), channel_id=1, source_target_pairs={{0,3},{1,2},{2,1},{3,0},{4,7},{5,6},{6,5},{7,4},{8,11},{9,10},{10,... | collective-permute-start | bytes 98312 | tf_op jit(solution)/shard_map/ppermute | solution.py:493
  68.6 41.6 %copy-start.3 = (f32[1,2048]{1,0:T(1,128)S(1)}, f32[1,2048]{1,0:T(1,128)}, u32[]{:S(2)}) copy-start(f32[1,2048]{1,0:T(1,128)} %param.17) | copy-start | bytes 24580
  68.6 41.6 %copy-start.4 = (f32[1,512]{1,0:T(1,128)S(1)}, f32[1,512]{1,0:T(1,128)}, u32[]{:S(2)}) copy-start(f32[1,512]{1,0:T(1,128)} %param.20) | copy-start | bytes 6148
  68.6 41.6 %copy-start.5 = (f32[1,2048]{1,0:T(1,128)S(1)}, f32[1,2048]{1,0:T(1,128)}, u32[]{:S(2)}) copy-start(f32[1,2048]{1,0:T(1,128)} %param.18) | copy-start | bytes 24580
  68.6 41.6 %copy-start.6 = (f32[1,2048]{1,0:T(1,128)S(1)}, f32[1,2048]{1,0:T(1,128)}, u32[]{:S(2)}) copy-start(f32[1,2048]{1,0:T(1,128)} %param.19) | copy-start | bytes 24580
  68.6 41.6 %copy-start.9 = (f32[1,512]{1,0:T(1,128)S(1)}, f32[1,512]{1,0:T(1,128)}, u32[]{:S(2)}) copy-start(f32[1,512]{1,0:T(1,128)} %param.21) | copy-start | bytes 6148
  68.6 41.6 %copy-start.10 = (f32[1,512]{1,0:T(1,128)S(1)}, f32[1,512]{1,0:T(1,128)}, u32[]{:S(2)}) copy-start(f32[1,512]{1,0:T(1,128)} %param.22) | copy-start | bytes 6148
  72.3 37.9 %all-to-all-start.1 = ((bf16[64,20,128]{2,1,0:T(8,128)(2,1)}), bf16[64,20,128]{2,1,0:T(8,128)(2,1)S(1)}, u32[]{:S(2)}, u32[]{:S(2)}) async-start(bf16[64,20,128]{2,1,0:T(8,128)(2,1)} %pad_maximum_fusion), calls=%async_computation.1 | async-start | bytes 786432 | tf_op jit(solution)/shard_map/all_to_all | solution.py:509
  79.3 5.8 %collective-permute-start.17 = (bf16[2,256,128]{2,1,0:T(8,128)(2,1)S(1)}, bf16[2,256,128]{2,1,0:T(8,128)(2,1)S(1)}, u32[]{:S(2)}, u32[]{:S(2)}) collective-permute-start(bf16[2,256,128]{2,1,0:T(8,128)(2,1)S(1)} %get-tuple-element.66), channel_id=1, source_target_pairs={{0,12},{4,0},{8,4},{12,8},{16,28},{20,16},{24,20},{28,24},{32,44},... | collective-permute-start | bytes 393224 | tf_op jit(solution)/shard_map/ppermute | solution.py:454
  81.6 7.1 %collective-permute-start.18 = (bf16[2,256,128]{2,1,0:T(8,128)(2,1)S(1)}, bf16[2,256,128]{2,1,0:T(8,128)(2,1)S(1)}, u32[]{:S(2)}, u32[]{:S(2)}) collective-permute-start(bf16[2,256,128]{2,1,0:T(8,128)(2,1)S(1)} %get-tuple-element.67), channel_id=1, source_target_pairs={{0,8},{4,12},{8,0},{12,4},{16,24},{20,28},{24,16},{28,20},{32,40},... | collective-permute-start | bytes 393224 | tf_op jit(solution)/shard_map/ppermute | solution.py:454
  82.2 12.3 %collective-permute-start.19 = (bf16[2,256,128]{2,1,0:T(8,128)(2,1)S(1)}, bf16[2,256,128]{2,1,0:T(8,128)(2,1)S(1)}, u32[]{:S(2)}, u32[]{:S(2)}) collective-permute-start(bf16[2,256,128]{2,1,0:T(8,128)(2,1)S(1)} %get-tuple-element.68), channel_id=1, source_target_pairs={{0,4},{4,8},{8,12},{12,0},{16,20},{20,24},{24,28},{28,16},{32,36},... | collective-permute-start | bytes 393224 | tf_op jit(solution)/shard_map/ppermute | solution.py:454
  94.6 11.2 %collective-permute-start.20 = (bf16[256,128]{1,0:T(8,128)(2,1)S(1)}, bf16[256,128]{1,0:T(8,128)(2,1)S(1)}, u32[]{:S(2)}, u32[]{:S(2)}) collective-permute-start(bf16[256,128]{1,0:T(8,128)(2,1)S(1)} %get-tuple-element.69), channel_id=1, source_target_pairs={{0,0},{1,2},{2,1},{3,3},{4,4},{5,6},{6,5},{7,7},{8,8},{9,10},{10,9... | collective-permute-start | bytes 196616 | tf_op jit(solution)/shard_map/ppermute | solution.py:523
  98.7 7.2 %collective-permute-start.21 = (bf16[256,128]{1,0:T(8,128)(2,1)S(1)}, bf16[256,128]{1,0:T(8,128)(2,1)S(1)}, u32[]{:S(2)}, u32[]{:S(2)}) collective-permute-start(bf16[256,128]{1,0:T(8,128)(2,1)S(1)} %get-tuple-element.70), channel_id=1, source_target_pairs={{0,240},{1,242},{2,241},{3,243},{4,244},{5,246},{6,245},{7,247},{8... | collective-permute-start | bytes 196616 | tf_op jit(solution)/shard_map/ppermute | solution.py:523
  102.5 7.0 %collective-permute-start.22 = (bf16[256,128]{1,0:T(8,128)(2,1)S(1)}, bf16[256,128]{1,0:T(8,128)(2,1)S(1)}, u32[]{:S(2)}, u32[]{:S(2)}) collective-permute-start(bf16[256,128]{1,0:T(8,128)(2,1)S(1)} %get-tuple-element.71), channel_id=1, source_target_pairs={{0,224},{1,226},{2,225},{3,227},{4,228},{5,230},{6,229},{7,231},{8... | collective-permute-start | bytes 196616 | tf_op jit(solution)/shard_map/ppermute | solution.py:523

commit v6 on v5

--- a/solution.py
+++ b/solution.py
@@ -462,7 +462,8 @@
     row = spread(row, ctx)
     gathered = lax.all_to_all(row, "ctx", split_axis=0, concat_axis=0)
     packs = pack(mine, one, two)
-    direct = [one, two] + [across(p, n + 1) for n, p in enumerate(packs)]
+    far = across(packs[1], 2)
+    direct = [one, two, across(packs[0], 1), far, across(packs[2], 3)]
     queries_in, grads_in = stage(frozen_queries, output_gradient)
     masks_in, low = bounds(group_length, group_shift, rank_keep_mask, tokens, tokens * ctx)
     swapped = [lax.ppermute(piece, "head", swap) for piece in direct]
@@ -471,7 +472,7 @@
     up = gathered[:, down_rows:].reshape(ranks, width)
 
     part = dot32(down, inputs, NT).astype(jnp.bfloat16)
-    others = [[(h, h ^ k) for h in range(head_count)] for k in range(1, head_count)]
+    others = [[(h, h ^ k) for h in range(head_count)] for k in range(head_count - 1, 0, -1)]
     parts = [part] + [lax.ppermute(part, "head", pairs) for pairs in others]
 
     keep_masks = rank_keep_mask.astype(jnp.float32)[:, :, None]
@@ -523,7 +524,7 @@
         piece = lax.ppermute(piece, ("ctx", "head"), pairs)
         return piece.astype(jnp.float32)
 
-    kv_grad = home(own_sum, 0) + home(one_sum, COLUMNS) + home(two_sum, 2 * COLUMNS)
+    kv_grad = home(two_sum, 2 * COLUMNS) + home(one_sum, COLUMNS) + home(own_sum, 0)
 
     keep_row = lax.dynamic_slice_in_dim(keep_masks[1], ctx_place, 1, 0)
     small = [

time: 112 us -> 110 us (0.982)
  transfers between devices with their start and end apart: 25 -> 25, of which waited for: 7 -> 8; matrix products, arithmetic and copies ran while one was open for 2% -> 2% of each run, Pallas kernels for 2% -> 2%
where the time goes in v6:
time: 110 us
  starting transfers between devices  55.8 us (51%)
  waiting for transfers between devices  28.6 us (26%)
  Pallas kernels  15.9 us (14%)
  local copies, waits for them, and re-layouts  5.59 us (5%)
  other arithmetic  2.28 us (2%)
    all_to_all x1, starting transfers between devices, on_device(): gathered = lax.all_to_all(row, 'ctx', split_axis=0, concat_axis=0)  13.6 us
    ppermute x2, waiting for transfers between devices, along(): lax.ppermute(piece, 'ctx', [(i, (i + step) % ctx) for i in range(ctx)])  11.9 us
    ppermute x6, waiting for transfers between devices, across(): return lax.ppermute(piece, 'ctx', pairs)  11.8 us
    ppermute x3, starting transfers between devices, home(): piece = lax.ppermute(piece, ('ctx', 'head'), pairs)  9.83 us
    pallas_call x1, Pallas kernels, attention(): pl.pallas_call(functools.partial(attention_kernel, tokens=tokens, heads=h...  9.78 us
    ppermute x6, starting transfers between devices, across(): return lax.ppermute(piece, 'ctx', pairs)  8.01 us
    all_to_all x1, starting transfers between devices, on_device(): received = lax.all_to_all(packed, 'ctx', split_axis=0, concat_axis=0)  7.21 us
    ppermute x5, starting transfers between devices, on_device(): swapped = [lax.ppermute(piece, 'head', swap) for piece in direct]  6.24 us
  transfers between devices with their start and end apart: 25, of which 8 were waited for; matrix products, arithmetic and copies ran while one was open for 2% of the time, Pallas kernels for 2%

profile of v6, /device:TPU:1, one launch (start us, length us, event | category | flops | bytes accessed | tf_op | source)
XLA Modules:
  0.0 109.9 jit_solution(4092582968031311270)
XLA Ops:
  0.6 0.0 copy-start
  0.7 0.8 pad_maximum_fusion.1.row_ref
  1.5 0.8 spread.1
  2.3 13.6 %all-to-all-start = ((bf16[64,20,128]{2,1,0:T(8,128)(2,1)}), bf16[64,20,128]{2,1,0:T(8,128)(2,1)S(1)}, u32[]{:S(2)}, u32[]{:S(2)}) async-start(bf16[64,20,128]{2,1,0:T(8,128)(2,1)} %spread.1), calls=%async_computation | async-start | bytes 786432 | tf_op jit(solution)/shard_map/all_to_all | solution.py:463
  15.9 0.9 constant_dynamic-slice_fusion.1
  16.8 1.1 collective-permute-start
  17.9 2.1 %collective-permute-start.1 = (bf16[256,128]{1,0:T(8,128)(2,1)S(1)}, bf16[256,128]{1,0:T(8,128)(2,1)S(1)}, u32[]{:S(2)}, u32[]{:S(2)}) collective-permute-start(bf16[256,128]{1,0:T(8,128)(2,1)S(1)} %get-tuple-element.83.own_ref), channel_id=1, source_target_pairs={{0,32},{4,36},{8,40},{12,44},{16,48},{20,52},{24,56},{28,60},{32,6... | collective-permute-start | bytes 196616 | tf_op jit(solution)/shard_map/ppermute | solution.py:450
  20.0 7.8 %collective-permute-done.one_ref.refs_7_ = bf16[256,128]{1,0:T(8,128)(2,1)S(1)} collective-permute-done((bf16[256,128]{1,0:T(8,128)(2,1)S(1)}, bf16[256,128]{1,0:T(8,128)(2,1)S(1)}, u32[]{:S(2)}, u32[]{:S(2)}) %collective-permute-start) | collective-permute-done | bytes 65568 | tf_op jit(solution)/shard_map/ppermute | solution.py:450
  27.8 4.2 %collective-permute-done.1.two_ref.refs_8_ = bf16[256,128]{1,0:T(8,128)(2,1)S(1)} collective-permute-done((bf16[256,128]{1,0:T(8,128)(2,1)S(1)}, bf16[256,128]{1,0:T(8,128)(2,1)S(1)}, u32[]{:S(2)}, u32[]{:S(2)}) %collective-permute-start.1) | collective-permute-done | bytes 65568 | tf_op jit(solution)/shard_map/ppermute | solution.py:450
  32.0 1.0 collective-permute-start.2
  33.0 2.5 %collective-permute-start.3 = (bf16[2,256,128]{2,1,0:T(8,128)(2,1)S(1)}, bf16[2,256,128]{2,1,0:T(8,128)(2,1)S(1)}, u32[]{:S(2)}, u32[]{:S(2)}) collective-permute-start(bf16[2,256,128]{2,1,0:T(8,128)(2,1)S(1)} %get-tuple-element.51), channel_id=1, source_target_pairs={{0,8},{4,12},{8,0},{12,4},{16,24},{20,28},{24,16},{28,20},{32,40},... | collective-permute-start | bytes 393224 | tf_op jit(solution)/shard_map/ppermute | solution.py:454
  35.4 1.1 collective-permute-start.4
  36.5 2.9 %collective-permute-start.5 = (bf16[256,128]{1,0:T(8,128)(2,1)S(1)}, bf16[256,128]{1,0:T(8,128)(2,1)S(1)}, u32[]{:S(2)}, u32[]{:S(2)}) collective-permute-start(bf16[256,128]{1,0:T(8,128)(2,1)S(1)} %collective-permute-done.one_ref.refs_7_), channel_id=1, source_target_pairs={{0,1},{1,0},{2,3},{3,2},{4,5},{5,4},{6,7},{7,6},{8,9},{9,8},{10,11... | collective-permute-start | bytes 196616 | tf_op jit(solution)/shard_map/ppermute | solution.py:469
  39.4 0.0 collective-permute-start.6
  39.4 0.0 collective-permute-done.2.refs_9_
  39.4 1.9 %collective-permute-start.7 = (bf16[2,256,128]{2,1,0:T(8,128)(2,1)S(1)}, bf16[2,256,128]{2,1,0:T(8,128)(2,1)S(1)}, u32[]{:S(2)}, u32[]{:S(2)}) collective-permute-start(bf16[2,256,128]{2,1,0:T(8,128)(2,1)S(1)} %collective-permute-done.2.refs_9_), channel_id=1, source_target_pairs={{0,1},{1,0},{2,3},{3,2},{4,5},{5,4},{6,7},{7,6},{8,9},{9,8},{10,11... | collective-permute-start | bytes 393224 | tf_op jit(solution)/shard_map/ppermute | solution.py:469
  41.3 1.4 %collective-permute-start.8 = (bf16[2,256,128]{2,1,0:T(8,128)(2,1)S(1)}, bf16[2,256,128]{2,1,0:T(8,128)(2,1)S(1)}, u32[]{:S(2)}, u32[]{:S(2)}) collective-permute-start(bf16[2,256,128]{2,1,0:T(8,128)(2,1)S(1)} %collective-permute-done.3.refs_10_), channel_id=1, source_target_pairs={{0,1},{1,0},{2,3},{3,2},{4,5},{5,4},{6,7},{7,6},{8,9},{9,8},{10,11... | collective-permute-start | bytes 393224 | tf_op jit(solution)/shard_map/ppermute | solution.py:469
  42.7 0.0 collective-permute-done.4.refs_11_
  42.7 0.1 collective-permute-start.9
  42.8 0.4 convolution_convert_fusion.1.refs_17_
  43.3 2.9 %collective-permute-start.10 = (bf16[64,256]{1,0:T(8,128)(2,1)S(1)}, bf16[64,256]{1,0:T(8,128)(2,1)S(1)}, u32[]{:S(2)}, u32[]{:S(2)}) collective-permute-start(bf16[64,256]{1,0:T(8,128)(2,1)S(1)} %convolution_convert_fusion.1.refs_17_), channel_id=1, source_target_pairs={{0,3},{1,2},{2,1},{3,0},{4,7},{5,6},{6,5},{7,4},{8,11},{9,10},{10,... | collective-permute-start | bytes 98312 | tf_op jit(solution)/shard_map/ppermute | solution.py:476
  46.1 0.5 collective-permute-start.11
  46.7 0.4 collective-permute-start.12
  47.0 0.9 copy-done.1
  48.0 0.9 copy-done.2
  48.9 0.1 stage.1
  49.0 0.0 copy-start.7
  49.0 0.7 copy-done.7
  49.7 0.7 copy-done.11
  50.4 0.7 copy-done.12
  51.0 0.6 bounds.1
  51.7 9.8 %attention.1 = (bf16[256,512]{1,0:T(8,128)(2,1)}, bf16[256,512]{1,0:T(8,128)(2,1)}, bf16[64,256]{1,0:T(8,128)(2,1)S(1)}, bf16[64,512]{1,0:T(8,128)(2,1)S(1)}, bf...) custom-call(bf16[4,256,128]{2,1,0:T(8,128)(2,1)S(1)} %get-tuple-element.46.refs_, ...), custom_call_target="tpu_custom_call" | custom-call | flops 2415919104 | bytes 8388608 | tf_op jit(solution)/shard_map/attention/pallas_call | solution.py:257
  61.5 1.4 %kv_send.1 = bf16[2304,128]{1,0:T(8,128)(2,1)S(1)} custom-call(bf16[4,2304,256]{2,1,0:T(8,128)(2,1)S(1)} %get-tuple-element.55.w_ref, bf16[4,2304,256]{2,1,0:T(8,128)(2,1)S(1)} %get-tuple-element.56.gs_ref, bf16[4,256,128]{2,1,0:T(8,128)(2,1)S(1)} %get-tuple-element.47.refs_1_.go_ref, bf16[4,256,128]{2,1,0:T(8,128)(2,1)S(1)} %get-tuple-element.57.q_ref), custom_call_target="tpu_custom_call" | custom-call | flops 603979776 | bytes 2097152 | tf_op jit(solution)/shard_map/kv_send/pallas_call | solution.py:320
  62.9 0.3 collective-permute-start.13
  63.2 2.7 %collective-permute-start.14 = (bf16[64,256]{1,0:T(8,128)(2,1)S(1)}, bf16[64,256]{1,0:T(8,128)(2,1)S(1)}, u32[]{:S(2)}, u32[]{:S(2)}) collective-permute-start(bf16[64,256]{1,0:T(8,128)(2,1)S(1)} %get-tuple-element.72), channel_id=1, source_target_pairs={{0,3},{1,2},{2,1},{3,0},{4,7},{5,6},{6,5},{7,4},{8,11},{9,10},{10,... | collective-permute-start | bytes 98312 | tf_op jit(solution)/shard_map/ppermute | solution.py:494
  65.9 0.5 collective-permute-start.15
  66.4 0.5 collective-permute-start.16
  66.9 1.7 %kv_keep.1.keep_ref = f32[2304,128]{1,0:T(8,128)S(1)} custom-call(bf16[4,2304,256]{2,1,0:T(8,128)(2,1)S(1)} %get-tuple-element.55.w_ref, bf16[4,2304,256]{2,1,0:T(8,128)(2,1)S(1)} %get-tuple-element.56.gs_ref, bf16[4,256,128]{2,1,0:T(8,128)(2,1)S(1)} %get-tuple-element.47.refs_1_.go_ref, bf16[4,256,128]{2,1,0:T(8,128)(2,1)S(1)} %get-tuple-element.57.q_ref), custom_call_target="tpu_custom_call" | custom-call | flops 603979776 | bytes 2097152 | tf_op jit(solution)/shard_map/kv_keep/pallas_call | solution.py:320
  68.6 0.0 copy-start.3
  68.6 0.0 copy-start.4
  68.6 0.0 copy-start.5
  68.6 0.0 copy-start.6
  68.6 0.0 copy-start.9
  68.6 0.0 copy-start.10
  68.7 0.1 pair_sum.1
  68.8 1.4 %collective-permute-done.15 = bf16[64,256]{1,0:T(8,128)(2,1)S(1)} collective-permute-done((bf16[64,256]{1,0:T(8,128)(2,1)S(1)}, bf16[64,256]{1,0:T(8,128)(2,1)S(1)}, u32[]{:S(2)}, u32[]{:S(2)}) %collective-permute-start.15) | collective-permute-done | bytes 32800 | tf_op jit(solution)/shard_map/ppermute | solution.py:494
  70.2 0.3 fusion
  70.6 0.8 pad_maximum_fusion
  71.4 7.2 %all-to-all-start.1 = ((bf16[64,20,128]{2,1,0:T(8,128)(2,1)}), bf16[64,20,128]{2,1,0:T(8,128)(2,1)S(1)}, u32[]{:S(2)}, u32[]{:S(2)}) async-start(bf16[64,20,128]{2,1,0:T(8,128)(2,1)} %pad_maximum_fusion), calls=%async_computation.1 | async-start | bytes 786432 | tf_op jit(solution)/shard_map/all_to_all | solution.py:510
  78.6 2.3 %collective-permute-start.17 = (bf16[2,256,128]{2,1,0:T(8,128)(2,1)S(1)}, bf16[2,256,128]{2,1,0:T(8,128)(2,1)S(1)}, u32[]{:S(2)}, u32[]{:S(2)}) collective-permute-start(bf16[2,256,128]{2,1,0:T(8,128)(2,1)S(1)} %get-tuple-element.66), channel_id=1, source_target_pairs={{0,12},{4,0},{8,4},{12,8},{16,28},{20,16},{24,20},{28,24},{32,44},... | collective-permute-start | bytes 393224 | tf_op jit(solution)/shard_map/ppermute | solution.py:454
  80.9 0.6 collective-permute-start.18
  81.5 0.6 collective-permute-start.19
  82.0 3.4 %collective-permute-done.17.rest_0_ = bf16[2,256,128]{2,1,0:T(8,128)(2,1)S(1)} collective-permute-done((bf16[2,256,128]{2,1,0:T(8,128)(2,1)S(1)}, bf16[2,256,128]{2,1,0:T(8,128)(2,1)S(1)}, u32[]{:S(2)}, u32[]{:S(2)}) %collective-permute-start.17) | collective-permute-done | bytes 131104 | tf_op jit(solution)/shard_map/ppermute | solution.py:454
  85.5 2.0 %collective-permute-done.18.rest_1_ = bf16[2,256,128]{2,1,0:T(8,128)(2,1)S(1)} collective-permute-done((bf16[2,256,128]{2,1,0:T(8,128)(2,1)S(1)}, bf16[2,256,128]{2,1,0:T(8,128)(2,1)S(1)}, u32[]{:S(2)}, u32[]{:S(2)}) %collective-permute-start.18) | collective-permute-done | bytes 131104 | tf_op jit(solution)/shard_map/ppermute | solution.py:454
  87.4 6.4 %collective-permute-done.19.rest_2_ = bf16[2,256,128]{2,1,0:T(8,128)(2,1)S(1)} collective-permute-done((bf16[2,256,128]{2,1,0:T(8,128)(2,1)S(1)}, bf16[2,256,128]{2,1,0:T(8,128)(2,1)S(1)}, u32[]{:S(2)}, u32[]{:S(2)}) %collective-permute-start.19) | collective-permute-done | bytes 131104 | tf_op jit(solution)/shard_map/ppermute | solution.py:454
  93.9 0.1 row_sum.1
  94.0 4.6 %collective-permute-start.20 = (bf16[256,128]{1,0:T(8,128)(2,1)S(1)}, bf16[256,128]{1,0:T(8,128)(2,1)S(1)}, u32[]{:S(2)}, u32[]{:S(2)}) collective-permute-start(bf16[256,128]{1,0:T(8,128)(2,1)S(1)} %get-tuple-element.69), channel_id=1, source_target_pairs={{0,224},{1,226},{2,225},{3,227},{4,228},{5,230},{6,229},{7,231},{8... | collective-permute-start | bytes 196616 | tf_op jit(solution)/shard_map/ppermute | solution.py:524
  98.6 2.2 %collective-permute-start.21 = (bf16[256,128]{1,0:T(8,128)(2,1)S(1)}, bf16[256,128]{1,0:T(8,128)(2,1)S(1)}, u32[]{:S(2)}, u32[]{:S(2)}) collective-permute-start(bf16[256,128]{1,0:T(8,128)(2,1)S(1)} %get-tuple-element.70), channel_id=1, source_target_pairs={{0,240},{1,242},{2,241},{3,243},{4,244},{5,246},{6,245},{7,247},{8... | collective-permute-start | bytes 196616 | tf_op jit(solution)/shard_map/ppermute | solution.py:524
  100.7 3.1 %collective-permute-start.22 = (bf16[256,128]{1,0:T(8,128)(2,1)S(1)}, bf16[256,128]{1,0:T(8,128)(2,1)S(1)}, u32[]{:S(2)}, u32[]{:S(2)}) collective-permute-start(bf16[256,128]{1,0:T(8,128)(2,1)S(1)} %get-tuple-element.71), channel_id=1, source_target_pairs={{0,0},{1,2},{2,1},{3,3},{4,4},{5,6},{6,5},{7,7},{8,8},{9,10},{10,9... | collective-permute-start | bytes 196616 | tf_op jit(solution)/shard_map/ppermute | solution.py:524
  103.8 0.6 constant_dynamic-slice_fusion.keep_ref
  104.4 0.2 collective-permute-done.21
  104.7 3.1 %collective-permute-done.22 = bf16[256,128]{1,0:T(8,128)(2,1)S(1)} collective-permute-done((bf16[256,128]{1,0:T(8,128)(2,1)S(1)}, bf16[256,128]{1,0:T(8,128)(2,1)S(1)}, u32[]{:S(2)}, u32[]{:S(2)}) %collective-permute-start.22) | collective-permute-done | bytes 65568 | tf_op jit(solution)/shard_map/ppermute | solution.py:524
  107.8 0.7 convert_add_fusion
  108.5 1.3 %adam.1 = (f32[16,128]{1,0:T(8,128)}, f32[16,128]{1,0:T(8,128)}, f32[16,128]{1,0:T(8,128)}, f32[4,128]{1,0:T(4,128)}, f32[4,128]{1,0:T(4,128)}, /*index=5*/f32[4,128]{1,0:T(4,128)}) custom-call(bf16[64,20,128]{2,1,0:T(8,128)(2,1)S(1)} %all-to-all-done.1.got_ref, f32[16,128]{1,0:T(8,128)S(1)} %bitcast.29, f32[16,128]{1,0:T(8,128)S(1)} %bitcast.32, ...), custom_call_target="tpu_custom_call" | custom-call | tf_op jit(solution)/shard_map/adam/pallas_call | solution.py:541
  (36 shorter events, 0.2 us)
Async XLA Ops:
  0.6 42.2 %copy-start = (bf16[256,2048]{1,0:T(8,128)(2,1)S(1)}, bf16[256,2048]{1,0:T(8,128)(2,1)}, u32[]{:S(2)}) copy-start(bf16[256,2048]{1,0:T(8,128)(2,1)} %param.16) | copy-start | bytes 3145732
  2.3 40.5 %all-to-all-start = ((bf16[64,20,128]{2,1,0:T(8,128)(2,1)}), bf16[64,20,128]{2,1,0:T(8,128)(2,1)S(1)}, u32[]{:S(2)}, u32[]{:S(2)}) async-start(bf16[64,20,128]{2,1,0:T(8,128)(2,1)} %spread.1), calls=%async_computation | async-start | bytes 786432 | tf_op jit(solution)/shard_map/all_to_all | solution.py:463
  16.8 10.9 %collective-permute-start = (bf16[256,128]{1,0:T(8,128)(2,1)S(1)}, bf16[256,128]{1,0:T(8,128)(2,1)S(1)}, u32[]{:S(2)}, u32[]{:S(2)}) collective-permute-start(bf16[256,128]{1,0:T(8,128)(2,1)S(1)} %get-tuple-element.83.own_ref), channel_id=1, source_target_pairs={{0,16},{4,20},{8,24},{12,28},{16,32},{20,36},{24,40},{28,44},{32,4... | collective-permute-start | bytes 196616 | tf_op jit(solution)/shard_map/ppermute | solution.py:450
  17.9 14.0 %collective-permute-start.1 = (bf16[256,128]{1,0:T(8,128)(2,1)S(1)}, bf16[256,128]{1,0:T(8,128)(2,1)S(1)}, u32[]{:S(2)}, u32[]{:S(2)}) collective-permute-start(bf16[256,128]{1,0:T(8,128)(2,1)S(1)} %get-tuple-element.83.own_ref), channel_id=1, source_target_pairs={{0,32},{4,36},{8,40},{12,44},{16,48},{20,52},{24,56},{28,60},{32,6... | collective-permute-start | bytes 196616 | tf_op jit(solution)/shard_map/ppermute | solution.py:450
  32.0 7.5 %collective-permute-start.2 = (bf16[2,256,128]{2,1,0:T(8,128)(2,1)S(1)}, bf16[2,256,128]{2,1,0:T(8,128)(2,1)S(1)}, u32[]{:S(2)}, u32[]{:S(2)}) collective-permute-start(bf16[2,256,128]{2,1,0:T(8,128)(2,1)S(1)} %get-tuple-element.50), channel_id=1, source_target_pairs={{0,4},{4,8},{8,12},{12,0},{16,20},{20,24},{24,28},{28,16},{32,36},... | collective-permute-start | bytes 393224 | tf_op jit(solution)/shard_map/ppermute | solution.py:454
  33.0 8.3 %collective-permute-start.3 = (bf16[2,256,128]{2,1,0:T(8,128)(2,1)S(1)}, bf16[2,256,128]{2,1,0:T(8,128)(2,1)S(1)}, u32[]{:S(2)}, u32[]{:S(2)}) collective-permute-start(bf16[2,256,128]{2,1,0:T(8,128)(2,1)S(1)} %get-tuple-element.51), channel_id=1, source_target_pairs={{0,8},{4,12},{8,0},{12,4},{16,24},{20,28},{24,16},{28,20},{32,40},... | collective-permute-start | bytes 393224 | tf_op jit(solution)/shard_map/ppermute | solution.py:454
  35.4 7.3 %collective-permute-start.4 = (bf16[2,256,128]{2,1,0:T(8,128)(2,1)S(1)}, bf16[2,256,128]{2,1,0:T(8,128)(2,1)S(1)}, u32[]{:S(2)}, u32[]{:S(2)}) collective-permute-start(bf16[2,256,128]{2,1,0:T(8,128)(2,1)S(1)} %get-tuple-element.52), channel_id=1, source_target_pairs={{0,12},{4,0},{8,4},{12,8},{16,28},{20,16},{24,20},{28,24},{32,44},... | collective-permute-start | bytes 393224 | tf_op jit(solution)/shard_map/ppermute | solution.py:454
  36.5 6.7 %collective-permute-start.5 = (bf16[256,128]{1,0:T(8,128)(2,1)S(1)}, bf16[256,128]{1,0:T(8,128)(2,1)S(1)}, u32[]{:S(2)}, u32[]{:S(2)}) collective-permute-start(bf16[256,128]{1,0:T(8,128)(2,1)S(1)} %collective-permute-done.one_ref.refs_7_), channel_id=1, source_target_pairs={{0,1},{1,0},{2,3},{3,2},{4,5},{5,4},{6,7},{7,6},{8,9},{9,8},{10,11... | collective-permute-start | bytes 196616 | tf_op jit(solution)/shard_map/ppermute | solution.py:469
  39.4 6.7 %collective-permute-start.6 = (bf16[256,128]{1,0:T(8,128)(2,1)S(1)}, bf16[256,128]{1,0:T(8,128)(2,1)S(1)}, u32[]{:S(2)}, u32[]{:S(2)}) collective-permute-start(bf16[256,128]{1,0:T(8,128)(2,1)S(1)} %collective-permute-done.1.two_ref.refs_8_), channel_id=1, source_target_pairs={{0,1},{1,0},{2,3},{3,2},{4,5},{5,4},{6,7},{7,6},{8,9},{9,8},{10,11... | collective-permute-start | bytes 196616 | tf_op jit(solution)/shard_map/ppermute | solution.py:469
  39.4 7.2 %collective-permute-start.7 = (bf16[2,256,128]{2,1,0:T(8,128)(2,1)S(1)}, bf16[2,256,128]{2,1,0:T(8,128)(2,1)S(1)}, u32[]{:S(2)}, u32[]{:S(2)}) collective-permute-start(bf16[2,256,128]{2,1,0:T(8,128)(2,1)S(1)} %collective-permute-done.2.refs_9_), channel_id=1, source_target_pairs={{0,1},{1,0},{2,3},{3,2},{4,5},{5,4},{6,7},{7,6},{8,9},{9,8},{10,11... | collective-permute-start | bytes 393224 | tf_op jit(solution)/shard_map/ppermute | solution.py:469
  41.3 10.3 %collective-permute-start.8 = (bf16[2,256,128]{2,1,0:T(8,128)(2,1)S(1)}, bf16[2,256,128]{2,1,0:T(8,128)(2,1)S(1)}, u32[]{:S(2)}, u32[]{:S(2)}) collective-permute-start(bf16[2,256,128]{2,1,0:T(8,128)(2,1)S(1)} %collective-permute-done.3.refs_10_), channel_id=1, source_target_pairs={{0,1},{1,0},{2,3},{3,2},{4,5},{5,4},{6,7},{7,6},{8,9},{9,8},{10,11... | collective-permute-start | bytes 393224 | tf_op jit(solution)/shard_map/ppermute | solution.py:469
  42.7 8.9 %collective-permute-start.9 = (bf16[2,256,128]{2,1,0:T(8,128)(2,1)S(1)}, bf16[2,256,128]{2,1,0:T(8,128)(2,1)S(1)}, u32[]{:S(2)}, u32[]{:S(2)}) collective-permute-start(bf16[2,256,128]{2,1,0:T(8,128)(2,1)S(1)} %collective-permute-done.4.refs_11_), channel_id=1, source_target_pairs={{0,1},{1,0},{2,3},{3,2},{4,5},{5,4},{6,7},{7,6},{8,9},{9,8},{10,11... | collective-permute-start | bytes 393224 | tf_op jit(solution)/shard_map/ppermute | solution.py:469
  43.3 8.4 %collective-permute-start.10 = (bf16[64,256]{1,0:T(8,128)(2,1)S(1)}, bf16[64,256]{1,0:T(8,128)(2,1)S(1)}, u32[]{:S(2)}, u32[]{:S(2)}) collective-permute-start(bf16[64,256]{1,0:T(8,128)(2,1)S(1)} %convolution_convert_fusion.1.refs_17_), channel_id=1, source_target_pairs={{0,3},{1,2},{2,1},{3,0},{4,7},{5,6},{6,5},{7,4},{8,11},{9,10},{10,... | collective-permute-start | bytes 98312 | tf_op jit(solution)/shard_map/ppermute | solution.py:476
  46.1 5.5 %collective-permute-start.11 = (bf16[64,256]{1,0:T(8,128)(2,1)S(1)}, bf16[64,256]{1,0:T(8,128)(2,1)S(1)}, u32[]{:S(2)}, u32[]{:S(2)}) collective-permute-start(bf16[64,256]{1,0:T(8,128)(2,1)S(1)} %convolution_convert_fusion.1.refs_17_), channel_id=1, source_target_pairs={{0,2},{1,3},{2,0},{3,1},{4,6},{5,7},{6,4},{7,5},{8,10},{9,11},{10,... | collective-permute-start | bytes 98312 | tf_op jit(solution)/shard_map/ppermute | solution.py:476
  46.7 5.0 %collective-permute-start.12 = (bf16[64,256]{1,0:T(8,128)(2,1)S(1)}, bf16[64,256]{1,0:T(8,128)(2,1)S(1)}, u32[]{:S(2)}, u32[]{:S(2)}) collective-permute-start(bf16[64,256]{1,0:T(8,128)(2,1)S(1)} %convolution_convert_fusion.1.refs_17_), channel_id=1, source_target_pairs={{0,1},{1,0},{2,3},{3,2},{4,5},{5,4},{6,7},{7,6},{8,9},{9,8},{10,11... | collective-permute-start | bytes 98312 | tf_op jit(solution)/shard_map/ppermute | solution.py:476
  47.0 0.9 copy-start.1
  48.0 0.9 copy-start.2
  49.0 0.7 copy-start.7
  49.7 0.7 copy-start.11
  50.3 0.7 copy-start.12
  61.5 1.7 %copy-start.8 = (s32[2,64]{1,0:T(2,128)S(1)}, s32[2,64]{1,0:T(2,128)}, u32[]{:S(2)}) copy-start(s32[2,64]{1,0:T(2,128)} %mask_ref.1) | copy-start | bytes 1540
  62.9 5.8 %collective-permute-start.13 = (bf16[2304,128]{1,0:T(8,128)(2,1)S(1)}, bf16[2304,128]{1,0:T(8,128)(2,1)S(1)}, u32[]{:S(2)}, u32[]{:S(2)}) collective-permute-start(bf16[2304,128]{1,0:T(8,128)(2,1)S(1)} %kv_send.1), channel_id=1, source_target_pairs={{0,1},{1,0},{2,3},{3,2},{4,5},{5,4},{6,7},{7,6},{8,9},{9,8},{10,11... | collective-permute-start | bytes 1769480 | tf_op jit(solution)/shard_map/ppermute | solution.py:496
  63.2 5.6 %collective-permute-start.14 = (bf16[64,256]{1,0:T(8,128)(2,1)S(1)}, bf16[64,256]{1,0:T(8,128)(2,1)S(1)}, u32[]{:S(2)}, u32[]{:S(2)}) collective-permute-start(bf16[64,256]{1,0:T(8,128)(2,1)S(1)} %get-tuple-element.72), channel_id=1, source_target_pairs={{0,3},{1,2},{2,1},{3,0},{4,7},{5,6},{6,5},{7,4},{8,11},{9,10},{10,... | collective-permute-start | bytes 98312 | tf_op jit(solution)/shard_map/ppermute | solution.py:494
  65.9 4.3 %collective-permute-start.15 = (bf16[64,256]{1,0:T(8,128)(2,1)S(1)}, bf16[64,256]{1,0:T(8,128)(2,1)S(1)}, u32[]{:S(2)}, u32[]{:S(2)}) collective-permute-start(bf16[64,256]{1,0:T(8,128)(2,1)S(1)} %get-tuple-element.72), channel_id=1, source_target_pairs={{0,2},{1,3},{2,0},{3,1},{4,6},{5,7},{6,4},{7,5},{8,10},{9,11},{10,... | collective-permute-start | bytes 98312 | tf_op jit(solution)/shard_map/ppermute | solution.py:494
  66.4 3.8 %collective-permute-start.16 = (bf16[64,256]{1,0:T(8,128)(2,1)S(1)}, bf16[64,256]{1,0:T(8,128)(2,1)S(1)}, u32[]{:S(2)}, u32[]{:S(2)}) collective-permute-start(bf16[64,256]{1,0:T(8,128)(2,1)S(1)} %get-tuple-element.72), channel_id=1, source_target_pairs={{0,1},{1,0},{2,3},{3,2},{4,5},{5,4},{6,7},{7,6},{8,9},{9,8},{10,11... | collective-permute-start | bytes 98312 | tf_op jit(solution)/shard_map/ppermute | solution.py:494
  68.6 39.9 %copy-start.3 = (f32[1,2048]{1,0:T(1,128)S(1)}, f32[1,2048]{1,0:T(1,128)}, u32[]{:S(2)}) copy-start(f32[1,2048]{1,0:T(1,128)} %param.17) | copy-start | bytes 24580
  68.6 39.9 %copy-start.4 = (f32[1,512]{1,0:T(1,128)S(1)}, f32[1,512]{1,0:T(1,128)}, u32[]{:S(2)}) copy-start(f32[1,512]{1,0:T(1,128)} %param.20) | copy-start | bytes 6148
  68.6 39.9 %copy-start.5 = (f32[1,2048]{1,0:T(1,128)S(1)}, f32[1,2048]{1,0:T(1,128)}, u32[]{:S(2)}) copy-start(f32[1,2048]{1,0:T(1,128)} %param.18) | copy-start | bytes 24580
  68.6 39.9 %copy-start.6 = (f32[1,2048]{1,0:T(1,128)S(1)}, f32[1,2048]{1,0:T(1,128)}, u32[]{:S(2)}) copy-start(f32[1,2048]{1,0:T(1,128)} %param.19) | copy-start | bytes 24580
  68.6 39.9 %copy-start.9 = (f32[1,512]{1,0:T(1,128)S(1)}, f32[1,512]{1,0:T(1,128)}, u32[]{:S(2)}) copy-start(f32[1,512]{1,0:T(1,128)} %param.21) | copy-start | bytes 6148
  68.6 39.9 %copy-start.10 = (f32[1,512]{1,0:T(1,128)S(1)}, f32[1,512]{1,0:T(1,128)}, u32[]{:S(2)}) copy-start(f32[1,512]{1,0:T(1,128)} %param.22) | copy-start | bytes 6148
  71.4 37.1 %all-to-all-start.1 = ((bf16[64,20,128]{2,1,0:T(8,128)(2,1)}), bf16[64,20,128]{2,1,0:T(8,128)(2,1)S(1)}, u32[]{:S(2)}, u32[]{:S(2)}) async-start(bf16[64,20,128]{2,1,0:T(8,128)(2,1)} %pad_maximum_fusion), calls=%async_computation.1 | async-start | bytes 786432 | tf_op jit(solution)/shard_map/all_to_all | solution.py:510
  78.6 6.9 %collective-permute-start.17 = (bf16[2,256,128]{2,1,0:T(8,128)(2,1)S(1)}, bf16[2,256,128]{2,1,0:T(8,128)(2,1)S(1)}, u32[]{:S(2)}, u32[]{:S(2)}) collective-permute-start(bf16[2,256,128]{2,1,0:T(8,128)(2,1)S(1)} %get-tuple-element.66), channel_id=1, source_target_pairs={{0,12},{4,0},{8,4},{12,8},{16,28},{20,16},{24,20},{28,24},{32,44},... | collective-permute-start | bytes 393224 | tf_op jit(solution)/shard_map/ppermute | solution.py:454
  80.9 6.6 %collective-permute-start.18 = (bf16[2,256,128]{2,1,0:T(8,128)(2,1)S(1)}, bf16[2,256,128]{2,1,0:T(8,128)(2,1)S(1)}, u32[]{:S(2)}, u32[]{:S(2)}) collective-permute-start(bf16[2,256,128]{2,1,0:T(8,128)(2,1)S(1)} %get-tuple-element.67), channel_id=1, source_target_pairs={{0,8},{4,12},{8,0},{12,4},{16,24},{20,28},{24,16},{28,20},{32,40},... | collective-permute-start | bytes 393224 | tf_op jit(solution)/shard_map/ppermute | solution.py:454
  81.5 12.4 %collective-permute-start.19 = (bf16[2,256,128]{2,1,0:T(8,128)(2,1)S(1)}, bf16[2,256,128]{2,1,0:T(8,128)(2,1)S(1)}, u32[]{:S(2)}, u32[]{:S(2)}) collective-permute-start(bf16[2,256,128]{2,1,0:T(8,128)(2,1)S(1)} %get-tuple-element.68), channel_id=1, source_target_pairs={{0,4},{4,8},{8,12},{12,0},{16,20},{20,24},{24,28},{28,16},{32,36},... | collective-permute-start | bytes 393224 | tf_op jit(solution)/shard_map/ppermute | solution.py:454
  94.0 10.4 %collective-permute-start.20 = (bf16[256,128]{1,0:T(8,128)(2,1)S(1)}, bf16[256,128]{1,0:T(8,128)(2,1)S(1)}, u32[]{:S(2)}, u32[]{:S(2)}) collective-permute-start(bf16[256,128]{1,0:T(8,128)(2,1)S(1)} %get-tuple-element.69), channel_id=1, source_target_pairs={{0,224},{1,226},{2,225},{3,227},{4,228},{5,230},{6,229},{7,231},{8... | collective-permute-start | bytes 196616 | tf_op jit(solution)/shard_map/ppermute | solution.py:524
  98.6 6.1 %collective-permute-start.21 = (bf16[256,128]{1,0:T(8,128)(2,1)S(1)}, bf16[256,128]{1,0:T(8,128)(2,1)S(1)}, u32[]{:S(2)}, u32[]{:S(2)}) collective-permute-start(bf16[256,128]{1,0:T(8,128)(2,1)S(1)} %get-tuple-element.70), channel_id=1, source_target_pairs={{0,240},{1,242},{2,241},{3,243},{4,244},{5,246},{6,245},{7,247},{8... | collective-permute-start | bytes 196616 | tf_op jit(solution)/shard_map/ppermute | solution.py:524
  100.7 7.1 %collective-permute-start.22 = (bf16[256,128]{1,0:T(8,128)(2,1)S(1)}, bf16[256,128]{1,0:T(8,128)(2,1)S(1)}, u32[]{:S(2)}, u32[]{:S(2)}) collective-permute-start(bf16[256,128]{1,0:T(8,128)(2,1)S(1)} %get-tuple-element.71), channel_id=1, source_target_pairs={{0,0},{1,2},{2,1},{3,3},{4,4},{5,6},{6,5},{7,7},{8,8},{9,10},{10,9... | collective-permute-start | bytes 196616 | tf_op jit(solution)/shard_map/ppermute | solution.py:524

commit v7 on v6

--- a/solution.py
+++ b/solution.py
@@ -398,9 +398,9 @@
 
 
 def adam_kernel(got_ref, pd, md, vd, pu, mu, vu, keep_ref, opd, omd, ovd, opu, omu, ovu):
-    down_rows = pd.shape[0]
+    groups = pd.shape[0]
     total = jnp.sum(got_ref[...].astype(jnp.float32), axis=0)
-    grads = (total[:down_rows], total[down_rows:] * keep_ref[0, 0])
+    grads = (total[:groups], total[groups:] * keep_ref[0, 0])
     for grad, p, m, v, op, om, ov in (
         (grads[0], pd, md, vd, opd, omd, ovd),
         (grads[1], pu, mu, vu, opu, omu, ovu),
@@ -502,8 +502,8 @@
     grad_down_part = dot32(low_rank, inputs, NN).astype(jnp.bfloat16)
     packed = jnp.concatenate(
         [
-            grad_down_part.reshape(ranks, down_rows, 128),
-            grad_up_part.reshape(ranks, up_rows, 128),
+            grad_down_part.reshape(ranks, down_rows // 4, 4, 128),
+            grad_up_part.reshape(ranks, up_rows // 4, 4, 128),
         ],
         1,
     )
@@ -528,7 +528,7 @@
 
     keep_row = lax.dynamic_slice_in_dim(keep_masks[1], ctx_place, 1, 0)
     small = [
-        a.reshape(-1, 128)
+        a.reshape(-1, 4, 128)
         for a in (
             adapter_down,
             down_first_moment,

time: 110 us -> 110 us (level)
    unnamed x28 -> x27, local copies, waits for them, and re-layouts: 3.98 us -> 3.95 us
  transfers between devices with their start and end apart: 25 -> 25, of which waited for: 8 -> 8; matrix products, arithmetic and copies ran while one was open for 2% -> 3% of each run, Pallas kernels for 2% -> 2%
where the time goes in v7:
time: 110 us
  starting transfers between devices  56 us (51%)
  waiting for transfers between devices  28 us (25%)
  Pallas kernels  16 us (15%)
  local copies, waits for them, and re-layouts  5.78 us (5%)
  other arithmetic  2.44 us (2%)
    all_to_all x1, starting transfers between devices, on_device(): gathered = lax.all_to_all(row, 'ctx', split_axis=0, concat_axis=0)  13.6 us
    ppermute x2, waiting for transfers between devices, along(): lax.ppermute(piece, 'ctx', [(i, (i + step) % ctx) for i in range(ctx)])  11.9 us
    ppermute x6, waiting for transfers between devices, across(): return lax.ppermute(piece, 'ctx', pairs)  11.2 us
    ppermute x3, starting transfers between devices, home(): piece = lax.ppermute(piece, ('ctx', 'head'), pairs)  10 us
    pallas_call x1, Pallas kernels, attention(): pl.pallas_call(functools.partial(attention_kernel, tokens=tokens, heads=h...  9.78 us
    ppermute x6, starting transfers between devices, across(): return lax.ppermute(piece, 'ctx', pairs)  8.01 us
    all_to_all x1, starting transfers between devices, on_device(): received = lax.all_to_all(packed, 'ctx', split_axis=0, concat_axis=0)  7.21 us
    ppermute x5, starting transfers between devices, on_device(): swapped = [lax.ppermute(piece, 'head', swap) for piece in direct]  6.24 us
  transfers between devices with their start and end apart: 25, of which 8 were waited for; matrix products, arithmetic and copies ran while one was open for 3% of the time, Pallas kernels for 2%

profile of v7, /device:TPU:1, one launch (start us, length us, event | category | flops | bytes accessed | tf_op | source)
XLA Modules:
  0.0 110.0 jit_solution(8383110061078784139)
XLA Ops:
  0.6 0.0 copy-start
  0.7 0.8 pad_maximum_fusion.1.row_ref
  1.5 0.8 spread.1
  2.3 13.6 %all-to-all-start = ((bf16[64,20,128]{2,1,0:T(8,128)(2,1)}), bf16[64,20,128]{2,1,0:T(8,128)(2,1)S(1)}, u32[]{:S(2)}, u32[]{:S(2)}) async-start(bf16[64,20,128]{2,1,0:T(8,128)(2,1)} %spread.1), calls=%async_computation | async-start | bytes 786432 | tf_op jit(solution)/shard_map/all_to_all | solution.py:463
  15.9 0.9 constant_dynamic-slice_fusion.1
  16.8 1.1 collective-permute-start
  17.9 2.1 %collective-permute-start.1 = (bf16[256,128]{1,0:T(8,128)(2,1)S(1)}, bf16[256,128]{1,0:T(8,128)(2,1)S(1)}, u32[]{:S(2)}, u32[]{:S(2)}) collective-permute-start(bf16[256,128]{1,0:T(8,128)(2,1)S(1)} %get-tuple-element.83.own_ref), channel_id=1, source_target_pairs={{0,32},{4,36},{8,40},{12,44},{16,48},{20,52},{24,56},{28,60},{32,6... | collective-permute-start | bytes 196616 | tf_op jit(solution)/shard_map/ppermute | solution.py:450
  20.0 7.8 %collective-permute-done.one_ref.refs_7_ = bf16[256,128]{1,0:T(8,128)(2,1)S(1)} collective-permute-done((bf16[256,128]{1,0:T(8,128)(2,1)S(1)}, bf16[256,128]{1,0:T(8,128)(2,1)S(1)}, u32[]{:S(2)}, u32[]{:S(2)}) %collective-permute-start) | collective-permute-done | bytes 65568 | tf_op jit(solution)/shard_map/ppermute | solution.py:450
  27.8 4.2 %collective-permute-done.1.two_ref.refs_8_ = bf16[256,128]{1,0:T(8,128)(2,1)S(1)} collective-permute-done((bf16[256,128]{1,0:T(8,128)(2,1)S(1)}, bf16[256,128]{1,0:T(8,128)(2,1)S(1)}, u32[]{:S(2)}, u32[]{:S(2)}) %collective-permute-start.1) | collective-permute-done | bytes 65568 | tf_op jit(solution)/shard_map/ppermute | solution.py:450
  32.0 1.0 collective-permute-start.2
  33.0 2.5 %collective-permute-start.3 = (bf16[2,256,128]{2,1,0:T(8,128)(2,1)S(1)}, bf16[2,256,128]{2,1,0:T(8,128)(2,1)S(1)}, u32[]{:S(2)}, u32[]{:S(2)}) collective-permute-start(bf16[2,256,128]{2,1,0:T(8,128)(2,1)S(1)} %get-tuple-element.51), channel_id=1, source_target_pairs={{0,8},{4,12},{8,0},{12,4},{16,24},{20,28},{24,16},{28,20},{32,40},... | collective-permute-start | bytes 393224 | tf_op jit(solution)/shard_map/ppermute | solution.py:454
  35.4 1.1 collective-permute-start.4
  36.5 2.9 %collective-permute-start.5 = (bf16[256,128]{1,0:T(8,128)(2,1)S(1)}, bf16[256,128]{1,0:T(8,128)(2,1)S(1)}, u32[]{:S(2)}, u32[]{:S(2)}) collective-permute-start(bf16[256,128]{1,0:T(8,128)(2,1)S(1)} %collective-permute-done.one_ref.refs_7_), channel_id=1, source_target_pairs={{0,1},{1,0},{2,3},{3,2},{4,5},{5,4},{6,7},{7,6},{8,9},{9,8},{10,11... | collective-permute-start | bytes 196616 | tf_op jit(solution)/shard_map/ppermute | solution.py:469
  39.4 0.0 collective-permute-start.6
  39.4 0.0 collective-permute-done.2.refs_9_
  39.4 1.9 %collective-permute-start.7 = (bf16[2,256,128]{2,1,0:T(8,128)(2,1)S(1)}, bf16[2,256,128]{2,1,0:T(8,128)(2,1)S(1)}, u32[]{:S(2)}, u32[]{:S(2)}) collective-permute-start(bf16[2,256,128]{2,1,0:T(8,128)(2,1)S(1)} %collective-permute-done.2.refs_9_), channel_id=1, source_target_pairs={{0,1},{1,0},{2,3},{3,2},{4,5},{5,4},{6,7},{7,6},{8,9},{9,8},{10,11... | collective-permute-start | bytes 393224 | tf_op jit(solution)/shard_map/ppermute | solution.py:469
  41.3 1.4 %collective-permute-start.8 = (bf16[2,256,128]{2,1,0:T(8,128)(2,1)S(1)}, bf16[2,256,128]{2,1,0:T(8,128)(2,1)S(1)}, u32[]{:S(2)}, u32[]{:S(2)}) collective-permute-start(bf16[2,256,128]{2,1,0:T(8,128)(2,1)S(1)} %collective-permute-done.3.refs_10_), channel_id=1, source_target_pairs={{0,1},{1,0},{2,3},{3,2},{4,5},{5,4},{6,7},{7,6},{8,9},{9,8},{10,11... | collective-permute-start | bytes 393224 | tf_op jit(solution)/shard_map/ppermute | solution.py:469
  42.7 0.1 collective-permute-start.9
  42.8 0.4 convolution_convert_fusion.1.refs_17_
  43.3 2.9 %collective-permute-start.10 = (bf16[64,256]{1,0:T(8,128)(2,1)S(1)}, bf16[64,256]{1,0:T(8,128)(2,1)S(1)}, u32[]{:S(2)}, u32[]{:S(2)}) collective-permute-start(bf16[64,256]{1,0:T(8,128)(2,1)S(1)} %convolution_convert_fusion.1.refs_17_), channel_id=1, source_target_pairs={{0,3},{1,2},{2,1},{3,0},{4,7},{5,6},{6,5},{7,4},{8,11},{9,10},{10,... | collective-permute-start | bytes 98312 | tf_op jit(solution)/shard_map/ppermute | solution.py:476
  46.1 0.5 collective-permute-start.11
  46.7 0.4 collective-permute-start.12
  47.0 0.9 copy-done.1
  48.0 0.9 copy-done.2
  48.9 0.1 stage.1
  49.0 0.0 copy-start.7
  49.0 0.7 copy-done.7
  49.7 0.7 copy-done.11
  50.4 0.7 copy-done.12
  51.0 0.6 bounds.1
  51.7 9.8 %attention.1 = (bf16[256,512]{1,0:T(8,128)(2,1)}, bf16[256,512]{1,0:T(8,128)(2,1)}, bf16[64,256]{1,0:T(8,128)(2,1)S(1)}, bf16[64,512]{1,0:T(8,128)(2,1)S(1)}, bf...) custom-call(bf16[4,256,128]{2,1,0:T(8,128)(2,1)S(1)} %get-tuple-element.46.refs_, ...), custom_call_target="tpu_custom_call" | custom-call | flops 2415919104 | bytes 8388608 | tf_op jit(solution)/shard_map/attention/pallas_call | solution.py:257
  61.5 1.4 %kv_send.1 = bf16[2304,128]{1,0:T(8,128)(2,1)S(1)} custom-call(bf16[4,2304,256]{2,1,0:T(8,128)(2,1)S(1)} %get-tuple-element.55.w_ref, bf16[4,2304,256]{2,1,0:T(8,128)(2,1)S(1)} %get-tuple-element.56.gs_ref, bf16[4,256,128]{2,1,0:T(8,128)(2,1)S(1)} %get-tuple-element.47.refs_1_.go_ref, bf16[4,256,128]{2,1,0:T(8,128)(2,1)S(1)} %get-tuple-element.57.q_ref), custom_call_target="tpu_custom_call" | custom-call | flops 603979776 | bytes 2097152 | tf_op jit(solution)/shard_map/kv_send/pallas_call | solution.py:320
  62.9 0.3 collective-permute-start.13
  63.2 2.7 %collective-permute-start.14 = (bf16[64,256]{1,0:T(8,128)(2,1)S(1)}, bf16[64,256]{1,0:T(8,128)(2,1)S(1)}, u32[]{:S(2)}, u32[]{:S(2)}) collective-permute-start(bf16[64,256]{1,0:T(8,128)(2,1)S(1)} %get-tuple-element.72), channel_id=1, source_target_pairs={{0,3},{1,2},{2,1},{3,0},{4,7},{5,6},{6,5},{7,4},{8,11},{9,10},{10,... | collective-permute-start | bytes 98312 | tf_op jit(solution)/shard_map/ppermute | solution.py:494
  65.9 0.5 collective-permute-start.15
  66.4 0.5 collective-permute-start.16
  66.9 1.7 %kv_keep.1.keep_ref = f32[2304,128]{1,0:T(8,128)S(1)} custom-call(bf16[4,2304,256]{2,1,0:T(8,128)(2,1)S(1)} %get-tuple-element.55.w_ref, bf16[4,2304,256]{2,1,0:T(8,128)(2,1)S(1)} %get-tuple-element.56.gs_ref, bf16[4,256,128]{2,1,0:T(8,128)(2,1)S(1)} %get-tuple-element.47.refs_1_.go_ref, bf16[4,256,128]{2,1,0:T(8,128)(2,1)S(1)} %get-tuple-element.57.q_ref), custom_call_target="tpu_custom_call" | custom-call | flops 603979776 | bytes 2097152 | tf_op jit(solution)/shard_map/kv_keep/pallas_call | solution.py:320
  68.6 0.0 copy-start.3
  68.6 0.0 copy-start.4
  68.6 0.0 copy-start.5
  68.6 0.0 copy-start.6
  68.6 0.0 copy-start.9
  68.6 0.0 copy-start.10
  68.7 0.1 pair_sum.1
  68.8 1.4 %collective-permute-done.15 = bf16[64,256]{1,0:T(8,128)(2,1)S(1)} collective-permute-done((bf16[64,256]{1,0:T(8,128)(2,1)S(1)}, bf16[64,256]{1,0:T(8,128)(2,1)S(1)}, u32[]{:S(2)}, u32[]{:S(2)}) %collective-permute-start.15) | collective-permute-done | bytes 32800 | tf_op jit(solution)/shard_map/ppermute | solution.py:494
  70.2 0.3 convolution_convert_fusion
  70.5 0.2 reshape.82
  70.7 0.9 pad_maximum_fusion
  71.7 7.2 %all-to-all-start.1 = ((bf16[64,5,4,128]{3,2,1,0:T(4,128)(2,1)}), bf16[64,5,4,128]{3,2,1,0:T(4,128)(2,1)S(1)}, u32[]{:S(2)}, u32[]{:S(2)}) async-start(bf16[64,5,4,128]{3,2,1,0:T(4,128)(2,1)} %pad_maximum_fusion), calls=%async_computation.1 | async-start | bytes 655360 | tf_op jit(solution)/shard_map/all_to_all | solution.py:510
  78.9 2.3 %collective-permute-start.17 = (bf16[2,256,128]{2,1,0:T(8,128)(2,1)S(1)}, bf16[2,256,128]{2,1,0:T(8,128)(2,1)S(1)}, u32[]{:S(2)}, u32[]{:S(2)}) collective-permute-start(bf16[2,256,128]{2,1,0:T(8,128)(2,1)S(1)} %get-tuple-element.66), channel_id=1, source_target_pairs={{0,12},{4,0},{8,4},{12,8},{16,28},{20,16},{24,20},{28,24},{32,44},... | collective-permute-start | bytes 393224 | tf_op jit(solution)/shard_map/ppermute | solution.py:454
  81.2 0.6 collective-permute-start.18
  81.8 0.6 collective-permute-start.19
  82.3 3.5 %collective-permute-done.17.rest_0_ = bf16[2,256,128]{2,1,0:T(8,128)(2,1)S(1)} collective-permute-done((bf16[2,256,128]{2,1,0:T(8,128)(2,1)S(1)}, bf16[2,256,128]{2,1,0:T(8,128)(2,1)S(1)}, u32[]{:S(2)}, u32[]{:S(2)}) %collective-permute-start.17) | collective-permute-done | bytes 131104 | tf_op jit(solution)/shard_map/ppermute | solution.py:454
  85.8 2.2 %collective-permute-done.18.rest_1_ = bf16[2,256,128]{2,1,0:T(8,128)(2,1)S(1)} collective-permute-done((bf16[2,256,128]{2,1,0:T(8,128)(2,1)S(1)}, bf16[2,256,128]{2,1,0:T(8,128)(2,1)S(1)}, u32[]{:S(2)}, u32[]{:S(2)}) %collective-permute-start.18) | collective-permute-done | bytes 131104 | tf_op jit(solution)/shard_map/ppermute | solution.py:454
  88.0 5.5 %collective-permute-done.19.rest_2_ = bf16[2,256,128]{2,1,0:T(8,128)(2,1)S(1)} collective-permute-done((bf16[2,256,128]{2,1,0:T(8,128)(2,1)S(1)}, bf16[2,256,128]{2,1,0:T(8,128)(2,1)S(1)}, u32[]{:S(2)}, u32[]{:S(2)}) %collective-permute-start.19) | collective-permute-done | bytes 131104 | tf_op jit(solution)/shard_map/ppermute | solution.py:454
  93.5 0.1 row_sum.1
  93.6 4.8 %collective-permute-start.20 = (bf16[256,128]{1,0:T(8,128)(2,1)S(1)}, bf16[256,128]{1,0:T(8,128)(2,1)S(1)}, u32[]{:S(2)}, u32[]{:S(2)}) collective-permute-start(bf16[256,128]{1,0:T(8,128)(2,1)S(1)} %get-tuple-element.69), channel_id=1, source_target_pairs={{0,224},{1,226},{2,225},{3,227},{4,228},{5,230},{6,229},{7,231},{8... | collective-permute-start | bytes 196616 | tf_op jit(solution)/shard_map/ppermute | solution.py:524
  98.4 2.3 %collective-permute-start.21 = (bf16[256,128]{1,0:T(8,128)(2,1)S(1)}, bf16[256,128]{1,0:T(8,128)(2,1)S(1)}, u32[]{:S(2)}, u32[]{:S(2)}) collective-permute-start(bf16[256,128]{1,0:T(8,128)(2,1)S(1)} %get-tuple-element.70), channel_id=1, source_target_pairs={{0,240},{1,242},{2,241},{3,243},{4,244},{5,246},{6,245},{7,247},{8... | collective-permute-start | bytes 196616 | tf_op jit(solution)/shard_map/ppermute | solution.py:524
  100.7 3.0 %collective-permute-start.22 = (bf16[256,128]{1,0:T(8,128)(2,1)S(1)}, bf16[256,128]{1,0:T(8,128)(2,1)S(1)}, u32[]{:S(2)}, u32[]{:S(2)}) collective-permute-start(bf16[256,128]{1,0:T(8,128)(2,1)S(1)} %get-tuple-element.71), channel_id=1, source_target_pairs={{0,0},{1,2},{2,1},{3,3},{4,4},{5,6},{6,5},{7,7},{8,8},{9,10},{10,9... | collective-permute-start | bytes 196616 | tf_op jit(solution)/shard_map/ppermute | solution.py:524
  103.7 0.7 constant_dynamic-slice_fusion.keep_ref
  104.3 0.2 collective-permute-done.21
  104.5 3.3 %collective-permute-done.22 = bf16[256,128]{1,0:T(8,128)(2,1)S(1)} collective-permute-done((bf16[256,128]{1,0:T(8,128)(2,1)S(1)}, bf16[256,128]{1,0:T(8,128)(2,1)S(1)}, u32[]{:S(2)}, u32[]{:S(2)}) %collective-permute-start.22) | collective-permute-done | bytes 65568 | tf_op jit(solution)/shard_map/ppermute | solution.py:524
  107.7 0.7 convert_add_fusion
  108.5 1.5 %adam.1 = (f32[4,4,128]{2,1,0:T(4,128)}, f32[4,4,128]{2,1,0:T(4,128)}, f32[4,4,128]{2,1,0:T(4,128)}, f32[1,4,128]{2,1,0:T(4,128)}, f32[1,4,128]{2,1,0:T(4,128)}, /*index=5*/f32[1,4,128]{2,1,0:T(4,128)}) custom-call(bf16[64,5,4,128]{3,2,1,0:T(4,128)(2,1)S(1)} %all-to-all-done.1.got_ref, f32[4,4,128]{2,1,0:T(4,128)S(1)} %bitcast.28, ...), custom_call_target="tpu_custom_call" | custom-call | tf_op jit(solution)/shard_map/adam/pallas_call | solution.py:541
  (36 shorter events, 0.2 us)
Async XLA Ops:
  0.6 42.2 %copy-start = (bf16[256,2048]{1,0:T(8,128)(2,1)S(1)}, bf16[256,2048]{1,0:T(8,128)(2,1)}, u32[]{:S(2)}) copy-start(bf16[256,2048]{1,0:T(8,128)(2,1)} %param.16) | copy-start | bytes 3145732
  2.3 40.5 %all-to-all-start = ((bf16[64,20,128]{2,1,0:T(8,128)(2,1)}), bf16[64,20,128]{2,1,0:T(8,128)(2,1)S(1)}, u32[]{:S(2)}, u32[]{:S(2)}) async-start(bf16[64,20,128]{2,1,0:T(8,128)(2,1)} %spread.1), calls=%async_computation | async-start | bytes 786432 | tf_op jit(solution)/shard_map/all_to_all | solution.py:463
  16.8 10.9 %collective-permute-start = (bf16[256,128]{1,0:T(8,128)(2,1)S(1)}, bf16[256,128]{1,0:T(8,128)(2,1)S(1)}, u32[]{:S(2)}, u32[]{:S(2)}) collective-permute-start(bf16[256,128]{1,0:T(8,128)(2,1)S(1)} %get-tuple-element.83.own_ref), channel_id=1, source_target_pairs={{0,16},{4,20},{8,24},{12,28},{16,32},{20,36},{24,40},{28,44},{32,4... | collective-permute-start | bytes 196616 | tf_op jit(solution)/shard_map/ppermute | solution.py:450
  17.9 14.0 %collective-permute-start.1 = (bf16[256,128]{1,0:T(8,128)(2,1)S(1)}, bf16[256,128]{1,0:T(8,128)(2,1)S(1)}, u32[]{:S(2)}, u32[]{:S(2)}) collective-permute-start(bf16[256,128]{1,0:T(8,128)(2,1)S(1)} %get-tuple-element.83.own_ref), channel_id=1, source_target_pairs={{0,32},{4,36},{8,40},{12,44},{16,48},{20,52},{24,56},{28,60},{32,6... | collective-permute-start | bytes 196616 | tf_op jit(solution)/shard_map/ppermute | solution.py:450
  32.0 7.5 %collective-permute-start.2 = (bf16[2,256,128]{2,1,0:T(8,128)(2,1)S(1)}, bf16[2,256,128]{2,1,0:T(8,128)(2,1)S(1)}, u32[]{:S(2)}, u32[]{:S(2)}) collective-permute-start(bf16[2,256,128]{2,1,0:T(8,128)(2,1)S(1)} %get-tuple-element.50), channel_id=1, source_target_pairs={{0,4},{4,8},{8,12},{12,0},{16,20},{20,24},{24,28},{28,16},{32,36},... | collective-permute-start | bytes 393224 | tf_op jit(solution)/shard_map/ppermute | solution.py:454
  33.0 8.3 %collective-permute-start.3 = (bf16[2,256,128]{2,1,0:T(8,128)(2,1)S(1)}, bf16[2,256,128]{2,1,0:T(8,128)(2,1)S(1)}, u32[]{:S(2)}, u32[]{:S(2)}) collective-permute-start(bf16[2,256,128]{2,1,0:T(8,128)(2,1)S(1)} %get-tuple-element.51), channel_id=1, source_target_pairs={{0,8},{4,12},{8,0},{12,4},{16,24},{20,28},{24,16},{28,20},{32,40},... | collective-permute-start | bytes 393224 | tf_op jit(solution)/shard_map/ppermute | solution.py:454
  35.4 7.3 %collective-permute-start.4 = (bf16[2,256,128]{2,1,0:T(8,128)(2,1)S(1)}, bf16[2,256,128]{2,1,0:T(8,128)(2,1)S(1)}, u32[]{:S(2)}, u32[]{:S(2)}) collective-permute-start(bf16[2,256,128]{2,1,0:T(8,128)(2,1)S(1)} %get-tuple-element.52), channel_id=1, source_target_pairs={{0,12},{4,0},{8,4},{12,8},{16,28},{20,16},{24,20},{28,24},{32,44},... | collective-permute-start | bytes 393224 | tf_op jit(solution)/shard_map/ppermute | solution.py:454
  36.5 6.7 %collective-permute-start.5 = (bf16[256,128]{1,0:T(8,128)(2,1)S(1)}, bf16[256,128]{1,0:T(8,128)(2,1)S(1)}, u32[]{:S(2)}, u32[]{:S(2)}) collective-permute-start(bf16[256,128]{1,0:T(8,128)(2,1)S(1)} %collective-permute-done.one_ref.refs_7_), channel_id=1, source_target_pairs={{0,1},{1,0},{2,3},{3,2},{4,5},{5,4},{6,7},{7,6},{8,9},{9,8},{10,11... | collective-permute-start | bytes 196616 | tf_op jit(solution)/shard_map/ppermute | solution.py:469
  39.4 6.7 %collective-permute-start.6 = (bf16[256,128]{1,0:T(8,128)(2,1)S(1)}, bf16[256,128]{1,0:T(8,128)(2,1)S(1)}, u32[]{:S(2)}, u32[]{:S(2)}) collective-permute-start(bf16[256,128]{1,0:T(8,128)(2,1)S(1)} %collective-permute-done.1.two_ref.refs_8_), channel_id=1, source_target_pairs={{0,1},{1,0},{2,3},{3,2},{4,5},{5,4},{6,7},{7,6},{8,9},{9,8},{10,11... | collective-permute-start | bytes 196616 | tf_op jit(solution)/shard_map/ppermute | solution.py:469
  39.4 7.2 %collective-permute-start.7 = (bf16[2,256,128]{2,1,0:T(8,128)(2,1)S(1)}, bf16[2,256,128]{2,1,0:T(8,128)(2,1)S(1)}, u32[]{:S(2)}, u32[]{:S(2)}) collective-permute-start(bf16[2,256,128]{2,1,0:T(8,128)(2,1)S(1)} %collective-permute-done.2.refs_9_), channel_id=1, source_target_pairs={{0,1},{1,0},{2,3},{3,2},{4,5},{5,4},{6,7},{7,6},{8,9},{9,8},{10,11... | collective-permute-start | bytes 393224 | tf_op jit(solution)/shard_map/ppermute | solution.py:469
  41.3 10.3 %collective-permute-start.8 = (bf16[2,256,128]{2,1,0:T(8,128)(2,1)S(1)}, bf16[2,256,128]{2,1,0:T(8,128)(2,1)S(1)}, u32[]{:S(2)}, u32[]{:S(2)}) collective-permute-start(bf16[2,256,128]{2,1,0:T(8,128)(2,1)S(1)} %collective-permute-done.3.refs_10_), channel_id=1, source_target_pairs={{0,1},{1,0},{2,3},{3,2},{4,5},{5,4},{6,7},{7,6},{8,9},{9,8},{10,11... | collective-permute-start | bytes 393224 | tf_op jit(solution)/shard_map/ppermute | solution.py:469
  42.7 8.9 %collective-permute-start.9 = (bf16[2,256,128]{2,1,0:T(8,128)(2,1)S(1)}, bf16[2,256,128]{2,1,0:T(8,128)(2,1)S(1)}, u32[]{:S(2)}, u32[]{:S(2)}) collective-permute-start(bf16[2,256,128]{2,1,0:T(8,128)(2,1)S(1)} %collective-permute-done.4.refs_11_), channel_id=1, source_target_pairs={{0,1},{1,0},{2,3},{3,2},{4,5},{5,4},{6,7},{7,6},{8,9},{9,8},{10,11... | collective-permute-start | bytes 393224 | tf_op jit(solution)/shard_map/ppermute | solution.py:469
  43.3 8.4 %collective-permute-start.10 = (bf16[64,256]{1,0:T(8,128)(2,1)S(1)}, bf16[64,256]{1,0:T(8,128)(2,1)S(1)}, u32[]{:S(2)}, u32[]{:S(2)}) collective-permute-start(bf16[64,256]{1,0:T(8,128)(2,1)S(1)} %convolution_convert_fusion.1.refs_17_), channel_id=1, source_target_pairs={{0,3},{1,2},{2,1},{3,0},{4,7},{5,6},{6,5},{7,4},{8,11},{9,10},{10,... | collective-permute-start | bytes 98312 | tf_op jit(solution)/shard_map/ppermute | solution.py:476
  46.1 5.5 %collective-permute-start.11 = (bf16[64,256]{1,0:T(8,128)(2,1)S(1)}, bf16[64,256]{1,0:T(8,128)(2,1)S(1)}, u32[]{:S(2)}, u32[]{:S(2)}) collective-permute-start(bf16[64,256]{1,0:T(8,128)(2,1)S(1)} %convolution_convert_fusion.1.refs_17_), channel_id=1, source_target_pairs={{0,2},{1,3},{2,0},{3,1},{4,6},{5,7},{6,4},{7,5},{8,10},{9,11},{10,... | collective-permute-start | bytes 98312 | tf_op jit(solution)/shard_map/ppermute | solution.py:476
  46.7 5.0 %collective-permute-start.12 = (bf16[64,256]{1,0:T(8,128)(2,1)S(1)}, bf16[64,256]{1,0:T(8,128)(2,1)S(1)}, u32[]{:S(2)}, u32[]{:S(2)}) collective-permute-start(bf16[64,256]{1,0:T(8,128)(2,1)S(1)} %convolution_convert_fusion.1.refs_17_), channel_id=1, source_target_pairs={{0,1},{1,0},{2,3},{3,2},{4,5},{5,4},{6,7},{7,6},{8,9},{9,8},{10,11... | collective-permute-start | bytes 98312 | tf_op jit(solution)/shard_map/ppermute | solution.py:476
  47.0 0.9 copy-start.1
  48.0 0.9 copy-start.2
  49.0 0.7 copy-start.7
  49.7 0.7 copy-start.11
  50.3 0.7 copy-start.12
  61.5 1.7 %copy-start.8 = (s32[2,64]{1,0:T(2,128)S(1)}, s32[2,64]{1,0:T(2,128)}, u32[]{:S(2)}) copy-start(s32[2,64]{1,0:T(2,128)} %mask_ref.1) | copy-start | bytes 1540
  62.9 5.8 %collective-permute-start.13 = (bf16[2304,128]{1,0:T(8,128)(2,1)S(1)}, bf16[2304,128]{1,0:T(8,128)(2,1)S(1)}, u32[]{:S(2)}, u32[]{:S(2)}) collective-permute-start(bf16[2304,128]{1,0:T(8,128)(2,1)S(1)} %kv_send.1), channel_id=1, source_target_pairs={{0,1},{1,0},{2,3},{3,2},{4,5},{5,4},{6,7},{7,6},{8,9},{9,8},{10,11... | collective-permute-start | bytes 1769480 | tf_op jit(solution)/shard_map/ppermute | solution.py:496
  63.2 5.6 %collective-permute-start.14 = (bf16[64,256]{1,0:T(8,128)(2,1)S(1)}, bf16[64,256]{1,0:T(8,128)(2,1)S(1)}, u32[]{:S(2)}, u32[]{:S(2)}) collective-permute-start(bf16[64,256]{1,0:T(8,128)(2,1)S(1)} %get-tuple-element.72), channel_id=1, source_target_pairs={{0,3},{1,2},{2,1},{3,0},{4,7},{5,6},{6,5},{7,4},{8,11},{9,10},{10,... | collective-permute-start | bytes 98312 | tf_op jit(solution)/shard_map/ppermute | solution.py:494
  65.9 4.3 %collective-permute-start.15 = (bf16[64,256]{1,0:T(8,128)(2,1)S(1)}, bf16[64,256]{1,0:T(8,128)(2,1)S(1)}, u32[]{:S(2)}, u32[]{:S(2)}) collective-permute-start(bf16[64,256]{1,0:T(8,128)(2,1)S(1)} %get-tuple-element.72), channel_id=1, source_target_pairs={{0,2},{1,3},{2,0},{3,1},{4,6},{5,7},{6,4},{7,5},{8,10},{9,11},{10,... | collective-permute-start | bytes 98312 | tf_op jit(solution)/shard_map/ppermute | solution.py:494
  66.4 3.8 %collective-permute-start.16 = (bf16[64,256]{1,0:T(8,128)(2,1)S(1)}, bf16[64,256]{1,0:T(8,128)(2,1)S(1)}, u32[]{:S(2)}, u32[]{:S(2)}) collective-permute-start(bf16[64,256]{1,0:T(8,128)(2,1)S(1)} %get-tuple-element.72), channel_id=1, source_target_pairs={{0,1},{1,0},{2,3},{3,2},{4,5},{5,4},{6,7},{7,6},{8,9},{9,8},{10,11... | collective-permute-start | bytes 98312 | tf_op jit(solution)/shard_map/ppermute | solution.py:494
  68.6 39.9 %copy-start.3 = (f32[1,2048]{1,0:T(1,128)S(1)}, f32[1,2048]{1,0:T(1,128)}, u32[]{:S(2)}) copy-start(f32[1,2048]{1,0:T(1,128)} %param.17) | copy-start | bytes 24580
  68.6 39.9 %copy-start.4 = (f32[1,512]{1,0:T(1,128)S(1)}, f32[1,512]{1,0:T(1,128)}, u32[]{:S(2)}) copy-start(f32[1,512]{1,0:T(1,128)} %param.20) | copy-start | bytes 6148
  68.6 39.8 %copy-start.5 = (f32[1,2048]{1,0:T(1,128)S(1)}, f32[1,2048]{1,0:T(1,128)}, u32[]{:S(2)}) copy-start(f32[1,2048]{1,0:T(1,128)} %param.18) | copy-start | bytes 24580
  68.6 39.8 %copy-start.6 = (f32[1,2048]{1,0:T(1,128)S(1)}, f32[1,2048]{1,0:T(1,128)}, u32[]{:S(2)}) copy-start(f32[1,2048]{1,0:T(1,128)} %param.19) | copy-start | bytes 24580
  68.6 39.8 %copy-start.9 = (f32[1,512]{1,0:T(1,128)S(1)}, f32[1,512]{1,0:T(1,128)}, u32[]{:S(2)}) copy-start(f32[1,512]{1,0:T(1,128)} %param.21) | copy-start | bytes 6148
  68.6 39.8 %copy-start.10 = (f32[1,512]{1,0:T(1,128)S(1)}, f32[1,512]{1,0:T(1,128)}, u32[]{:S(2)}) copy-start(f32[1,512]{1,0:T(1,128)} %param.22) | copy-start | bytes 6148
  71.7 36.8 %all-to-all-start.1 = ((bf16[64,5,4,128]{3,2,1,0:T(4,128)(2,1)}), bf16[64,5,4,128]{3,2,1,0:T(4,128)(2,1)S(1)}, u32[]{:S(2)}, u32[]{:S(2)}) async-start(bf16[64,5,4,128]{3,2,1,0:T(4,128)(2,1)} %pad_maximum_fusion), calls=%async_computation.1 | async-start | bytes 655360 | tf_op jit(solution)/shard_map/all_to_all | solution.py:510
  78.9 6.9 %collective-permute-start.17 = (bf16[2,256,128]{2,1,0:T(8,128)(2,1)S(1)}, bf16[2,256,128]{2,1,0:T(8,128)(2,1)S(1)}, u32[]{:S(2)}, u32[]{:S(2)}) collective-permute-start(bf16[2,256,128]{2,1,0:T(8,128)(2,1)S(1)} %get-tuple-element.66), channel_id=1, source_target_pairs={{0,12},{4,0},{8,4},{12,8},{16,28},{20,16},{24,20},{28,24},{32,44},... | collective-permute-start | bytes 393224 | tf_op jit(solution)/shard_map/ppermute | solution.py:454
  81.2 6.8 %collective-permute-start.18 = (bf16[2,256,128]{2,1,0:T(8,128)(2,1)S(1)}, bf16[2,256,128]{2,1,0:T(8,128)(2,1)S(1)}, u32[]{:S(2)}, u32[]{:S(2)}) collective-permute-start(bf16[2,256,128]{2,1,0:T(8,128)(2,1)S(1)} %get-tuple-element.67), channel_id=1, source_target_pairs={{0,8},{4,12},{8,0},{12,4},{16,24},{20,28},{24,16},{28,20},{32,40},... | collective-permute-start | bytes 393224 | tf_op jit(solution)/shard_map/ppermute | solution.py:454
  81.8 11.7 %collective-permute-start.19 = (bf16[2,256,128]{2,1,0:T(8,128)(2,1)S(1)}, bf16[2,256,128]{2,1,0:T(8,128)(2,1)S(1)}, u32[]{:S(2)}, u32[]{:S(2)}) collective-permute-start(bf16[2,256,128]{2,1,0:T(8,128)(2,1)S(1)} %get-tuple-element.68), channel_id=1, source_target_pairs={{0,4},{4,8},{8,12},{12,0},{16,20},{20,24},{24,28},{28,16},{32,36},... | collective-permute-start | bytes 393224 | tf_op jit(solution)/shard_map/ppermute | solution.py:454
  93.6 10.7 %collective-permute-start.20 = (bf16[256,128]{1,0:T(8,128)(2,1)S(1)}, bf16[256,128]{1,0:T(8,128)(2,1)S(1)}, u32[]{:S(2)}, u32[]{:S(2)}) collective-permute-start(bf16[256,128]{1,0:T(8,128)(2,1)S(1)} %get-tuple-element.69), channel_id=1, source_target_pairs={{0,224},{1,226},{2,225},{3,227},{4,228},{5,230},{6,229},{7,231},{8... | collective-permute-start | bytes 196616 | tf_op jit(solution)/shard_map/ppermute | solution.py:524
  98.4 6.1 %collective-permute-start.21 = (bf16[256,128]{1,0:T(8,128)(2,1)S(1)}, bf16[256,128]{1,0:T(8,128)(2,1)S(1)}, u32[]{:S(2)}, u32[]{:S(2)}) collective-permute-start(bf16[256,128]{1,0:T(8,128)(2,1)S(1)} %get-tuple-element.70), channel_id=1, source_target_pairs={{0,240},{1,242},{2,241},{3,243},{4,244},{5,246},{6,245},{7,247},{8... | collective-permute-start | bytes 196616 | tf_op jit(solution)/shard_map/ppermute | solution.py:524
  100.7 7.1 %collective-permute-start.22 = (bf16[256,128]{1,0:T(8,128)(2,1)S(1)}, bf16[256,128]{1,0:T(8,128)(2,1)S(1)}, u32[]{:S(2)}, u32[]{:S(2)}) collective-permute-start(bf16[256,128]{1,0:T(8,128)(2,1)S(1)} %get-tuple-element.71), channel_id=1, source_target_pairs={{0,0},{1,2},{2,1},{3,3},{4,4},{5,6},{6,5},{7,7},{8,8},{9,10},{10,9... | collective-permute-start | bytes 196616 | tf_op jit(solution)/shard_map/ppermute | solution.py:524
